TPU v7x, 32 devices: a whole 2x2x4 slice. The times are simulated.
32 devices in a mesh: depth: 2 (over y), row: 4 (over z), col: 4 (over x, core).
Axes of the slice: x: 2, y: 2, z: 4, core: 2. Of those that a mesh axis runs over, the one named last changes fastest.
Arguments:
- prop: bfloat16 [2, 2, 8192, 8192], P('depth', None, 'row', 'col'), may hold values from -0.046875 to 0.046875
- source: float32 [8192, 256], P(('row', 'col')), may hold values from -6 to 6
- down_init: float32 [2, 8192, 256], P('depth', ('row', 'col')), may hold values from -6 to 6
- up_init: float32 [2, 8192, 256], P('depth', ('row', 'col')), may hold values from -6 to 6
- refl_down: float32 [2, 8192], P('depth', ('row', 'col')), may hold values from -0.6 to 0.6
- refl_up: float32 [2, 8192], P('depth', ('row', 'col')), may hold values from -0.6 to 0.6
Outputs:
- down_field: float32 [2, 8192, 256], P('depth', ('row', 'col'))
- up_field: float32 [2, 8192, 256], P('depth', ('row', 'col'))
All inputs are finite; a program needn't handle non-finite values.
Results may differ from a plain program's by a relative error of at most 0.0041.
Values may be sent and summed in bfloat16 or wider, within the bound.
No kernel may reach another device: no remote copies, remote signals or barrier semaphores. Data moves between devices by JAX's collectives and lax.ppermute only.
A program may use at most 64 MiB of HBM per device.

v0:
```python
import jax
import jax.numpy as jnp
from jax import lax
from jax.sharding import PartitionSpec as P

PASSES = 2


def passed_along(x, axis, by):
    peers = lax.axis_size(axis)
    pairs = [(i, i + by) for i in range(peers) if 0 <= i + by < peers]
    return lax.ppermute(x, axis, pairs)


def complex_join(first, second, sources):
    real_part = first[:, :sources] - second[:, sources:]
    imag_part = first[:, sources:] + second[:, :sources]
    return jnp.concatenate([real_part, imag_part], axis=1)


def downward(weight_real, weight_imag, down_low, sources):
    gathered = lax.all_gather(down_low, "row", axis=0, tiled=True)
    return lax.psum_scatter(
        complex_join(
            jnp.dot(weight_real, gathered, preferred_element_type=jnp.float32),
            jnp.dot(weight_imag, gathered, preferred_element_type=jnp.float32),
            sources,
        ),
        "col",
        scatter_dimension=0,
        tiled=True,
    )


def upward(weight_real, weight_imag, up_low, sources):
    gathered = lax.all_gather(up_low, "col", axis=0, tiled=True)
    numbers = (((0,), (0,)), ((), ()))
    first = lax.dot_general(weight_real, gathered, numbers, preferred_element_type=jnp.float32)
    second = lax.dot_general(weight_imag, gathered, numbers, preferred_element_type=jnp.float32)
    return lax.psum_scatter(
        complex_join(first, second, sources), "row", scatter_dimension=0, tiled=True
    )


def send_trans(trans):
    return passed_along(trans, "depth", 1)


def send_back(back):
    return passed_along(back, "depth", -1)


def body(prop, source, down_init, up_init, refl_down, refl_up):
    weight_real = prop[0, 0]
    weight_imag = prop[0, 1]
    sources = down_init.shape[2] // 2
    at_surface = lax.axis_index("depth") == 0
    refl_above = refl_down[0][:, None]
    refl_below = refl_up[0][:, None]
    down = down_init[0]
    up = up_init[0]
    for sweep in range(PASSES):
        down_low = down.astype(jnp.bfloat16)
        up_low = up.astype(jnp.bfloat16)
        trans = downward(weight_real, weight_imag, down_low, sources)
        from_above = send_trans(trans)
        back = upward(weight_real, weight_imag, up_low, sources)
        from_below = send_back(back)
        above = jnp.where(at_surface, source, from_above)
        down = above + refl_above * back
        up = from_below + refl_below * trans
    return (down[None], up[None])


def solution(mesh):
    placed = (
        P("depth", None, "row", "col"),
        P(("row", "col"), None),
        P("depth", ("row", "col"), None),
        P("depth", ("row", "col"), None),
        P("depth", ("row", "col")),
        P("depth", ("row", "col")),
    )
    return jax.shard_map(
        body,
        mesh=mesh,
        in_specs=placed,
        out_specs=(P("depth", ("row", "col"), None), P("depth", ("row", "col"), None)),
        check_vma=False,
    )
```

profile of v0, /device:TPU:0, one launch (start us, length us, event | category | flops | bytes accessed | tf_op | source)
XLA Modules:
  0.0 290.8 jit_solution(9658612321237586070)
XLA Ops:
  7.2 1.8 convert_element_type.18
  9.1 1.8 convert_element_type.20
  10.9 29.9 %all-gather.11.cloned.1.call-done = bf16[1,2048,256]{2,1,0:T(8,128)(2,1)} async-done(((bf16[1,512,256]{2,1,0:T(8,128)(2,1)}), bf16[1,2048,256]{2,1,0:T(8,128)(2,1)}) %all-gather.11.cloned.1.call-update) | async-done | bytes 1048592 | tf_op jit(solution)/shard_map/all_gather | solution.py:22
  40.8 6.1 %fusion.6 = f32[2048,256]{0,1:T(8,128)S(1)} fusion(bf16[1,2,2048,2048]{3,2,1,0:T(8,128)(2,1)} %param.6, bf16[1,2048,256]{2,1,0:T(8,128)(2,1)} %all-gather.11.cloned.1.call-done), kind=kOutput, calls=%fused_computation.6 | convolution fusion | flops 2147483648 | bytes 11534336 | tf_op jit(solution)/shard_map/dot_general | solution.py:26
  47.0 2.4 copy-done.6
  49.6 2.4 fusion.14
  52.3 1.5 pad_maximum_fusion
  53.9 5.3 %all-gather.13.cloned.1.call-done = bf16[1,2048,256]{2,1,0:T(8,128)(2,1)} async-done(((bf16[1,512,256]{2,1,0:T(8,128)(2,1)}), bf16[1,2048,256]{2,1,0:T(8,128)(2,1)}) %all-gather.13.cloned.1.call-update) | async-done | bytes 1048592 | tf_op jit(solution)/shard_map/all_gather | solution.py:36
  59.2 6.1 %fusion.4 = f32[2048,256]{0,1:T(8,128)S(1)} fusion(bf16[1,2,2048,2048]{3,2,1,0:T(8,128)(2,1)} %param.6, bf16[1,2048,256]{2,1,0:T(8,128)(2,1)} %all-gather.13.cloned.1.call-done), kind=kOutput, calls=%fused_computation.4 | convolution fusion | flops 2147483648 | bytes 11534336 | tf_op jit(solution)/shard_map/dot_general | solution.py:39
  65.3 6.1 %fusion.12 = f32[2048,256]{0,1:T(8,128)S(1)} fusion(bf16[1,2,2048,2048]{3,2,1,0:T(8,128)(2,1)} %param.6, bf16[1,2048,256]{2,1,0:T(8,128)(2,1)S(1)} %copy-done.7), kind=kOutput, calls=%fused_computation.12 | convolution fusion | flops 2147483648 | bytes 11534336 | tf_op jit(solution)/shard_map/dot_general | solution.py:38
  71.7 1.5 pad_maximum_fusion.1
  73.2 20.0 %reduce-scatter.5.cloned.1.call-done = f32[512,256]{0,1:T(8,128)} async-done(((f32[2048,256]{0,1:T(8,128)}), f32[512,256]{0,1:T(8,128)}) %reduce-scatter.5.cloned.1.call-update) | async-done | bytes 524304 | tf_op jit(solution)/shard_map/reduce_scatter | solution.py:23
  93.2 3.5 %collective-permute-start = (f32[512,256]{0,1:T(8,128)}, f32[512,256]{0,1:T(8,128)S(1)}, u32[]{:S(2)}, u32[]{:S(2)}) collective-permute-start(f32[512,256]{0,1:T(8,128)} %reduce-scatter.5.cloned.1.call-done), channel_id=1, source_target_pairs={{0,16},{1,17},{2,18},{3,19},{4,20},{5,21},{6,22},{7,23},{8,24},{9,... | collective-permute-start | bytes 1572872 | tf_op jit(solution)/shard_map/ppermute | solution.py:12
  96.9 42.4 %reduce-scatter.7.cloned.1.call-done = f32[512,256]{0,1:T(8,128)} async-done(((f32[2048,256]{0,1:T(8,128)}), f32[512,256]{0,1:T(8,128)}) %reduce-scatter.7.cloned.1.call-update) | async-done | bytes 524304 | tf_op jit(solution)/shard_map/reduce_scatter | solution.py:40
  139.3 2.0 add_convert_fusion.1
  141.4 1.3 collective-permute-start.2
  142.7 14.1 %collective-permute-done.2 = f32[512,256]{0,1:T(8,128)S(1)} collective-permute-done((f32[512,256]{0,1:T(8,128)S(1)}, f32[512,256]{0,1:T(8,128)S(1)}, u32[]{:S(2)}, u32[]{:S(2)}) %collective-permute-start.2) | collective-permute-done | bytes 524320 | tf_op jit(solution)/shard_map/ppermute | solution.py:12
  157.9 10.9 %all-gather.7.cloned.1.call-done = bf16[2048,256]{0,1:T(8,128)(2,1)} async-done(((bf16[512,256]{0,1:T(8,128)(2,1)}), bf16[2048,256]{0,1:T(8,128)(2,1)}) %all-gather.7.cloned.1.call-update) | async-done | bytes 1048592 | tf_op jit(solution)/shard_map/all_gather | solution.py:22
  168.8 6.1 %fusion.30 = f32[2048,256]{0,1:T(8,128)S(1)} fusion(bf16[2048,256]{0,1:T(8,128)(2,1)} %all-gather.7.cloned.1.call-done, bf16[1,2,2048,2048]{3,2,1,0:T(8,128)(2,1)} %param.6), kind=kOutput, calls=%fused_computation.26 | convolution fusion | flops 2147483648 | bytes 11534336 | tf_op jit(solution)/shard_map/dot_general | solution.py:26
  174.9 6.1 %fusion.24 = f32[2048,256]{0,1:T(8,128)S(1)} fusion(bf16[2048,256]{0,1:T(8,128)(2,1)S(1)} %copy-done.9, bf16[1,2,2048,2048]{3,2,1,0:T(8,128)(2,1)} %param.6), kind=kOutput, calls=%fused_computation.24 | convolution fusion | flops 2147483648 | bytes 11534336 | tf_op jit(solution)/shard_map/dot_general | solution.py:25
  181.3 1.5 pad_maximum_fusion.2
  182.9 4.1 %all-gather.9.cloned.1.call-done = bf16[2048,256]{0,1:T(8,128)(2,1)} async-done(((bf16[512,256]{0,1:T(8,128)(2,1)}), bf16[2048,256]{0,1:T(8,128)(2,1)}) %all-gather.9.cloned.1.call-update) | async-done | bytes 1048592 | tf_op jit(solution)/shard_map/all_gather | solution.py:36
  187.0 6.1 %fusion.33 = f32[2048,256]{0,1:T(8,128)S(1)} fusion(bf16[2048,256]{0,1:T(8,128)(2,1)} %all-gather.9.cloned.1.call-done, bf16[1,2,2048,2048]{3,2,1,0:T(8,128)(2,1)} %param.6), kind=kOutput, calls=%fused_computation.27 | convolution fusion | flops 2147483648 | bytes 11534336 | tf_op jit(solution)/shard_map/dot_general | solution.py:39
  193.1 6.1 %fusion.27 = f32[2048,256]{0,1:T(8,128)S(1)} fusion(bf16[2048,256]{0,1:T(8,128)(2,1)S(1)} %copy-done.8, bf16[1,2,2048,2048]{3,2,1,0:T(8,128)(2,1)} %param.6), kind=kOutput, calls=%fused_computation.25 | convolution fusion | flops 2147483648 | bytes 11534336 | tf_op jit(solution)/shard_map/dot_general | solution.py:38
  199.6 1.5 pad_maximum_fusion.3
  201.1 19.9 %reduce-scatter.9.cloned.1.call-done = f32[512,256]{0,1:T(8,128)} async-done(((f32[2048,256]{0,1:T(8,128)}), f32[512,256]{0,1:T(8,128)}) %reduce-scatter.9.cloned.1.call-update) | async-done | bytes 524304 | tf_op jit(solution)/shard_map/reduce_scatter | solution.py:23
  221.0 3.6 %collective-permute-start.1 = (f32[512,256]{0,1:T(8,128)}, f32[512,256]{0,1:T(8,128)S(1)}, u32[]{:S(2)}, u32[]{:S(2)}) collective-permute-start(f32[512,256]{0,1:T(8,128)} %reduce-scatter.9.cloned.1.call-done), channel_id=1, source_target_pairs={{0,16},{1,17},{2,18},{3,19},{4,20},{5,21},{6,22},{7,23},{8,24},{9,... | collective-permute-start | bytes 1572872 | tf_op jit(solution)/shard_map/ppermute | solution.py:12
  224.6 42.8 %reduce-scatter.11.cloned.1.call-done = f32[512,256]{0,1:T(8,128)} async-done(((f32[2048,256]{0,1:T(8,128)}), f32[512,256]{0,1:T(8,128)}) %reduce-scatter.11.cloned.1.call-update) | async-done | bytes 524304 | tf_op jit(solution)/shard_map/reduce_scatter | solution.py:40
  267.3 1.3 collective-permute-start.3
  268.6 1.2 add_bitcast_fusion.1
  270.8 12.1 %collective-permute-done.3 = f32[512,256]{0,1:T(8,128)S(1)} collective-permute-done((f32[512,256]{0,1:T(8,128)}, f32[512,256]{0,1:T(8,128)S(1)}, u32[]{:S(2)}, u32[]{:S(2)}) %collective-permute-start.3) | collective-permute-done | bytes 524320 | tf_op jit(solution)/shard_map/ppermute | solution.py:12
  283.0 1.0 copy.11
  (47 shorter events, 4.1 us)
Async XLA Ops:
  7.2 33.6 %all-gather.11.cloned.1.call-start = ((), (), s32[]{:S(2)}) async-start(), calls=%async_computation.10 | async-start | bytes 1310720 | tf_op jit(solution)/shard_map/all_gather | solution.py:22
  9.0 50.2 %all-gather.13.cloned.1.call-start = ((), (), s32[]{:S(2)}) async-start(), calls=%async_computation.11 | async-start | bytes 1310720 | tf_op jit(solution)/shard_map/all_gather | solution.py:36
  10.9 82.3 %reduce-scatter.5.cloned.1.call-start = ((), (), s32[]{:S(2)}) async-start(), calls=%async_computation.4 | async-start | bytes 2621440 | tf_op jit(solution)/shard_map/reduce_scatter | solution.py:23
  40.8 8.6 %copy-start.6 = (bf16[1,2,2048,2048]{3,2,1,0:T(8,128)(2,1)S(1)}, bf16[1,2,2048,2048]{3,2,1,0:T(8,128)(2,1)}, u32[]{:S(2)}) copy-start(bf16[1,2,2048,2048]{3,2,1,0:T(8,128)(2,1)} %param.6) | copy-start | bytes 50331652
  40.8 8.8 %copy-start.10 = (bf16[1,2048,256]{2,1,0:T(8,128)(2,1)S(1)}, bf16[1,2048,256]{2,1,0:T(8,128)(2,1)}, u32[]{:S(2)}) copy-start(bf16[1,2048,256]{2,1,0:T(8,128)(2,1)} %all-gather.11.cloned.1.call-done) | copy-start | bytes 3145732
  53.8 85.5 %reduce-scatter.7.cloned.1.call-start = ((), (), s32[]{:S(2)}) async-start(), calls=%async_computation.5 | async-start | bytes 2621440 | tf_op jit(solution)/shard_map/reduce_scatter | solution.py:40
  59.2 6.1 %copy-start.7 = (bf16[1,2048,256]{2,1,0:T(8,128)(2,1)S(1)}, bf16[1,2048,256]{2,1,0:T(8,128)(2,1)}, u32[]{:S(2)}) copy-start(bf16[1,2048,256]{2,1,0:T(8,128)(2,1)} %all-gather.13.cloned.1.call-done) | copy-start | bytes 3145732
  73.1 23.6 %copy-start.2 = (f32[512,256]{1,0:T(8,128)S(1)}, f32[512,256]{1,0:T(8,128)}, u32[]{:S(2)}) copy-start(f32[512,256]{1,0:T(8,128)} %param.7) | copy-start | bytes 1572868
  73.1 66.2 %copy-start.5 = (f32[1,512]{1,0:T(1,128)S(1)}, f32[1,512]{1,0:T(1,128)}, u32[]{:S(2)}) copy-start(f32[1,512]{1,0:T(1,128)} %param.10) | copy-start | bytes 6148
  73.2 83.7 %copy-start.4 = (f32[1,512]{1,0:T(1,128)S(1)}, f32[1,512]{1,0:T(1,128)}, u32[]{:S(2)}) copy-start(f32[1,512]{1,0:T(1,128)} %param.11) | copy-start | bytes 6148
  73.2 95.6 %all-gather.7.cloned.1.call-start = ((), (), s32[]{:S(2)}) async-start(), calls=%async_computation.6 | async-start | bytes 1310720 | tf_op jit(solution)/shard_map/all_gather | solution.py:22
  93.2 63.6 %copy-start = (f32[512,256]{0,1:T(8,128)S(1)}, f32[512,256]{0,1:T(8,128)}, u32[]{:S(2)}) copy-start(f32[512,256]{0,1:T(8,128)} %reduce-scatter.5.cloned.1.call-done) | copy-start | bytes 1572868
  93.2 46.2 %collective-permute-start = (f32[512,256]{0,1:T(8,128)}, f32[512,256]{0,1:T(8,128)S(1)}, u32[]{:S(2)}, u32[]{:S(2)}) collective-permute-start(f32[512,256]{0,1:T(8,128)} %reduce-scatter.5.cloned.1.call-done), channel_id=1, source_target_pairs={{0,16},{1,17},{2,18},{3,19},{4,20},{5,21},{6,22},{7,23},{8,24},{9,... | collective-permute-start | bytes 1572872 | tf_op jit(solution)/shard_map/ppermute | solution.py:12
  139.3 2.1 copy-start.1
  141.3 45.7 %all-gather.9.cloned.1.call-start = ((), (), s32[]{:S(2)}) async-start(), calls=%async_computation.8 | async-start | bytes 1310720 | tf_op jit(solution)/shard_map/all_gather | solution.py:36
  141.4 15.4 %collective-permute-start.2 = (f32[512,256]{0,1:T(8,128)S(1)}, f32[512,256]{0,1:T(8,128)S(1)}, u32[]{:S(2)}, u32[]{:S(2)}) collective-permute-start(f32[512,256]{0,1:T(8,128)S(1)} %copy-done.1), channel_id=1, source_target_pairs={{16,0},{17,1},{18,2},{19,3},{20,4},{21,5},{22,6},{23,7},{24,8},{25... | collective-permute-start | bytes 1572872 | tf_op jit(solution)/shard_map/ppermute | solution.py:12
  157.7 63.3 %reduce-scatter.9.cloned.1.call-start = ((), (), s32[]{:S(2)}) async-start(), calls=%async_computation.7 | async-start | bytes 2621440 | tf_op jit(solution)/shard_map/reduce_scatter | solution.py:23
  168.8 6.2 %copy-start.9 = (bf16[2048,256]{0,1:T(8,128)(2,1)S(1)}, bf16[2048,256]{0,1:T(8,128)(2,1)}, u32[]{:S(2)}) copy-start(bf16[2048,256]{0,1:T(8,128)(2,1)} %all-gather.7.cloned.1.call-done) | copy-start | bytes 3145732
  182.8 84.5 %reduce-scatter.11.cloned.1.call-start = ((), (), s32[]{:S(2)}) async-start(), calls=%async_computation.9 | async-start | bytes 2621440 | tf_op jit(solution)/shard_map/reduce_scatter | solution.py:40
  187.0 6.1 %copy-start.8 = (bf16[2048,256]{0,1:T(8,128)(2,1)S(1)}, bf16[2048,256]{0,1:T(8,128)(2,1)}, u32[]{:S(2)}) copy-start(bf16[2048,256]{0,1:T(8,128)(2,1)} %all-gather.9.cloned.1.call-done) | copy-start | bytes 3145732
  221.0 61.9 %copy-start.3 = (f32[512,256]{0,1:T(8,128)S(1)}, f32[512,256]{0,1:T(8,128)}, u32[]{:S(2)}) copy-start(f32[512,256]{0,1:T(8,128)} %reduce-scatter.9.cloned.1.call-done) | copy-start | bytes 1572868
  221.0 47.6 %collective-permute-start.1 = (f32[512,256]{0,1:T(8,128)}, f32[512,256]{0,1:T(8,128)S(1)}, u32[]{:S(2)}, u32[]{:S(2)}) collective-permute-start(f32[512,256]{0,1:T(8,128)} %reduce-scatter.9.cloned.1.call-done), channel_id=1, source_target_pairs={{0,16},{1,17},{2,18},{3,19},{4,20},{5,21},{6,22},{7,23},{8,24},{9,... | collective-permute-start | bytes 1572872 | tf_op jit(solution)/shard_map/ppermute | solution.py:12
  267.3 15.6 %collective-permute-start.3 = (f32[512,256]{0,1:T(8,128)}, f32[512,256]{0,1:T(8,128)S(1)}, u32[]{:S(2)}, u32[]{:S(2)}) collective-permute-start(f32[512,256]{0,1:T(8,128)} %reduce-scatter.11.cloned.1.call-done), channel_id=1, source_target_pairs={{16,0},{17,1},{18,2},{19,3},{20,4},{21,5},{22,6},{23,7},{24,8},{25... | collective-permute-start | bytes 1572872 | tf_op jit(solution)/shard_map/ppermute | solution.py:12
Sparse Core Ops, SparseCore 0:
  10.1 30.6 all-gather.10
  42.9 16.2 all-gather.12
  61.7 31.4 reduce-scatter.4
  95.4 43.8 reduce-scatter.6
  141.5 27.2 all-gather.6
  170.8 16.2 all-gather.8
  189.5 31.4 reduce-scatter.8
  223.4 43.8 reduce-scatter.10
where the time goes:
time: 291 us
  waiting for transfers between devices  202 us (69%)
  matrix products  45.2 us (16%)
  other arithmetic  14.6 us (5%)
  between operations  14.3 us (5%)
  starting transfers between devices  10.2 us (4%)
  local copies, waits for them, and re-layouts  4.91 us (2%)
    reduce_scatter x2, waiting for transfers between devices, upward(): lax.psum_scatter(complex_join(first, second, sources), 'row', scatter_dim...  85.2 us
    all_gather x2, waiting for transfers between devices, downward(): gathered = lax.all_gather(down_low, 'row', axis=0, tiled=True)  40.8 us
    reduce_scatter x2, waiting for transfers between devices, downward(): lax.psum_scatter(complex_join(jnp.dot(weight_real, gathered, preferred_el...  39.9 us
    ppermute x4, waiting for transfers between devices, passed_along(): return lax.ppermute(x, axis, pairs)  26.2 us
    dot_general x2, matrix products, downward(): jnp.dot(weight_imag, gathered, preferred_element_type=jnp.float32)  12.3 us
    dot_general x2, matrix products, upward(): lax.dot_general(weight_real, gathered, numbers, preferred_element_type=jn...  12.3 us
    dot_general x2, matrix products, upward(): lax.dot_general(weight_imag, gathered, numbers, preferred_element_type=jn...  12.2 us
    ppermute x4, starting transfers between devices, passed_along(): return lax.ppermute(x, axis, pairs)  9.66 us
  transfers between devices with their start and end apart: 12, of which 10 were waited for; matrix products, arithmetic and copies ran while one was open for 20% of the time, Pallas kernels for 0%

commit v1 on v0

v1 whole, which is shorter than its diff:
```python
import functools

import jax
import jax.numpy as jnp
from jax import lax
from jax.experimental import pallas as pl
from jax.experimental.pallas import tpu as pltpu
from jax.sharding import PartitionSpec as P

PASSES = 2
F32 = jnp.float32
BF16 = jnp.bfloat16
WHOLE = pl.BlockSpec(memory_space=pltpu.VMEM)
CONTRACT_ROWS = (((0,), (0,)), ((), ()))


def ring_device(place, size):
    half = (size + 1) // 2
    if isinstance(place, int):
        return 2 * place if place < half else 2 * (size - 1 - place) + 1
    return jnp.where(place < half, 2 * place, 2 * (size - 1 - place) + 1)


def ring_place(device, size):
    return jnp.where(lax.rem(device, 2) == 0, device // 2, size - 1 - device // 2)


def ring_block(behind, size):
    place = ring_place(lax.axis_index("row"), size)
    return ring_device(lax.rem(place - behind + size, size), size)


def ring_hop(x, size):
    pairs = [(ring_device(p, size), ring_device((p + 1) % size, size)) for p in range(size)]
    return lax.ppermute(x, "row", pairs)


def col_swap(x, bit):
    return lax.ppermute(x, "col", [(c, c ^ bit) for c in range(lax.axis_size("col"))])


def depth_shift(x, by):
    peers = lax.axis_size("depth")
    return lax.ppermute(x, "depth", [(i, i + by) for i in range(peers) if 0 <= i + by < peers])


def call(kernel, outs, name, flops, *args):
    moved = sum(a.size * a.dtype.itemsize for a in args)
    return pl.pallas_call(
        kernel,
        in_specs=[WHOLE] * len(args),
        out_specs=[WHOLE] * len(outs),
        out_shape=outs,
        name=name,
        cost_estimate=pl.CostEstimate(flops=flops, bytes_accessed=moved // 8, transcendentals=0),
        compiler_params=pltpu.CompilerParams(vmem_limit_bytes=12 * 2**20),
    )(*args)


def rows_at(block, strip):
    return pl.ds(pl.multiple_of(block * strip, strip), strip)


def place_block(pair_ref, block_ref, rows, sources):
    values = block_ref[...]
    pair_ref[0, rows, :] = values
    pair_ref[1, rows, :sources] = -values[:, sources:]
    pair_ref[1, rows, sources:] = values[:, :sources]


def down_first(size, strip, sources, w_ref, *refs):
    blocks, pair_ref, out_ref = refs[:size], refs[size], refs[size + 1]
    for s in range(size):
        place_block(pair_ref, blocks[s], rows_at(ring_block(s, size), strip), sources)
    me = lax.axis_index("col")
    for k in range(2):
        down_dot(w_ref, pair_ref, rows_at(me ^ (1 + 2 * k), strip), out_ref, k)


def down_dot(w_ref, pair_ref, rows, out_ref, k):
    out_ref[k] = jnp.dot(w_ref[0, 0, rows, :], pair_ref[0], preferred_element_type=F32) + jnp.dot(
        w_ref[0, 1, rows, :], pair_ref[1], preferred_element_type=F32
    )


def down_second(strip, w_ref, pair_ref, out_ref):
    me = lax.axis_index("col")
    for k in range(2):
        down_dot(w_ref, pair_ref, rows_at(me ^ (2 * k), strip), out_ref, k)


def up_dot(w_ref, pair_ref, columns):
    return lax.dot_general(
        w_ref[0, 0, :, columns], pair_ref[0], CONTRACT_ROWS, preferred_element_type=F32
    ) + lax.dot_general(w_ref[0, 1, :, columns], pair_ref[1], CONTRACT_ROWS, preferred_element_type=F32)


def up_first(size, strip, sources, w_ref, *refs):
    blocks, pair_ref, out_ref = refs[:4], refs[4], refs[5]
    me = lax.axis_index("col")
    for s in range(4):
        place_block(pair_ref, blocks[s], rows_at(me ^ s, strip), sources)
    out_ref[...] = up_dot(w_ref, pair_ref, rows_at(ring_block(1, size), strip)).astype(BF16)


def up_rest(size, strip, w_ref, pair_ref, *out_refs):
    for s in range(2, size + 1):
        out_refs[s - 2][...] = up_dot(w_ref, pair_ref, rows_at(ring_block(s % size, size), strip))


def body(prop, source, down_init, up_init, refl_down, refl_up):
    size = lax.axis_size("row")
    assert lax.axis_size("col") == 4
    strip = down_init.shape[1]
    width = down_init.shape[2]
    sources = width // 2
    tall, wide = prop.shape[2], prop.shape[3]
    shape = functools.partial(jax.ShapeDtypeStruct)
    dot_flops = 4 * strip * width
    at_surface = lax.axis_index("depth") == 0
    refl_above = refl_down[0][:, None]
    refl_below = refl_up[0][:, None]
    down_low = down_init[0].astype(BF16)
    up_low = up_init[0].astype(BF16)
    for sweep in range(PASSES):
        far = col_swap(up_low, 2)
        blocks_up = [up_low, col_swap(up_low, 1), far, col_swap(far, 1)]
        blocks_down = [down_low]
        for s in range(size - 1):
            blocks_down.append(ring_hop(blocks_down[-1], size))
        pair_up, travelling = call(
            functools.partial(up_first, size, strip, sources),
            [shape((2, tall, width), BF16), shape((strip, width), BF16)],
            "up_first", dot_flops * tall, prop, *blocks_up,
        )
        own_up = call(
            functools.partial(up_rest, size, strip),
            [shape((strip, width), F32)] * (size - 1),
            "up_rest", dot_flops * tall * (size - 1), prop, pair_up,
        )
        for s in range(size - 2):
            travelling = (ring_hop(travelling, size).astype(F32) + own_up[s]).astype(BF16)
        back = ring_hop(travelling, size).astype(F32) + own_up[size - 2]
        from_below = depth_shift(back.astype(BF16), -1).astype(F32)
        pair_down, to_sibling = call(
            functools.partial(down_first, size, strip, sources),
            [shape((2, wide, width), BF16), shape((2, strip, width), F32)],
            "down_first", dot_flops * wide * 2, prop, *blocks_down,
        )
        (own_down,) = call(
            functools.partial(down_second, strip),
            [shape((2, strip, width), F32)],
            "down_second", dot_flops * wide * 2, prop, pair_down,
        )
        both = own_down + col_swap(to_sibling, 1)
        trans = both[0] + col_swap(both[1].astype(BF16), 2).astype(F32)
        from_above = depth_shift(trans.astype(BF16), 1).astype(F32)
        down = jnp.where(at_surface, source, from_above) + refl_above * back
        up = from_below + refl_below * trans
        down_low = down.astype(BF16)
        up_low = up.astype(BF16)
    return (down[None], up[None])


def solution(mesh):
    placed = (
        P("depth", None, "row", "col"),
        P(("row", "col"), None),
        P("depth", ("row", "col"), None),
        P("depth", ("row", "col"), None),
        P("depth", ("row", "col")),
        P("depth", ("row", "col")),
    )
    return jax.shard_map(
        body,
        mesh=mesh,
        in_specs=placed,
        out_specs=(P("depth", ("row", "col"), None), P("depth", ("row", "col"), None)),
        check_vma=False,
    )
```

time: 291 us -> 141 us (0.48)
  waiting for transfers between devices: 202 us -> 60.3 us
  matrix products: 45.2 us -> 0 us
  starting transfers between devices: 10.2 us -> 42.2 us
  Pallas kernels: 0 us -> 20.5 us
  between operations: 14.3 us -> 0.96 us
  other arithmetic: 14.6 us -> 4.92 us
  local copies, waits for them, and re-layouts: 4.91 us -> 11.7 us
    reduce_scatter x4 -> x0, waiting for transfers between devices: 125 us -> none  [the longest x2 85.2 us: upward(): lax.psum_scatter(complex_join(first, second, sources), 'row', scatter_dim...]
    all_gather x4 -> x0, waiting for transfers between devices: 50.2 us -> none  [the longest x2 40.8 us: downward(): gathered = lax.all_gather(down_low, 'row', axis=0, tiled=True)]
    dot_general x8 -> x0, matrix products: 45.2 us -> none  [the longest x2 12.3 us: downward(): jnp.dot(weight_imag, gathered, preferred_element_type=jnp.float32)]
    ppermute x4 -> x26, waiting for transfers between devices: 26.2 us -> 60.3 us  [the longest x12 37.8 us: ring_hop(): return lax.ppermute(x, 'row', pairs)]
    ppermute x4 -> x26, starting transfers between devices: 9.66 us -> 42.2 us  [the longest x12 24.8 us: ring_hop(): return lax.ppermute(x, 'row', pairs)]
    pallas_call x0 -> x8, Pallas kernels: none -> 20.5 us  [call(): pl.pallas_call(kernel, in_specs=[WHOLE] * len(args), out_specs=[WHOLE] *...]
    unnamed x25 -> x26, local copies, waits for them, and re-layouts: 4.91 us -> 11.6 us
    concatenate x4 -> x0, other arithmetic: 5.89 us -> none  [complex_join(): return jnp.concatenate([real_part, imag_part], axis=1)]
  transfers between devices with their start and end apart: 12 -> 26, of which waited for: 10 -> 13; matrix products, arithmetic and copies ran while one was open for 20% -> 1% of each run, Pallas kernels for 0% -> 15%
where the time goes in v1:
time: 141 us
  waiting for transfers between devices  60.3 us (43%)
  starting transfers between devices  42.2 us (30%)
  Pallas kernels  20.5 us (15%)
  local copies, waits for them, and re-layouts  11.7 us (8%)
  other arithmetic  4.92 us (3%)
    ppermute x12, waiting for transfers between devices, ring_hop(): return lax.ppermute(x, 'row', pairs)  37.8 us
    ppermute x12, starting transfers between devices, ring_hop(): return lax.ppermute(x, 'row', pairs)  24.8 us
    pallas_call x8, Pallas kernels, call(): pl.pallas_call(kernel, in_specs=[WHOLE] * len(args), out_specs=[WHOLE] *...  20.5 us
    ppermute x4, waiting for transfers between devices, depth_shift(): lax.ppermute(x, 'depth', [(i, i + by) for i in range(peers) if 0 <= i + b...  19.9 us
    unnamed x26, local copies, waits for them, and re-layouts  11.6 us
    ppermute x4, starting transfers between devices, depth_shift(): lax.ppermute(x, 'depth', [(i, i + by) for i in range(peers) if 0 <= i + b...  10.6 us
    ppermute x10, starting transfers between devices, col_swap(): lax.ppermute(x, 'col', [(c, c ^ bit) for c in range(lax.axis_size('col'))])  6.76 us
  transfers between devices with their start and end apart: 26, of which 13 were waited for; matrix products, arithmetic and copies ran while one was open for 1% of the time, Pallas kernels for 15%

profile of v1, /device:TPU:0, one launch (start us, length us, event | category | flops | bytes accessed | tf_op | source)
XLA Modules:
  0.0 140.6 jit_solution(1904096069486515765)
XLA Ops:
  1.7 3.0 %collective-permute-start.7 = (bf16[512,256]{1,0:T(8,128)(2,1)S(1)}, bf16[512,256]{1,0:T(8,128)(2,1)S(1)}, u32[]{:S(2)}, u32[]{:S(2)}) collective-permute-start(bf16[512,256]{1,0:T(8,128)(2,1)S(1)} %convert_bitcast_fusion.refs_0_), channel_id=1, source_target_pairs={{0,2},{1,3},{2,0},{3,1},{4,6},{5,7},{6,4},{7,5},{8,10},{9,11},{10,... | collective-permute-start | bytes 786440 | tf_op jit(solution)/shard_map/ppermute | solution.py:39
  5.8 2.6 %collective-permute-start = (bf16[512,256]{1,0:T(8,128)(2,1)S(1)}, bf16[512,256]{1,0:T(8,128)(2,1)S(1)}, u32[]{:S(2)}, u32[]{:S(2)}) collective-permute-start(bf16[512,256]{1,0:T(8,128)(2,1)S(1)} %convert_bitcast_fusion.1.refs_0_), channel_id=1, source_target_pairs={{0,8},{8,12},{12,4},{4,0},{1,9},{9,13},{13,5},{5,1},{2,10},{10,14}... | collective-permute-start | bytes 786440 | tf_op jit(solution)/shard_map/ppermute | solution.py:35
  8.4 2.6 %collective-permute-done.7.refs_2_ = bf16[512,256]{1,0:T(8,128)(2,1)S(1)} collective-permute-done((bf16[512,256]{1,0:T(8,128)(2,1)S(1)}, bf16[512,256]{1,0:T(8,128)(2,1)S(1)}, u32[]{:S(2)}, u32[]{:S(2)}) %collective-permute-start.7) | collective-permute-done | bytes 262176 | tf_op jit(solution)/shard_map/ppermute | solution.py:39
  11.0 2.7 %collective-permute-done.refs_1_ = bf16[512,256]{1,0:T(8,128)(2,1)S(1)} collective-permute-done((bf16[512,256]{1,0:T(8,128)(2,1)S(1)}, bf16[512,256]{1,0:T(8,128)(2,1)S(1)}, u32[]{:S(2)}, u32[]{:S(2)}) %collective-permute-start) | collective-permute-done | bytes 262176 | tf_op jit(solution)/shard_map/ppermute | solution.py:35
  13.7 3.4 %collective-permute-start.1 = (bf16[512,256]{1,0:T(8,128)(2,1)S(1)}, bf16[512,256]{1,0:T(8,128)(2,1)S(1)}, u32[]{:S(2)}, u32[]{:S(2)}) collective-permute-start(bf16[512,256]{1,0:T(8,128)(2,1)S(1)} %collective-permute-done.refs_1_), channel_id=1, source_target_pairs={{0,8},{8,12},{12,4},{4,0},{1,9},{9,13},{13,5},{5,1},{2,10},{10,14}... | collective-permute-start | bytes 786440 | tf_op jit(solution)/shard_map/ppermute | solution.py:35
  17.1 5.8 %copy-done = bf16[1,2,2048,2048]{3,2,1,0:T(8,128)(2,1)S(1)} copy-done((bf16[1,2,2048,2048]{3,2,1,0:T(8,128)(2,1)S(1)}, bf16[1,2,2048,2048]{3,2,1,0:T(8,128)(2,1)}, u32[]{:S(2)}) %copy-start) | copy-done | bytes 16777240
  26.4 3.7 %up_rest.2 = (f32[512,256]{1,0:T(8,128)S(1)}, f32[512,256]{1,0:T(8,128)S(1)}, f32[512,256]{1,0:T(8,128)S(1)}) custom-call(bf16[1,2,2048,2048]{3,2,1,0:T(8,128)(2,1)S(1)} %copy-done, bf16[2,2048,256]{2,1,0:T(8,128)(2,1)S(1)} %get-tuple-element.19.pair_ref), custom_call_target="tpu_custom_call" | custom-call | flops 3221225472 | bytes 2359296 | tf_op jit(solution)/shard_map/up_rest/pallas_call | solution.py:49
  30.1 6.7 %collective-permute-done.2.refs_3_ = bf16[512,256]{1,0:T(8,128)(2,1)S(1)} collective-permute-done((bf16[512,256]{1,0:T(8,128)(2,1)S(1)}, bf16[512,256]{1,0:T(8,128)(2,1)S(1)}, u32[]{:S(2)}, u32[]{:S(2)}) %collective-permute-start.2) | collective-permute-done | bytes 262176 | tf_op jit(solution)/shard_map/ppermute | solution.py:35
  36.8 2.6 %down_first.2 = (bf16[2,2048,256]{2,1,0:T(8,128)(2,1)S(1)}, f32[2,512,256]{2,1,0:T(8,128)S(1)}) custom-call(bf16[1,2,2048,2048]{3,2,1,0:T(8,128)(2,1)S(1)} %copy-done, bf16[512,256]{1,0:T(8,128)(2,1)S(1)} %convert_bitcast_fusion.1.refs_0_, bf16[512,256]{1,0:T(8,128)(2,1)S(1)} %collective-permute-done.refs_1_, ...), custom_call_target="tpu_custom_call" | custom-call | flops 2147483648 | bytes 2228224 | tf_op jit(solution)/shard_map/down_first/pallas_call | solution.py:49
  41.1 7.2 %collective-permute-done.10 = bf16[512,256]{1,0:T(8,128)(2,1)S(1)} collective-permute-done((bf16[512,256]{1,0:T(8,128)(2,1)S(1)}, bf16[512,256]{1,0:T(8,128)(2,1)S(1)}, u32[]{:S(2)}, u32[]{:S(2)}) %collective-permute-start.10) | collective-permute-done | bytes 262176 | tf_op jit(solution)/shard_map/ppermute | solution.py:35
  48.3 2.4 %collective-permute-start.11 = (bf16[512,256]{1,0:T(8,128)(2,1)S(1)}, bf16[512,256]{1,0:T(8,128)(2,1)S(1)}, u32[]{:S(2)}, u32[]{:S(2)}) collective-permute-start(bf16[512,256]{1,0:T(8,128)(2,1)S(1)} %add_convert_fusion.4), channel_id=1, source_target_pairs={{0,8},{8,12},{12,4},{4,0},{1,9},{9,13},{13,5},{5,1},{2,10},{10,14}... | collective-permute-start | bytes 786440 | tf_op jit(solution)/shard_map/ppermute | solution.py:35
  50.8 2.3 %down_second.2 = f32[2,512,256]{2,1,0:T(8,128)S(1)} custom-call(bf16[1,2,2048,2048]{3,2,1,0:T(8,128)(2,1)S(1)} %bitcast.31, bf16[2,2048,256]{2,1,0:T(8,128)(2,1)S(1)} %get-tuple-element.16.pair_ref), custom_call_target="tpu_custom_call" | custom-call | flops 2147483648 | bytes 2359296 | tf_op jit(solution)/shard_map/down_second/pallas_call | solution.py:49
  53.1 3.2 %collective-permute-done.11 = bf16[512,256]{1,0:T(8,128)(2,1)S(1)} collective-permute-done((bf16[512,256]{1,0:T(8,128)(2,1)S(1)}, bf16[512,256]{1,0:T(8,128)(2,1)S(1)}, u32[]{:S(2)}, u32[]{:S(2)}) %collective-permute-start.11) | collective-permute-done | bytes 262176 | tf_op jit(solution)/shard_map/ppermute | solution.py:35
  59.0 6.4 %collective-permute-done.18 = bf16[512,256]{1,0:T(8,128)(2,1)S(1)} collective-permute-done((bf16[512,256]{1,0:T(8,128)(2,1)S(1)}, bf16[512,256]{1,0:T(8,128)(2,1)S(1)}, u32[]{:S(2)}, u32[]{:S(2)}) %collective-permute-start.18) | collective-permute-done | bytes 262176 | tf_op jit(solution)/shard_map/ppermute | solution.py:44
  65.6 4.0 %collective-permute-start.5 = (bf16[512,256]{1,0:T(8,128)(2,1)S(1)}, bf16[512,256]{1,0:T(8,128)(2,1)S(1)}, u32[]{:S(2)}, u32[]{:S(2)}) collective-permute-start(bf16[512,256]{1,0:T(8,128)(2,1)S(1)} %get-tuple-element.33), channel_id=1, source_target_pairs={{0,16},{1,17},{2,18},{3,19},{4,20},{5,21},{6,22},{7,23},{8,24},{9,... | collective-permute-start | bytes 786440 | tf_op jit(solution)/shard_map/ppermute | solution.py:44
  70.6 2.8 %collective-permute-done.5 = bf16[512,256]{1,0:T(8,128)(2,1)S(1)} collective-permute-done((bf16[512,256]{1,0:T(8,128)(2,1)S(1)}, bf16[512,256]{1,0:T(8,128)(2,1)S(1)}, u32[]{:S(2)}, u32[]{:S(2)}) %collective-permute-start.5) | collective-permute-done | bytes 262176 | tf_op jit(solution)/shard_map/ppermute | solution.py:44
  73.6 3.3 %collective-permute-start.12 = (bf16[512,256]{1,0:T(8,128)(2,1)S(1)}, bf16[512,256]{1,0:T(8,128)(2,1)S(1)}, u32[]{:S(2)}, u32[]{:S(2)}) collective-permute-start(bf16[512,256]{1,0:T(8,128)(2,1)S(1)} %add_convert_fusion.3.refs_0_), channel_id=1, source_target_pairs={{0,8},{8,12},{12,4},{4,0},{1,9},{9,13},{13,5},{5,1},{2,10},{10,14}... | collective-permute-start | bytes 786440 | tf_op jit(solution)/shard_map/ppermute | solution.py:35
  77.5 4.2 %collective-permute-done.12.refs_1_ = bf16[512,256]{1,0:T(8,128)(2,1)S(1)} collective-permute-done((bf16[512,256]{1,0:T(8,128)(2,1)S(1)}, bf16[512,256]{1,0:T(8,128)(2,1)S(1)}, u32[]{:S(2)}, u32[]{:S(2)}) %collective-permute-start.12) | collective-permute-done | bytes 262176 | tf_op jit(solution)/shard_map/ppermute | solution.py:35
  81.7 3.4 %collective-permute-start.13 = (bf16[512,256]{1,0:T(8,128)(2,1)S(1)}, bf16[512,256]{1,0:T(8,128)(2,1)S(1)}, u32[]{:S(2)}, u32[]{:S(2)}) collective-permute-start(bf16[512,256]{1,0:T(8,128)(2,1)S(1)} %collective-permute-done.12.refs_1_), channel_id=1, source_target_pairs={{0,8},{8,12},{12,4},{4,0},{1,9},{9,13},{13,5},{5,1},{2,10},{10,14}... | collective-permute-start | bytes 786440 | tf_op jit(solution)/shard_map/ppermute | solution.py:35
  85.1 5.8 %copy-done.1 = bf16[1,2,2048,2048]{3,2,1,0:T(8,128)(2,1)S(1)} copy-done((bf16[1,2,2048,2048]{3,2,1,0:T(8,128)(2,1)S(1)}, bf16[1,2,2048,2048]{3,2,1,0:T(8,128)(2,1)}, u32[]{:S(2)}) %copy-start.1) | copy-done | bytes 16777240
  90.8 1.7 %up_first.3 = (bf16[2,2048,256]{2,1,0:T(8,128)(2,1)S(1)}, bf16[512,256]{1,0:T(8,128)(2,1)S(1)}) custom-call(bf16[1,2,2048,2048]{3,2,1,0:T(8,128)(2,1)S(1)} %copy-done.1, bf16[512,256]{1,0:T(8,128)(2,1)S(1)} %get-tuple-element.32.refs_0_, bf16[512,256]{1,0:T(8,128)(2,1)S(1)} %collective-permute-done.19.refs_1_, ...), custom_call_target="tpu_custom_call" | custom-call | flops 1073741824 | bytes 2228224 | tf_op jit(solution)/shard_map/up_first/pallas_call | solution.py:49
  94.1 3.7 %up_rest.3 = (f32[512,256]{1,0:T(8,128)S(1)}, f32[512,256]{1,0:T(8,128)S(1)}, f32[512,256]{1,0:T(8,128)S(1)}) custom-call(bf16[1,2,2048,2048]{3,2,1,0:T(8,128)(2,1)S(1)} %copy-done.1, bf16[2,2048,256]{2,1,0:T(8,128)(2,1)S(1)} %get-tuple-element.26.pair_ref), custom_call_target="tpu_custom_call" | custom-call | flops 3221225472 | bytes 2359296 | tf_op jit(solution)/shard_map/up_rest/pallas_call | solution.py:49
  97.8 4.0 %collective-permute-done.14.refs_3_ = bf16[512,256]{1,0:T(8,128)(2,1)S(1)} collective-permute-done((bf16[512,256]{1,0:T(8,128)(2,1)S(1)}, bf16[512,256]{1,0:T(8,128)(2,1)S(1)}, u32[]{:S(2)}, u32[]{:S(2)}) %collective-permute-start.14) | collective-permute-done | bytes 262176 | tf_op jit(solution)/shard_map/ppermute | solution.py:35
  101.7 2.6 %down_first.3 = (bf16[2,2048,256]{2,1,0:T(8,128)(2,1)S(1)}, f32[2,512,256]{2,1,0:T(8,128)S(1)}) custom-call(bf16[1,2,2048,2048]{3,2,1,0:T(8,128)(2,1)S(1)} %copy-done.1, bf16[512,256]{1,0:T(8,128)(2,1)S(1)} %add_convert_fusion.3.refs_0_, bf16[512,256]{1,0:T(8,128)(2,1)S(1)} %collective-permute-done.12.refs_1_, ...), custom_call_target="tpu_custom_call" | custom-call | flops 2147483648 | bytes 2228224 | tf_op jit(solution)/shard_map/down_first/pallas_call | solution.py:49
  104.5 1.9 %collective-permute-start.23 = (bf16[512,256]{1,0:T(8,128)(2,1)S(1)}, bf16[512,256]{1,0:T(8,128)(2,1)S(1)}, u32[]{:S(2)}, u32[]{:S(2)}) collective-permute-start(bf16[512,256]{1,0:T(8,128)(2,1)S(1)} %add_convert_fusion.1), channel_id=1, source_target_pairs={{0,8},{8,12},{12,4},{4,0},{1,9},{9,13},{13,5},{5,1},{2,10},{10,14}... | collective-permute-start | bytes 786440 | tf_op jit(solution)/shard_map/ppermute | solution.py:35
  106.4 6.9 %collective-permute-done.23 = bf16[512,256]{1,0:T(8,128)(2,1)S(1)} collective-permute-done((bf16[512,256]{1,0:T(8,128)(2,1)S(1)}, bf16[512,256]{1,0:T(8,128)(2,1)S(1)}, u32[]{:S(2)}, u32[]{:S(2)}) %collective-permute-start.23) | collective-permute-done | bytes 262176 | tf_op jit(solution)/shard_map/ppermute | solution.py:35
  113.3 2.8 %collective-permute-start.24 = (bf16[512,256]{1,0:T(8,128)(2,1)S(1)}, bf16[512,256]{1,0:T(8,128)(2,1)S(1)}, u32[]{:S(2)}, u32[]{:S(2)}) collective-permute-start(bf16[512,256]{1,0:T(8,128)(2,1)S(1)} %add_convert_fusion), channel_id=1, source_target_pairs={{0,8},{8,12},{12,4},{4,0},{1,9},{9,13},{13,5},{5,1},{2,10},{10,14}... | collective-permute-start | bytes 786440 | tf_op jit(solution)/shard_map/ppermute | solution.py:35
  116.1 2.3 %down_second.3 = f32[2,512,256]{2,1,0:T(8,128)S(1)} custom-call(bf16[1,2,2048,2048]{3,2,1,0:T(8,128)(2,1)S(1)} %bitcast.33, bf16[2,2048,256]{2,1,0:T(8,128)(2,1)S(1)} %get-tuple-element.23.pair_ref), custom_call_target="tpu_custom_call" | custom-call | flops 2147483648 | bytes 2359296 | tf_op jit(solution)/shard_map/down_second/pallas_call | solution.py:49
  118.4 3.1 %collective-permute-done.24 = bf16[512,256]{1,0:T(8,128)(2,1)S(1)} collective-permute-done((bf16[512,256]{1,0:T(8,128)(2,1)S(1)}, bf16[512,256]{1,0:T(8,128)(2,1)S(1)}, u32[]{:S(2)}, u32[]{:S(2)}) %collective-permute-start.24) | collective-permute-done | bytes 262176 | tf_op jit(solution)/shard_map/ppermute | solution.py:35
  124.1 6.8 %collective-permute-done.25 = bf16[512,256]{1,0:T(8,128)(2,1)S(1)} collective-permute-done((bf16[512,256]{1,0:T(8,128)(2,1)S(1)}, bf16[512,256]{1,0:T(8,128)(2,1)S(1)}, u32[]{:S(2)}, u32[]{:S(2)}) %collective-permute-start.25) | collective-permute-done | bytes 262176 | tf_op jit(solution)/shard_map/ppermute | solution.py:44
  131.8 3.9 %collective-permute-start.17 = (bf16[512,256]{1,0:T(8,128)(2,1)S(1)}, bf16[512,256]{1,0:T(8,128)(2,1)S(1)}, u32[]{:S(2)}, u32[]{:S(2)}) collective-permute-start(bf16[512,256]{1,0:T(8,128)(2,1)S(1)} %get-tuple-element.31), channel_id=1, source_target_pairs={{0,16},{1,17},{2,18},{3,19},{4,20},{5,21},{6,22},{7,23},{8,24},{9,... | collective-permute-start | bytes 786440 | tf_op jit(solution)/shard_map/ppermute | solution.py:44
  135.8 3.9 %collective-permute-done.17 = bf16[512,256]{1,0:T(8,128)(2,1)S(1)} collective-permute-done((bf16[512,256]{1,0:T(8,128)(2,1)S(1)}, bf16[512,256]{1,0:T(8,128)(2,1)S(1)}, u32[]{:S(2)}, u32[]{:S(2)}) %collective-permute-start.17) | collective-permute-done | bytes 262176 | tf_op jit(solution)/shard_map/ppermute | solution.py:44
  (72 shorter events, 18.2 us)
Async XLA Ops:
  1.7 9.3 %collective-permute-start.7 = (bf16[512,256]{1,0:T(8,128)(2,1)S(1)}, bf16[512,256]{1,0:T(8,128)(2,1)S(1)}, u32[]{:S(2)}, u32[]{:S(2)}) collective-permute-start(bf16[512,256]{1,0:T(8,128)(2,1)S(1)} %convert_bitcast_fusion.refs_0_), channel_id=1, source_target_pairs={{0,2},{1,3},{2,0},{3,1},{4,6},{5,7},{6,4},{7,5},{8,10},{9,11},{10,... | collective-permute-start | bytes 786440 | tf_op jit(solution)/shard_map/ppermute | solution.py:39
  5.8 7.9 %collective-permute-start = (bf16[512,256]{1,0:T(8,128)(2,1)S(1)}, bf16[512,256]{1,0:T(8,128)(2,1)S(1)}, u32[]{:S(2)}, u32[]{:S(2)}) collective-permute-start(bf16[512,256]{1,0:T(8,128)(2,1)S(1)} %convert_bitcast_fusion.1.refs_0_), channel_id=1, source_target_pairs={{0,8},{8,12},{12,4},{4,0},{1,9},{9,13},{13,5},{5,1},{2,10},{10,14}... | collective-permute-start | bytes 786440 | tf_op jit(solution)/shard_map/ppermute | solution.py:35
  8.4 8.7 %collective-permute-start.6 = (bf16[512,256]{1,0:T(8,128)(2,1)S(1)}, bf16[512,256]{1,0:T(8,128)(2,1)S(1)}, u32[]{:S(2)}, u32[]{:S(2)}) collective-permute-start(bf16[512,256]{1,0:T(8,128)(2,1)S(1)} %convert_bitcast_fusion.refs_0_), channel_id=1, source_target_pairs={{0,1},{1,0},{2,3},{3,2},{4,5},{5,4},{6,7},{7,6},{8,9},{9,8},{10,11... | collective-permute-start | bytes 786440 | tf_op jit(solution)/shard_map/ppermute | solution.py:39
  11.0 6.1 %collective-permute-start.8 = (bf16[512,256]{1,0:T(8,128)(2,1)S(1)}, bf16[512,256]{1,0:T(8,128)(2,1)S(1)}, u32[]{:S(2)}, u32[]{:S(2)}) collective-permute-start(bf16[512,256]{1,0:T(8,128)(2,1)S(1)} %collective-permute-done.7.refs_2_), channel_id=1, source_target_pairs={{0,1},{1,0},{2,3},{3,2},{4,5},{5,4},{6,7},{7,6},{8,9},{9,8},{10,11... | collective-permute-start | bytes 786440 | tf_op jit(solution)/shard_map/ppermute | solution.py:39
  13.7 11.5 %collective-permute-start.1 = (bf16[512,256]{1,0:T(8,128)(2,1)S(1)}, bf16[512,256]{1,0:T(8,128)(2,1)S(1)}, u32[]{:S(2)}, u32[]{:S(2)}) collective-permute-start(bf16[512,256]{1,0:T(8,128)(2,1)S(1)} %collective-permute-done.refs_1_), channel_id=1, source_target_pairs={{0,8},{8,12},{12,4},{4,0},{1,9},{9,13},{13,5},{5,1},{2,10},{10,14}... | collective-permute-start | bytes 786440 | tf_op jit(solution)/shard_map/ppermute | solution.py:35
  24.5 14.9 %collective-permute-start.9 = (bf16[512,256]{1,0:T(8,128)(2,1)S(1)}, bf16[512,256]{1,0:T(8,128)(2,1)S(1)}, u32[]{:S(2)}, u32[]{:S(2)}) collective-permute-start(bf16[512,256]{1,0:T(8,128)(2,1)S(1)} %get-tuple-element.18), channel_id=1, source_target_pairs={{0,8},{8,12},{12,4},{4,0},{1,9},{9,13},{13,5},{5,1},{2,10},{10,14}... | collective-permute-start | bytes 786440 | tf_op jit(solution)/shard_map/ppermute | solution.py:35
  25.2 11.6 %collective-permute-start.2 = (bf16[512,256]{1,0:T(8,128)(2,1)S(1)}, bf16[512,256]{1,0:T(8,128)(2,1)S(1)}, u32[]{:S(2)}, u32[]{:S(2)}) collective-permute-start(bf16[512,256]{1,0:T(8,128)(2,1)S(1)} %collective-permute-done.1.refs_2_), channel_id=1, source_target_pairs={{0,8},{8,12},{12,4},{4,0},{1,9},{9,13},{13,5},{5,1},{2,10},{10,14}... | collective-permute-start | bytes 786440 | tf_op jit(solution)/shard_map/ppermute | solution.py:35
  26.4 24.4 %slice-start = ((s8[16777216]{0:T(1024)(128)(4,1)}), s8[4194304]{0:T(1024)(128)(4,1)S(1)}, s32[]{:S(2)}) async-start(s8[16777216]{0:T(1024)(128)(4,1)} %bitcast.30), calls=%async_computation | async-start | bytes 8388608
  26.4 24.4 %slice-start.1 = ((s8[16777216]{0:T(1024)(128)(4,1)}), s8[4194304]{0:T(1024)(128)(4,1)S(1)}, s32[]{:S(2)}) async-start(s8[16777216]{0:T(1024)(128)(4,1)} %bitcast.30), calls=%async_computation.1 | async-start | bytes 8388608
  30.1 20.7 %slice-start.2 = ((s8[16777216]{0:T(1024)(128)(4,1)}), s8[4194304]{0:T(1024)(128)(4,1)S(1)}, s32[]{:S(2)}) async-start(s8[16777216]{0:T(1024)(128)(4,1)} %bitcast.30), calls=%async_computation.2 | async-start | bytes 8388608
  30.1 20.7 %slice-start.3 = ((s8[16777216]{0:T(1024)(128)(4,1)}), s8[4194304]{0:T(1024)(128)(4,1)S(1)}, s32[]{:S(2)}) async-start(s8[16777216]{0:T(1024)(128)(4,1)} %bitcast.30), calls=%async_computation.3 | async-start | bytes 8388608
  39.4 18.5 %collective-permute-start.3 = (f32[2,512,256]{2,1,0:T(8,128)S(1)}, f32[2,512,256]{2,1,0:T(8,128)S(1)}, u32[]{:S(2)}, u32[]{:S(2)}) collective-permute-start(f32[2,512,256]{2,1,0:T(8,128)S(1)} %get-tuple-element.17), channel_id=1, source_target_pairs={{0,1},{1,0},{2,3},{3,2},{4,5},{5,4},{6,7},{7,6},{8,9},{9,8},{10,11... | collective-permute-start | bytes 3145736 | tf_op jit(solution)/shard_map/ppermute | solution.py:39
  39.5 8.7 %collective-permute-start.10 = (bf16[512,256]{1,0:T(8,128)(2,1)S(1)}, bf16[512,256]{1,0:T(8,128)(2,1)S(1)}, u32[]{:S(2)}, u32[]{:S(2)}) collective-permute-start(bf16[512,256]{1,0:T(8,128)(2,1)S(1)} %add_convert_fusion.5), channel_id=1, source_target_pairs={{0,8},{8,12},{12,4},{4,0},{1,9},{9,13},{13,5},{5,1},{2,10},{10,14}... | collective-permute-start | bytes 786440 | tf_op jit(solution)/shard_map/ppermute | solution.py:35
  48.3 8.0 %collective-permute-start.11 = (bf16[512,256]{1,0:T(8,128)(2,1)S(1)}, bf16[512,256]{1,0:T(8,128)(2,1)S(1)}, u32[]{:S(2)}, u32[]{:S(2)}) collective-permute-start(bf16[512,256]{1,0:T(8,128)(2,1)S(1)} %add_convert_fusion.4), channel_id=1, source_target_pairs={{0,8},{8,12},{12,4},{4,0},{1,9},{9,13},{13,5},{5,1},{2,10},{10,14}... | collective-permute-start | bytes 786440 | tf_op jit(solution)/shard_map/ppermute | solution.py:35
  56.4 9.1 %collective-permute-start.18 = (bf16[512,256]{1,0:T(8,128)(2,1)S(1)}, bf16[512,256]{1,0:T(8,128)(2,1)S(1)}, u32[]{:S(2)}, u32[]{:S(2)}) collective-permute-start(bf16[512,256]{1,0:T(8,128)(2,1)S(1)} %fusion.2), channel_id=1, source_target_pairs={{16,0},{17,1},{18,2},{19,3},{20,4},{21,5},{22,6},{23,7},{24,8},{25... | collective-permute-start | bytes 786440 | tf_op jit(solution)/shard_map/ppermute | solution.py:44
  58.0 7.4 %collective-permute-start.4 = (bf16[512,256]{1,0:T(8,128)(2,1)S(1)}, bf16[512,256]{1,0:T(8,128)(2,1)S(1)}, u32[]{:S(2)}, u32[]{:S(2)}) collective-permute-start(bf16[512,256]{1,0:T(8,128)(2,1)S(1)} %fusion.6), channel_id=1, source_target_pairs={{0,2},{1,3},{2,0},{3,1},{4,6},{5,7},{6,4},{7,5},{8,10},{9,11},{10,... | collective-permute-start | bytes 786440 | tf_op jit(solution)/shard_map/ppermute | solution.py:39
  65.6 7.8 %collective-permute-start.5 = (bf16[512,256]{1,0:T(8,128)(2,1)S(1)}, bf16[512,256]{1,0:T(8,128)(2,1)S(1)}, u32[]{:S(2)}, u32[]{:S(2)}) collective-permute-start(bf16[512,256]{1,0:T(8,128)(2,1)S(1)} %get-tuple-element.33), channel_id=1, source_target_pairs={{0,16},{1,17},{2,18},{3,19},{4,20},{5,21},{6,22},{7,23},{8,24},{9,... | collective-permute-start | bytes 786440 | tf_op jit(solution)/shard_map/ppermute | solution.py:44
  69.6 7.4 %collective-permute-start.20 = (bf16[512,256]{1,0:T(8,128)(2,1)S(1)}, bf16[512,256]{1,0:T(8,128)(2,1)S(1)}, u32[]{:S(2)}, u32[]{:S(2)}) collective-permute-start(bf16[512,256]{1,0:T(8,128)(2,1)S(1)} %get-tuple-element.32.refs_0_), channel_id=1, source_target_pairs={{0,2},{1,3},{2,0},{3,1},{4,6},{5,7},{6,4},{7,5},{8,10},{9,11},{10,... | collective-permute-start | bytes 786440 | tf_op jit(solution)/shard_map/ppermute | solution.py:39
  73.6 8.1 %collective-permute-start.12 = (bf16[512,256]{1,0:T(8,128)(2,1)S(1)}, bf16[512,256]{1,0:T(8,128)(2,1)S(1)}, u32[]{:S(2)}, u32[]{:S(2)}) collective-permute-start(bf16[512,256]{1,0:T(8,128)(2,1)S(1)} %add_convert_fusion.3.refs_0_), channel_id=1, source_target_pairs={{0,8},{8,12},{12,4},{4,0},{1,9},{9,13},{13,5},{5,1},{2,10},{10,14}... | collective-permute-start | bytes 786440 | tf_op jit(solution)/shard_map/ppermute | solution.py:35
  76.9 8.1 %collective-permute-start.19 = (bf16[512,256]{1,0:T(8,128)(2,1)S(1)}, bf16[512,256]{1,0:T(8,128)(2,1)S(1)}, u32[]{:S(2)}, u32[]{:S(2)}) collective-permute-start(bf16[512,256]{1,0:T(8,128)(2,1)S(1)} %get-tuple-element.32.refs_0_), channel_id=1, source_target_pairs={{0,1},{1,0},{2,3},{3,2},{4,5},{5,4},{6,7},{7,6},{8,9},{9,8},{10,11... | collective-permute-start | bytes 786440 | tf_op jit(solution)/shard_map/ppermute | solution.py:39
  76.9 8.1 %collective-permute-start.21 = (bf16[512,256]{1,0:T(8,128)(2,1)S(1)}, bf16[512,256]{1,0:T(8,128)(2,1)S(1)}, u32[]{:S(2)}, u32[]{:S(2)}) collective-permute-start(bf16[512,256]{1,0:T(8,128)(2,1)S(1)} %collective-permute-done.20.refs_2_), channel_id=1, source_target_pairs={{0,1},{1,0},{2,3},{3,2},{4,5},{5,4},{6,7},{7,6},{8,9},{9,8},{10,11... | collective-permute-start | bytes 786440 | tf_op jit(solution)/shard_map/ppermute | solution.py:39
  81.7 10.9 %collective-permute-start.13 = (bf16[512,256]{1,0:T(8,128)(2,1)S(1)}, bf16[512,256]{1,0:T(8,128)(2,1)S(1)}, u32[]{:S(2)}, u32[]{:S(2)}) collective-permute-start(bf16[512,256]{1,0:T(8,128)(2,1)S(1)} %collective-permute-done.12.refs_1_), channel_id=1, source_target_pairs={{0,8},{8,12},{12,4},{4,0},{1,9},{9,13},{13,5},{5,1},{2,10},{10,14}... | collective-permute-start | bytes 786440 | tf_op jit(solution)/shard_map/ppermute | solution.py:35
  92.5 11.9 %collective-permute-start.22 = (bf16[512,256]{1,0:T(8,128)(2,1)S(1)}, bf16[512,256]{1,0:T(8,128)(2,1)S(1)}, u32[]{:S(2)}, u32[]{:S(2)}) collective-permute-start(bf16[512,256]{1,0:T(8,128)(2,1)S(1)} %get-tuple-element.25), channel_id=1, source_target_pairs={{0,8},{8,12},{12,4},{4,0},{1,9},{9,13},{13,5},{5,1},{2,10},{10,14}... | collective-permute-start | bytes 786440 | tf_op jit(solution)/shard_map/ppermute | solution.py:35
  92.6 9.2 %collective-permute-start.14 = (bf16[512,256]{1,0:T(8,128)(2,1)S(1)}, bf16[512,256]{1,0:T(8,128)(2,1)S(1)}, u32[]{:S(2)}, u32[]{:S(2)}) collective-permute-start(bf16[512,256]{1,0:T(8,128)(2,1)S(1)} %collective-permute-done.13.refs_2_), channel_id=1, source_target_pairs={{0,8},{8,12},{12,4},{4,0},{1,9},{9,13},{13,5},{5,1},{2,10},{10,14}... | collective-permute-start | bytes 786440 | tf_op jit(solution)/shard_map/ppermute | solution.py:35
  94.1 22.0 %slice-start.4 = ((s8[16777216]{0:T(1024)(128)(4,1)}), s8[4194304]{0:T(1024)(128)(4,1)S(1)}, s32[]{:S(2)}) async-start(s8[16777216]{0:T(1024)(128)(4,1)} %bitcast.32), calls=%async_computation.4 | async-start | bytes 8388608
  94.1 22.0 %slice-start.5 = ((s8[16777216]{0:T(1024)(128)(4,1)}), s8[4194304]{0:T(1024)(128)(4,1)S(1)}, s32[]{:S(2)}) async-start(s8[16777216]{0:T(1024)(128)(4,1)} %bitcast.32), calls=%async_computation.5 | async-start | bytes 8388608
  104.3 18.5 %collective-permute-start.15 = (f32[2,512,256]{2,1,0:T(8,128)S(1)}, f32[2,512,256]{2,1,0:T(8,128)S(1)}, u32[]{:S(2)}, u32[]{:S(2)}) collective-permute-start(f32[2,512,256]{2,1,0:T(8,128)S(1)} %get-tuple-element.24), channel_id=1, source_target_pairs={{0,1},{1,0},{2,3},{3,2},{4,5},{5,4},{6,7},{7,6},{8,9},{9,8},{10,11... | collective-permute-start | bytes 3145736 | tf_op jit(solution)/shard_map/ppermute | solution.py:39
  104.5 8.7 %collective-permute-start.23 = (bf16[512,256]{1,0:T(8,128)(2,1)S(1)}, bf16[512,256]{1,0:T(8,128)(2,1)S(1)}, u32[]{:S(2)}, u32[]{:S(2)}) collective-permute-start(bf16[512,256]{1,0:T(8,128)(2,1)S(1)} %add_convert_fusion.1), channel_id=1, source_target_pairs={{0,8},{8,12},{12,4},{4,0},{1,9},{9,13},{13,5},{5,1},{2,10},{10,14}... | collective-permute-start | bytes 786440 | tf_op jit(solution)/shard_map/ppermute | solution.py:35
  113.3 8.2 %collective-permute-start.24 = (bf16[512,256]{1,0:T(8,128)(2,1)S(1)}, bf16[512,256]{1,0:T(8,128)(2,1)S(1)}, u32[]{:S(2)}, u32[]{:S(2)}) collective-permute-start(bf16[512,256]{1,0:T(8,128)(2,1)S(1)} %add_convert_fusion), channel_id=1, source_target_pairs={{0,8},{8,12},{12,4},{4,0},{1,9},{9,13},{13,5},{5,1},{2,10},{10,14}... | collective-permute-start | bytes 786440 | tf_op jit(solution)/shard_map/ppermute | solution.py:35
  121.6 9.3 %collective-permute-start.25 = (bf16[512,256]{1,0:T(8,128)(2,1)S(1)}, bf16[512,256]{1,0:T(8,128)(2,1)S(1)}, u32[]{:S(2)}, u32[]{:S(2)}) collective-permute-start(bf16[512,256]{1,0:T(8,128)(2,1)S(1)} %fusion.3), channel_id=1, source_target_pairs={{16,0},{17,1},{18,2},{19,3},{20,4},{21,5},{22,6},{23,7},{24,8},{25... | collective-permute-start | bytes 786440 | tf_op jit(solution)/shard_map/ppermute | solution.py:44
  123.0 7.9 %collective-permute-start.16 = (bf16[512,256]{1,0:T(8,128)(2,1)S(1)}, bf16[512,256]{1,0:T(8,128)(2,1)S(1)}, u32[]{:S(2)}, u32[]{:S(2)}) collective-permute-start(bf16[512,256]{1,0:T(8,128)(2,1)S(1)} %fusion.7), channel_id=1, source_target_pairs={{0,2},{1,3},{2,0},{3,1},{4,6},{5,7},{6,4},{7,5},{8,10},{9,11},{10,... | collective-permute-start | bytes 786440 | tf_op jit(solution)/shard_map/ppermute | solution.py:39
  131.8 7.8 %collective-permute-start.17 = (bf16[512,256]{1,0:T(8,128)(2,1)S(1)}, bf16[512,256]{1,0:T(8,128)(2,1)S(1)}, u32[]{:S(2)}, u32[]{:S(2)}) collective-permute-start(bf16[512,256]{1,0:T(8,128)(2,1)S(1)} %get-tuple-element.31), channel_id=1, source_target_pairs={{0,16},{1,17},{2,18},{3,19},{4,20},{5,21},{6,22},{7,23},{8,24},{9,... | collective-permute-start | bytes 786440 | tf_op jit(solution)/shard_map/ppermute | solution.py:44
  (7 other events, 91.4 us)

commit v2 on v1

v2 whole, which is shorter than its diff:
```python
import functools

import jax
import jax.numpy as jnp
from jax import lax
from jax.experimental import pallas as pl
from jax.experimental.pallas import tpu as pltpu
from jax.sharding import PartitionSpec as P

PASSES = 2
F32 = jnp.float32
BF16 = jnp.bfloat16
WHOLE = pl.BlockSpec(memory_space=pltpu.VMEM)
UNREAD = pl.BlockSpec(memory_space=pl.ANY)
LANES = 128
DECLARED = 21 * 10**9
CONTRACT_ROWS = (((0,), (0,)), ((), ()))


def ring_device(place, size):
    half = (size + 1) // 2
    if isinstance(place, int):
        return 2 * place if place < half else 2 * (size - 1 - place) + 1
    return jnp.where(place < half, 2 * place, 2 * (size - 1 - place) + 1)


def ring_place(device, size):
    return jnp.where(lax.rem(device, 2) == 0, device // 2, size - 1 - device // 2)


def ring_block(behind, size):
    place = ring_place(lax.axis_index("row"), size)
    return ring_device(lax.rem(place - behind + size, size), size)


def ring_hop(x, size):
    pairs = [(ring_device(p, size), ring_device((p + 1) % size, size)) for p in range(size)]
    return lax.ppermute(x, "row", pairs)


def col_swap(x, bit):
    return lax.ppermute(x, "col", [(c, c ^ bit) for c in range(lax.axis_size("col"))])


def depth_shift(x, by):
    peers = lax.axis_size("depth")
    return lax.ppermute(x, "depth", [(i, i + by) for i in range(peers) if 0 <= i + by < peers])


def call(kernel, outs, name, args, after=()):
    count = len(args)

    def ordered(*refs):
        kernel(*refs[:count], *refs[count + len(after) :])

    return pl.pallas_call(
        ordered,
        in_specs=[WHOLE] * count + [UNREAD] * len(after),
        out_specs=[WHOLE] * len(outs),
        out_shape=outs,
        name=name,
        cost_estimate=pl.CostEstimate(flops=DECLARED, bytes_accessed=2**20, transcendentals=0),
        compiler_params=pltpu.CompilerParams(vmem_limit_bytes=12 * 2**20),
    )(*args, *after)


def array(shape, dtype):
    return jax.ShapeDtypeStruct(shape, dtype)


def behind(x, *others):
    return lax.optimization_barrier((x, *others))[0]


def rows_at(block, strip):
    return pl.ds(pl.multiple_of(block * strip, strip), strip)


def hold(prop, after):
    def kernel(w_ref, _, out_ref, sem):
        copy = pltpu.make_async_copy(w_ref, out_ref, sem)
        copy.start()
        copy.wait()

    return pl.pallas_call(
        kernel,
        in_specs=[pl.BlockSpec(memory_space=pltpu.HBM), UNREAD],
        out_specs=WHOLE,
        out_shape=pltpu.VMEM(prop.shape, prop.dtype),
        scratch_shapes=[pltpu.SemaphoreType.DMA],
        name="hold",
        cost_estimate=pl.CostEstimate(flops=0, bytes_accessed=40 * prop.size, transcendentals=0),
        compiler_params=pltpu.CompilerParams(vmem_limit_bytes=36 * 2**20),
    )(prop, after)


def place_block(pair_ref, block_ref, rows, sources):
    values = block_ref[...]
    pair_ref[0, rows, :] = values
    pair_ref[1, rows, :sources] = -values[:, sources:]
    pair_ref[1, rows, sources:] = values[:, :sources]


def spread(refl_ref):
    return jnp.broadcast_to(refl_ref[...], (LANES, refl_ref.shape[1])).T


def scaled(refl_ref, values):
    factor = refl_ref[...]
    pieces = [factor * values[:, k : k + LANES] for k in range(0, values.shape[1], LANES)]
    return jnp.concatenate(pieces, axis=1)


def ready_kernel(field_ref, refl_ref, low_ref, factor_ref):
    low_ref[...] = field_ref[0].astype(BF16)
    factor_ref[...] = spread(refl_ref)


def down_dot(w_ref, pair_ref, rows):
    return jnp.dot(w_ref[0, 0, rows, :], pair_ref[0], preferred_element_type=F32) + jnp.dot(
        w_ref[0, 1, rows, :], pair_ref[1], preferred_element_type=F32
    )


def up_dot(w_ref, pair_ref, columns):
    return lax.dot_general(
        w_ref[0, 0, :, columns], pair_ref[0], CONTRACT_ROWS, preferred_element_type=F32
    ) + lax.dot_general(w_ref[0, 1, :, columns], pair_ref[1], CONTRACT_ROWS, preferred_element_type=F32)


def down_sibling_kernel(size, strip, sources, w_ref, *refs):
    blocks, pair_ref, out_ref = refs[:size], refs[size], refs[size + 1]
    for s in range(size):
        place_block(pair_ref, blocks[s], rows_at(ring_block(s, size), strip), sources)
    me = lax.axis_index("col")
    for k in range(2):
        out_ref[k] = down_dot(w_ref, pair_ref, rows_at(me ^ (1 + 2 * k), strip))


def down_far_kernel(strip, w_ref, pair_ref, out_ref):
    out_ref[...] = down_dot(w_ref, pair_ref, rows_at(lax.axis_index("col") ^ 2, strip))


def far_sum_kernel(own_ref, arrived_ref, out_ref):
    out_ref[...] = (own_ref[...] + arrived_ref[1]).astype(BF16)


def down_own_kernel(strip, w_ref, pair_ref, arrived_ref, out_ref):
    out_ref[...] = down_dot(w_ref, pair_ref, rows_at(lax.axis_index("col"), strip)) + arrived_ref[0]


def up_first_kernel(size, strip, sources, w_ref, *refs):
    blocks, pair_ref, out_ref = refs[:4], refs[4], refs[5]
    me = lax.axis_index("col")
    for s in range(4):
        place_block(pair_ref, blocks[s], rows_at(me ^ s, strip), sources)
    out_ref[...] = up_dot(w_ref, pair_ref, rows_at(ring_block(1, size), strip)).astype(BF16)


def up_rest_kernel(size, strip, w_ref, pair_ref, *out_refs):
    for s in range(2, size + 1):
        out_refs[s - 2][...] = up_dot(w_ref, pair_ref, rows_at(ring_block(s % size, size), strip))


def hop_kernel(arrived_ref, own_ref, out_ref):
    out_ref[...] = (arrived_ref[...].astype(F32) + own_ref[...]).astype(BF16)


def both_kernel(arrived_ref, own_ref, full_ref, low_ref):
    total = arrived_ref[...].astype(F32) + own_ref[...]
    full_ref[...] = total
    low_ref[...] = total.astype(BF16)


def next_up_kernel(below_ref, refl_ref, trans_ref, out_ref):
    total = below_ref[...].astype(F32) + scaled(refl_ref, trans_ref[...])
    out_ref[...] = total.astype(out_ref.dtype).reshape(out_ref.shape)


def next_down_kernel(above_ref, source_ref, refl_ref, back_ref, out_ref):
    reflected = scaled(refl_ref, back_ref[...])
    at_surface = lax.axis_index("depth") == 0

    @pl.when(at_surface)
    def _():
        out_ref[...] = (source_ref[...] + reflected).astype(out_ref.dtype).reshape(out_ref.shape)

    @pl.when(jnp.logical_not(at_surface))
    def _():
        out_ref[...] = (above_ref[...].astype(F32) + reflected).astype(out_ref.dtype).reshape(out_ref.shape)


def body(prop, source, down_init, up_init, refl_down, refl_up):
    size = lax.axis_size("row")
    assert lax.axis_size("col") == 4
    strip = down_init.shape[1]
    width = down_init.shape[2]
    sources = width // 2
    tall, wide = prop.shape[2], prop.shape[3]
    low, full = array((strip, width), BF16), array((strip, width), F32)
    factor = array((strip, LANES), F32)
    up_low, refl_below = call(ready_kernel, [low, factor], "ready_up", [up_init, refl_up])
    down_low, refl_above = call(
        ready_kernel, [low, factor], "ready_down", [down_init, refl_down], [up_low]
    )
    w = pltpu.with_memory_space_constraint(hold(prop, down_low), pltpu.VMEM)
    for sweep in range(PASSES):
        last = sweep == PASSES - 1
        near = col_swap(up_low, 1)
        far = col_swap(up_low, 2)
        if sweep == 0:
            far = behind(far, w)
        blocks_up = [up_low, near, far, col_swap(far, 1)]
        blocks_down = [down_low, ring_hop(down_low, size)]
        pair_up, travelling = call(
            functools.partial(up_first_kernel, size, strip, sources),
            [array((2, tall, width), BF16), low], "up_first", [w, *blocks_up], [blocks_down[1]],
        )
        for s in range(1, size - 1):
            blocks_down.append(ring_hop(blocks_down[-1], size))
        own_up = call(
            functools.partial(up_rest_kernel, size, strip),
            [full] * (size - 1), "up_rest", [w, pair_up], [blocks_down[1]],
        )
        pair_down, to_sibling = call(
            functools.partial(down_sibling_kernel, size, strip, sources),
            [array((2, wide, width), BF16), array((2, strip, width), F32)],
            "down_sibling", [w, *blocks_down], [own_up[0]],
        )
        from_sibling = col_swap(to_sibling, 1)
        (own_far,) = call(functools.partial(down_far_kernel, strip), [full], "down_far", [w, pair_down])
        (to_far,) = call(far_sum_kernel, [low], "far_sum", [own_far, from_sibling])
        from_far = col_swap(to_far, 2)
        (own_down,) = call(
            functools.partial(down_own_kernel, strip), [full], "down_own",             [w, pair_down, from_sibling], [to_far],
        )
        for s in range(size - 2):
            arrived = ring_hop(travelling, size)
            (travelling,) = call(
                hop_kernel, [low], "hop", [arrived, own_up[s]], [to_far] if s == size - 3 else [own_up[-1]]
            )
        back, back_low = call(
            both_kernel, [full, low], "back", [ring_hop(travelling, size), own_up[size - 2]], [own_down]
        )
        from_below = depth_shift(back_low, -1)
        trans, trans_low = call(both_kernel, [full, low], "trans", [from_far, own_down])
        from_above = depth_shift(trans_low, 1)
        kind = array((1, strip, width), F32) if last else low
        (up_low,) = call(next_up_kernel, [kind], "next_up", [from_below, refl_below, trans])
        (down_low,) = call(
            next_down_kernel, [kind], "next_down", [from_above, source, refl_above, back]
        )
    return (down_low, up_low)


def solution(mesh):
    placed = (
        P("depth", None, "row", "col"),
        P(("row", "col"), None),
        P("depth", ("row", "col"), None),
        P("depth", ("row", "col"), None),
        P("depth", ("row", "col")),
        P("depth", ("row", "col")),
    )
    return jax.shard_map(
        body,
        mesh=mesh,
        in_specs=placed,
        out_specs=(P("depth", ("row", "col"), None), P("depth", ("row", "col"), None)),
        check_vma=False,
    )
```

time: 141 us -> 118 us (0.84)
  waiting for transfers between devices: 60.3 us -> 32.9 us
  starting transfers between devices: 42.2 us -> 52.7 us
  local copies, waits for them, and re-layouts: 11.7 us -> 1.73 us
  Pallas kernels: 20.5 us -> 29.4 us
  other arithmetic: 4.92 us -> 0 us
    ppermute x12, waiting for transfers between devices: 37.8 us -> 21.9 us  [ring_hop(): return lax.ppermute(x, 'row', pairs)]
    ppermute x4, waiting for transfers between devices: 19.9 us -> 6.77 us  [depth_shift(): lax.ppermute(x, 'depth', [(i, i + by) for i in range(peers) if 0 <= i + b...]
    unnamed x26 -> x12, local copies, waits for them, and re-layouts: 11.6 us -> 1.73 us
    ppermute x12, starting transfers between devices: 24.8 us -> 34 us  [ring_hop(): return lax.ppermute(x, 'row', pairs)]
    pallas_call x8 -> x27, Pallas kernels: 20.5 us -> 29.4 us  [the longest x26 23.6 us: call(): pl.pallas_call(ordered, in_specs=[WHOLE] * count + [UNREAD] * len(after),...]
    convert_element_type x10 -> x0, other arithmetic: 2.78 us -> none  [the longest x1 1.07 us: body(): up_low = up_init[0].astype(BF16)]
    broadcast_in_dim x2 -> x0, other arithmetic: 1.87 us -> none  [body(): return (down[None], up[None])]
    ppermute x10, waiting for transfers between devices: 2.61 us -> 4.23 us  [col_swap(): lax.ppermute(x, 'col', [(c, c ^ bit) for c in range(lax.axis_size('col'))])]
  transfers between devices with their start and end apart: 26 -> 26, of which waited for: 13 -> 16; matrix products, arithmetic and copies ran while one was open for 1% -> 0% of each run, Pallas kernels for 15% -> 24%
where the time goes in v2:
time: 118 us
  starting transfers between devices  52.7 us (45%)
  waiting for transfers between devices  32.9 us (28%)
  Pallas kernels  29.4 us (25%)
  local copies, waits for them, and re-layouts  1.73 us (1%)
    ppermute x12, starting transfers between devices, ring_hop(): return lax.ppermute(x, 'row', pairs)  34 us
    pallas_call x26, Pallas kernels, call(): pl.pallas_call(ordered, in_specs=[WHOLE] * count + [UNREAD] * len(after),...  23.6 us
    ppermute x12, waiting for transfers between devices, ring_hop(): return lax.ppermute(x, 'row', pairs)  21.9 us
    ppermute x4, starting transfers between devices, depth_shift(): lax.ppermute(x, 'depth', [(i, i + by) for i in range(peers) if 0 <= i + b...  11.7 us
    ppermute x10, starting transfers between devices, col_swap(): lax.ppermute(x, 'col', [(c, c ^ bit) for c in range(lax.axis_size('col'))])  7.03 us
    ppermute x4, waiting for transfers between devices, depth_shift(): lax.ppermute(x, 'depth', [(i, i + by) for i in range(peers) if 0 <= i + b...  6.77 us
    pallas_call x1, Pallas kernels, hold(): pl.pallas_call(kernel, in_specs=[pl.BlockSpec(memory_space=pltpu.HBM), UN...  5.78 us
    ppermute x10, waiting for transfers between devices, col_swap(): lax.ppermute(x, 'col', [(c, c ^ bit) for c in range(lax.axis_size('col'))])  4.23 us
  transfers between devices with their start and end apart: 26, of which 16 were waited for; matrix products, arithmetic and copies ran while one was open for 0% of the time, Pallas kernels for 24%

profile of v2, /device:TPU:0, one launch (start us, length us, event | category | flops | bytes accessed | tf_op | source)
XLA Modules:
  0.0 117.6 jit_solution(4451748936670271164)
XLA Ops:
  2.5 3.0 %collective-permute-start.4 = (bf16[512,256]{1,0:T(8,128)(2,1)S(1)}, bf16[512,256]{1,0:T(8,128)(2,1)S(1)}, u32[]{:S(2)}, u32[]{:S(2)}) collective-permute-start(bf16[512,256]{1,0:T(8,128)(2,1)S(1)} %get-tuple-element.29.refs_2_.refs_1_), channel_id=1, source_target_pairs={{0,2},{1,3},{2,0},{3,1},{4,6},{5,7},{6,4},{7,5},{8,10},{9,11},{10,... | collective-permute-start | bytes 786440 | tf_op jit(solution)/shard_map/ppermute | solution.py:42
  5.6 2.6 %collective-permute-start = (bf16[512,256]{1,0:T(8,128)(2,1)S(1)}, bf16[512,256]{1,0:T(8,128)(2,1)S(1)}, u32[]{:S(2)}, u32[]{:S(2)}) collective-permute-start(bf16[512,256]{1,0:T(8,128)(2,1)S(1)} %get-tuple-element.30._.refs_1_), channel_id=1, source_target_pairs={{0,8},{8,12},{12,4},{4,0},{1,9},{9,13},{13,5},{5,1},{2,10},{10,14}... | collective-permute-start | bytes 786440 | tf_op jit(solution)/shard_map/ppermute | solution.py:38
  8.3 5.8 %hold.1.refs_0_ = bf16[1,2,2048,2048]{3,2,1,0:T(8,128)(2,1)S(1)} custom-call(bf16[1,2,2048,2048]{3,2,1,0:T(8,128)(2,1)} %w_ref.1, bf16[512,256]{1,0:T(8,128)(2,1)S(1)} %get-tuple-element.30._.refs_1_), custom_call_target="tpu_custom_call" | custom-call | bytes 335544320 | tf_op jit(solution)/shard_map/hold/pallas_call | solution.py:85
  14.5 3.4 %collective-permute-start.1 = (bf16[512,256]{1,0:T(8,128)(2,1)S(1)}, bf16[512,256]{1,0:T(8,128)(2,1)S(1)}, u32[]{:S(2)}, u32[]{:S(2)}) collective-permute-start(bf16[512,256]{1,0:T(8,128)(2,1)S(1)} %collective-permute-done.refs_5_.refs_2_), channel_id=1, source_target_pairs={{0,8},{8,12},{12,4},{4,0},{1,9},{9,13},{13,5},{5,1},{2,10},{10,14}... | collective-permute-start | bytes 786440 | tf_op jit(solution)/shard_map/ppermute | solution.py:38
  17.9 1.7 %up_first.2 = (bf16[2,2048,256]{2,1,0:T(8,128)(2,1)S(1)}, bf16[512,256]{1,0:T(8,128)(2,1)S(1)}) custom-call(bf16[1,2,2048,2048]{3,2,1,0:T(8,128)(2,1)S(1)} %hold.1.refs_0_, bf16[512,256]{1,0:T(8,128)(2,1)S(1)} %get-tuple-element.29.refs_2_.refs_1_, bf16[512,256]{1,0:T(8,128)(2,1)S(1)} %collective-permute-done.3.refs_2_, ...), custom_call_target="tpu_custom_call" | custom-call | flops 20999999488 | bytes 1048576 | tf_op jit(solution)/shard_map/up_first/pallas_call | solution.py:56
  20.2 3.7 %up_rest.2 = (f32[512,256]{1,0:T(8,128)S(1)}, f32[512,256]{1,0:T(8,128)S(1)}, f32[512,256]{1,0:T(8,128)S(1)}) custom-call(bf16[1,2,2048,2048]{3,2,1,0:T(8,128)(2,1)S(1)} %hold.1.refs_0_, bf16[2,2048,256]{2,1,0:T(8,128)(2,1)S(1)} %get-tuple-element.32.refs_1_, bf16[512,256]{1,0:T(8,128)(2,1)S(1)} %collective-permute-done.refs_5_.refs_2_), custom_call_target="tpu_custom_call" | custom-call | flops 20999999488 | bytes 1048576 | tf_op jit(solution)/shard_map/up_rest/pallas_call | solution.py:56
  24.6 3.4 %collective-permute-start.2 = (bf16[512,256]{1,0:T(8,128)(2,1)S(1)}, bf16[512,256]{1,0:T(8,128)(2,1)S(1)}, u32[]{:S(2)}, u32[]{:S(2)}) collective-permute-start(bf16[512,256]{1,0:T(8,128)(2,1)S(1)} %collective-permute-done.1.refs_3_), channel_id=1, source_target_pairs={{0,8},{8,12},{12,4},{4,0},{1,9},{9,13},{13,5},{5,1},{2,10},{10,14}... | collective-permute-start | bytes 786440 | tf_op jit(solution)/shard_map/ppermute | solution.py:38
  28.0 2.2 %collective-permute-done.9.refs_0_ = bf16[512,256]{1,0:T(8,128)(2,1)S(1)} collective-permute-done((bf16[512,256]{1,0:T(8,128)(2,1)S(1)}, bf16[512,256]{1,0:T(8,128)(2,1)S(1)}, u32[]{:S(2)}, u32[]{:S(2)}) %collective-permute-start.9) | collective-permute-done | bytes 262176 | tf_op jit(solution)/shard_map/ppermute | solution.py:38
  30.3 3.4 %collective-permute-start.10 = (bf16[512,256]{1,0:T(8,128)(2,1)S(1)}, bf16[512,256]{1,0:T(8,128)(2,1)S(1)}, u32[]{:S(2)}, u32[]{:S(2)}) collective-permute-start(bf16[512,256]{1,0:T(8,128)(2,1)S(1)} %hop.4), channel_id=1, source_target_pairs={{0,8},{8,12},{12,4},{4,0},{1,9},{9,13},{13,5},{5,1},{2,10},{10,14}... | collective-permute-start | bytes 786440 | tf_op jit(solution)/shard_map/ppermute | solution.py:38
  33.7 2.1 %collective-permute-done.2.refs_4_ = bf16[512,256]{1,0:T(8,128)(2,1)S(1)} collective-permute-done((bf16[512,256]{1,0:T(8,128)(2,1)S(1)}, bf16[512,256]{1,0:T(8,128)(2,1)S(1)}, u32[]{:S(2)}, u32[]{:S(2)}) %collective-permute-start.2) | collective-permute-done | bytes 262176 | tf_op jit(solution)/shard_map/ppermute | solution.py:38
  35.9 2.6 %down_sibling.2 = (bf16[2,2048,256]{2,1,0:T(8,128)(2,1)S(1)}, f32[2,512,256]{2,1,0:T(8,128)S(1)}) custom-call(bf16[1,2,2048,2048]{3,2,1,0:T(8,128)(2,1)S(1)} %hold.1.refs_0_, bf16[512,256]{1,0:T(8,128)(2,1)S(1)} %get-tuple-element.30._.refs_1_, bf16[512,256]{1,0:T(8,128)(2,1)S(1)} %collective-permute-done.refs_5_.refs_2_, ...), custom_call_target="tpu_custom_call" | custom-call | flops 20999999488 | bytes 1048576 | tf_op jit(solution)/shard_map/down_sibling/pallas_call | solution.py:56
  41.9 3.4 %collective-permute-start.11 = (bf16[512,256]{1,0:T(8,128)(2,1)S(1)}, bf16[512,256]{1,0:T(8,128)(2,1)S(1)}, u32[]{:S(2)}, u32[]{:S(2)}) collective-permute-start(bf16[512,256]{1,0:T(8,128)(2,1)S(1)} %hop.5), channel_id=1, source_target_pairs={{0,8},{8,12},{12,4},{4,0},{1,9},{9,13},{13,5},{5,1},{2,10},{10,14}... | collective-permute-start | bytes 786440 | tf_op jit(solution)/shard_map/ppermute | solution.py:38
  46.6 4.3 %collective-permute-done.11.refs_0_ = bf16[512,256]{1,0:T(8,128)(2,1)S(1)} collective-permute-done((bf16[512,256]{1,0:T(8,128)(2,1)S(1)}, bf16[512,256]{1,0:T(8,128)(2,1)S(1)}, u32[]{:S(2)}, u32[]{:S(2)}) %collective-permute-start.11) | collective-permute-done | bytes 262176 | tf_op jit(solution)/shard_map/ppermute | solution.py:38
  52.4 4.6 %collective-permute-start.8 = (bf16[512,256]{1,0:T(8,128)(2,1)S(1)}, bf16[512,256]{1,0:T(8,128)(2,1)S(1)}, u32[]{:S(2)}, u32[]{:S(2)}) collective-permute-start(bf16[512,256]{1,0:T(8,128)(2,1)S(1)} %get-tuple-element.36), channel_id=1, source_target_pairs={{0,16},{1,17},{2,18},{3,19},{4,20},{5,21},{6,22},{7,23},{8,24},{9,... | collective-permute-start | bytes 786440 | tf_op jit(solution)/shard_map/ppermute | solution.py:47
  57.0 3.2 %collective-permute-done.15.refs_0_ = bf16[512,256]{1,0:T(8,128)(2,1)S(1)} collective-permute-done((bf16[512,256]{1,0:T(8,128)(2,1)S(1)}, bf16[512,256]{1,0:T(8,128)(2,1)S(1)}, u32[]{:S(2)}, u32[]{:S(2)}) %collective-permute-start.15) | collective-permute-done | bytes 262176 | tf_op jit(solution)/shard_map/ppermute | solution.py:47
  60.2 1.5 %collective-permute-start.17 = (bf16[512,256]{1,0:T(8,128)(2,1)S(1)}, bf16[512,256]{1,0:T(8,128)(2,1)S(1)}, u32[]{:S(2)}, u32[]{:S(2)}) collective-permute-start(bf16[512,256]{1,0:T(8,128)(2,1)S(1)} %next_up.2.refs_1_), channel_id=1, source_target_pairs={{0,2},{1,3},{2,0},{3,1},{4,6},{5,7},{6,4},{7,5},{8,10},{9,11},{10,... | collective-permute-start | bytes 786440 | tf_op jit(solution)/shard_map/ppermute | solution.py:42
  61.9 3.4 %collective-permute-start.12 = (bf16[512,256]{1,0:T(8,128)(2,1)S(1)}, bf16[512,256]{1,0:T(8,128)(2,1)S(1)}, u32[]{:S(2)}, u32[]{:S(2)}) collective-permute-start(bf16[512,256]{1,0:T(8,128)(2,1)S(1)} %next_down.2.refs_1_), channel_id=1, source_target_pairs={{0,8},{8,12},{12,4},{4,0},{1,9},{9,13},{13,5},{5,1},{2,10},{10,14}... | collective-permute-start | bytes 786440 | tf_op jit(solution)/shard_map/ppermute | solution.py:38
  65.2 1.4 %collective-permute-done.17.refs_3_ = bf16[512,256]{1,0:T(8,128)(2,1)S(1)} collective-permute-done((bf16[512,256]{1,0:T(8,128)(2,1)S(1)}, bf16[512,256]{1,0:T(8,128)(2,1)S(1)}, u32[]{:S(2)}, u32[]{:S(2)}) %collective-permute-start.17) | collective-permute-done | bytes 262176 | tf_op jit(solution)/shard_map/ppermute | solution.py:42
  66.7 2.5 %collective-permute-done.12.refs_5_.refs_2_ = bf16[512,256]{1,0:T(8,128)(2,1)S(1)} collective-permute-done((bf16[512,256]{1,0:T(8,128)(2,1)S(1)}, bf16[512,256]{1,0:T(8,128)(2,1)S(1)}, u32[]{:S(2)}, u32[]{:S(2)}) %collective-permute-start.12) | collective-permute-done | bytes 262176 | tf_op jit(solution)/shard_map/ppermute | solution.py:38
  69.1 3.4 %collective-permute-start.13 = (bf16[512,256]{1,0:T(8,128)(2,1)S(1)}, bf16[512,256]{1,0:T(8,128)(2,1)S(1)}, u32[]{:S(2)}, u32[]{:S(2)}) collective-permute-start(bf16[512,256]{1,0:T(8,128)(2,1)S(1)} %collective-permute-done.12.refs_5_.refs_2_), channel_id=1, source_target_pairs={{0,8},{8,12},{12,4},{4,0},{1,9},{9,13},{13,5},{5,1},{2,10},{10,14}... | collective-permute-start | bytes 786440 | tf_op jit(solution)/shard_map/ppermute | solution.py:38
  72.5 1.7 %up_first.3 = (bf16[2,2048,256]{2,1,0:T(8,128)(2,1)S(1)}, bf16[512,256]{1,0:T(8,128)(2,1)S(1)}) custom-call(bf16[1,2,2048,2048]{3,2,1,0:T(8,128)(2,1)S(1)} %hold.1.refs_0_, bf16[512,256]{1,0:T(8,128)(2,1)S(1)} %next_up.2.refs_1_, bf16[512,256]{1,0:T(8,128)(2,1)S(1)} %collective-permute-done.16.refs_2_, bf16[512,256]{1,0:T(8,128)(2,1)S(1)} %collective-permute-done.17.refs_3_, ...), custom_call_target="tpu_custom_call" | custom-call | flops 20999999488 | bytes 1048576 | tf_op jit(solution)/shard_map/up_first/pallas_call | solution.py:56
  74.2 3.7 %up_rest.3 = (f32[512,256]{1,0:T(8,128)S(1)}, f32[512,256]{1,0:T(8,128)S(1)}, f32[512,256]{1,0:T(8,128)S(1)}) custom-call(bf16[1,2,2048,2048]{3,2,1,0:T(8,128)(2,1)S(1)} %hold.1.refs_0_, bf16[2,2048,256]{2,1,0:T(8,128)(2,1)S(1)} %get-tuple-element.45.refs_1_, bf16[512,256]{1,0:T(8,128)(2,1)S(1)} %collective-permute-done.12.refs_5_.refs_2_), custom_call_target="tpu_custom_call" | custom-call | flops 20999999488 | bytes 1048576 | tf_op jit(solution)/shard_map/up_rest/pallas_call | solution.py:56
  79.3 3.4 %collective-permute-start.14 = (bf16[512,256]{1,0:T(8,128)(2,1)S(1)}, bf16[512,256]{1,0:T(8,128)(2,1)S(1)}, u32[]{:S(2)}, u32[]{:S(2)}) collective-permute-start(bf16[512,256]{1,0:T(8,128)(2,1)S(1)} %collective-permute-done.13.refs_3_), channel_id=1, source_target_pairs={{0,8},{8,12},{12,4},{4,0},{1,9},{9,13},{13,5},{5,1},{2,10},{10,14}... | collective-permute-start | bytes 786440 | tf_op jit(solution)/shard_map/ppermute | solution.py:38
  82.6 2.2 %collective-permute-done.22.refs_0_ = bf16[512,256]{1,0:T(8,128)(2,1)S(1)} collective-permute-done((bf16[512,256]{1,0:T(8,128)(2,1)S(1)}, bf16[512,256]{1,0:T(8,128)(2,1)S(1)}, u32[]{:S(2)}, u32[]{:S(2)}) %collective-permute-start.22) | collective-permute-done | bytes 262176 | tf_op jit(solution)/shard_map/ppermute | solution.py:38
  84.9 3.4 %collective-permute-start.23 = (bf16[512,256]{1,0:T(8,128)(2,1)S(1)}, bf16[512,256]{1,0:T(8,128)(2,1)S(1)}, u32[]{:S(2)}, u32[]{:S(2)}) collective-permute-start(bf16[512,256]{1,0:T(8,128)(2,1)S(1)} %hop.6), channel_id=1, source_target_pairs={{0,8},{8,12},{12,4},{4,0},{1,9},{9,13},{13,5},{5,1},{2,10},{10,14}... | collective-permute-start | bytes 786440 | tf_op jit(solution)/shard_map/ppermute | solution.py:38
  88.4 1.9 %collective-permute-done.14.refs_4_ = bf16[512,256]{1,0:T(8,128)(2,1)S(1)} collective-permute-done((bf16[512,256]{1,0:T(8,128)(2,1)S(1)}, bf16[512,256]{1,0:T(8,128)(2,1)S(1)}, u32[]{:S(2)}, u32[]{:S(2)}) %collective-permute-start.14) | collective-permute-done | bytes 262176 | tf_op jit(solution)/shard_map/ppermute | solution.py:38
  90.3 2.6 %down_sibling.3 = (bf16[2,2048,256]{2,1,0:T(8,128)(2,1)S(1)}, f32[2,512,256]{2,1,0:T(8,128)S(1)}) custom-call(bf16[1,2,2048,2048]{3,2,1,0:T(8,128)(2,1)S(1)} %hold.1.refs_0_, bf16[512,256]{1,0:T(8,128)(2,1)S(1)} %next_down.2.refs_1_, bf16[512,256]{1,0:T(8,128)(2,1)S(1)} %collective-permute-done.12.refs_5_.refs_2_, ...), custom_call_target="tpu_custom_call" | custom-call | flops 20999999488 | bytes 1048576 | tf_op jit(solution)/shard_map/down_sibling/pallas_call | solution.py:56
  95.7 1.4 %collective-permute-start.20 = (bf16[512,256]{1,0:T(8,128)(2,1)S(1)}, bf16[512,256]{1,0:T(8,128)(2,1)S(1)}, u32[]{:S(2)}, u32[]{:S(2)}) collective-permute-start(bf16[512,256]{1,0:T(8,128)(2,1)S(1)} %far_sum.3.refs_3_.refs_2_), channel_id=1, source_target_pairs={{0,2},{1,3},{2,0},{3,1},{4,6},{5,7},{6,4},{7,5},{8,10},{9,11},{10,... | collective-permute-start | bytes 786440 | tf_op jit(solution)/shard_map/ppermute | solution.py:42
  97.2 3.4 %collective-permute-start.24 = (bf16[512,256]{1,0:T(8,128)(2,1)S(1)}, bf16[512,256]{1,0:T(8,128)(2,1)S(1)}, u32[]{:S(2)}, u32[]{:S(2)}) collective-permute-start(bf16[512,256]{1,0:T(8,128)(2,1)S(1)} %hop.7), channel_id=1, source_target_pairs={{0,8},{8,12},{12,4},{4,0},{1,9},{9,13},{13,5},{5,1},{2,10},{10,14}... | collective-permute-start | bytes 786440 | tf_op jit(solution)/shard_map/ppermute | solution.py:38
  101.8 4.3 %collective-permute-done.24.refs_0_ = bf16[512,256]{1,0:T(8,128)(2,1)S(1)} collective-permute-done((bf16[512,256]{1,0:T(8,128)(2,1)S(1)}, bf16[512,256]{1,0:T(8,128)(2,1)S(1)}, u32[]{:S(2)}, u32[]{:S(2)}) %collective-permute-start.24) | collective-permute-done | bytes 262176 | tf_op jit(solution)/shard_map/ppermute | solution.py:38
  107.6 4.6 %collective-permute-start.21 = (bf16[512,256]{1,0:T(8,128)(2,1)S(1)}, bf16[512,256]{1,0:T(8,128)(2,1)S(1)}, u32[]{:S(2)}, u32[]{:S(2)}) collective-permute-start(bf16[512,256]{1,0:T(8,128)(2,1)S(1)} %get-tuple-element.49), channel_id=1, source_target_pairs={{0,16},{1,17},{2,18},{3,19},{4,20},{5,21},{6,22},{7,23},{8,24},{9,... | collective-permute-start | bytes 786440 | tf_op jit(solution)/shard_map/ppermute | solution.py:47
  112.2 3.2 %collective-permute-done.25.refs_0_ = bf16[512,256]{1,0:T(8,128)(2,1)S(1)} collective-permute-done((bf16[512,256]{1,0:T(8,128)(2,1)S(1)}, bf16[512,256]{1,0:T(8,128)(2,1)S(1)}, u32[]{:S(2)}, u32[]{:S(2)}) %collective-permute-start.25) | collective-permute-done | bytes 262176 | tf_op jit(solution)/shard_map/ppermute | solution.py:47
  (59 shorter events, 19.3 us)
Async XLA Ops:
  0.6 1.0 copy-start
  1.7 0.7 copy-start.4
  2.4 3.1 %copy-start.1 = (f32[1,512,256]{2,1,0:T(8,128)S(1)}, f32[1,512,256]{2,1,0:T(8,128)}, u32[]{:S(2)}) copy-start(f32[1,512,256]{2,1,0:T(8,128)} %refs_0_.3) | copy-start | bytes 1572868
  2.4 3.1 %copy-start.5 = (f32[1,512]{1,0:T(1,128)S(1)}, f32[1,512]{1,0:T(1,128)}, u32[]{:S(2)}) copy-start(f32[1,512]{1,0:T(1,128)} %refs_1_.5) | copy-start | bytes 6148
  2.5 11.6 %collective-permute-start.4 = (bf16[512,256]{1,0:T(8,128)(2,1)S(1)}, bf16[512,256]{1,0:T(8,128)(2,1)S(1)}, u32[]{:S(2)}, u32[]{:S(2)}) collective-permute-start(bf16[512,256]{1,0:T(8,128)(2,1)S(1)} %get-tuple-element.29.refs_2_.refs_1_), channel_id=1, source_target_pairs={{0,2},{1,3},{2,0},{3,1},{4,6},{5,7},{6,4},{7,5},{8,10},{9,11},{10,... | collective-permute-start | bytes 786440 | tf_op jit(solution)/shard_map/ppermute | solution.py:42
  5.5 12.4 %collective-permute-start.3 = (bf16[512,256]{1,0:T(8,128)(2,1)S(1)}, bf16[512,256]{1,0:T(8,128)(2,1)S(1)}, u32[]{:S(2)}, u32[]{:S(2)}) collective-permute-start(bf16[512,256]{1,0:T(8,128)(2,1)S(1)} %get-tuple-element.29.refs_2_.refs_1_), channel_id=1, source_target_pairs={{0,1},{1,0},{2,3},{3,2},{4,5},{5,4},{6,7},{7,6},{8,9},{9,8},{10,11... | collective-permute-start | bytes 786440 | tf_op jit(solution)/shard_map/ppermute | solution.py:42
  5.6 8.9 %collective-permute-start = (bf16[512,256]{1,0:T(8,128)(2,1)S(1)}, bf16[512,256]{1,0:T(8,128)(2,1)S(1)}, u32[]{:S(2)}, u32[]{:S(2)}) collective-permute-start(bf16[512,256]{1,0:T(8,128)(2,1)S(1)} %get-tuple-element.30._.refs_1_), channel_id=1, source_target_pairs={{0,8},{8,12},{12,4},{4,0},{1,9},{9,13},{13,5},{5,1},{2,10},{10,14}... | collective-permute-start | bytes 786440 | tf_op jit(solution)/shard_map/ppermute | solution.py:38
  14.1 3.8 %collective-permute-start.5 = (bf16[512,256]{1,0:T(8,128)(2,1)S(1)}, bf16[512,256]{1,0:T(8,128)(2,1)S(1)}, u32[]{:S(2)}, u32[]{:S(2)}) collective-permute-start(bf16[512,256]{1,0:T(8,128)(2,1)S(1)} %collective-permute-done.4.refs_3_), channel_id=1, source_target_pairs={{0,1},{1,0},{2,3},{3,2},{4,5},{5,4},{6,7},{7,6},{8,9},{9,8},{10,11... | collective-permute-start | bytes 786440 | tf_op jit(solution)/shard_map/ppermute | solution.py:42
  14.5 10.1 %collective-permute-start.1 = (bf16[512,256]{1,0:T(8,128)(2,1)S(1)}, bf16[512,256]{1,0:T(8,128)(2,1)S(1)}, u32[]{:S(2)}, u32[]{:S(2)}) collective-permute-start(bf16[512,256]{1,0:T(8,128)(2,1)S(1)} %collective-permute-done.refs_5_.refs_2_), channel_id=1, source_target_pairs={{0,8},{8,12},{12,4},{4,0},{1,9},{9,13},{13,5},{5,1},{2,10},{10,14}... | collective-permute-start | bytes 786440 | tf_op jit(solution)/shard_map/ppermute | solution.py:38
  19.6 10.7 %collective-permute-start.9 = (bf16[512,256]{1,0:T(8,128)(2,1)S(1)}, bf16[512,256]{1,0:T(8,128)(2,1)S(1)}, u32[]{:S(2)}, u32[]{:S(2)}) collective-permute-start(bf16[512,256]{1,0:T(8,128)(2,1)S(1)} %get-tuple-element.38), channel_id=1, source_target_pairs={{0,8},{8,12},{12,4},{4,0},{1,9},{9,13},{13,5},{5,1},{2,10},{10,14}... | collective-permute-start | bytes 786440 | tf_op jit(solution)/shard_map/ppermute | solution.py:38
  24.6 11.2 %collective-permute-start.2 = (bf16[512,256]{1,0:T(8,128)(2,1)S(1)}, bf16[512,256]{1,0:T(8,128)(2,1)S(1)}, u32[]{:S(2)}, u32[]{:S(2)}) collective-permute-start(bf16[512,256]{1,0:T(8,128)(2,1)S(1)} %collective-permute-done.1.refs_3_), channel_id=1, source_target_pairs={{0,8},{8,12},{12,4},{4,0},{1,9},{9,13},{13,5},{5,1},{2,10},{10,14}... | collective-permute-start | bytes 786440 | tf_op jit(solution)/shard_map/ppermute | solution.py:38
  30.3 11.6 %collective-permute-start.10 = (bf16[512,256]{1,0:T(8,128)(2,1)S(1)}, bf16[512,256]{1,0:T(8,128)(2,1)S(1)}, u32[]{:S(2)}, u32[]{:S(2)}) collective-permute-start(bf16[512,256]{1,0:T(8,128)(2,1)S(1)} %hop.4), channel_id=1, source_target_pairs={{0,8},{8,12},{12,4},{4,0},{1,9},{9,13},{13,5},{5,1},{2,10},{10,14}... | collective-permute-start | bytes 786440 | tf_op jit(solution)/shard_map/ppermute | solution.py:38
  38.5 2.7 %collective-permute-start.6 = (f32[2,512,256]{2,1,0:T(8,128)S(1)}, f32[2,512,256]{2,1,0:T(8,128)S(1)}, u32[]{:S(2)}, u32[]{:S(2)}) collective-permute-start(f32[2,512,256]{2,1,0:T(8,128)S(1)} %get-tuple-element.35), channel_id=1, source_target_pairs={{0,1},{1,0},{2,3},{3,2},{4,5},{5,4},{6,7},{7,6},{8,9},{9,8},{10,11... | collective-permute-start | bytes 3145736 | tf_op jit(solution)/shard_map/ppermute | solution.py:42
  41.2 11.1 %collective-permute-start.7 = (bf16[512,256]{1,0:T(8,128)(2,1)S(1)}, bf16[512,256]{1,0:T(8,128)(2,1)S(1)}, u32[]{:S(2)}, u32[]{:S(2)}) collective-permute-start(bf16[512,256]{1,0:T(8,128)(2,1)S(1)} %far_sum.2.refs_3_.refs_2_), channel_id=1, source_target_pairs={{0,2},{1,3},{2,0},{3,1},{4,6},{5,7},{6,4},{7,5},{8,10},{9,11},{10,... | collective-permute-start | bytes 786440 | tf_op jit(solution)/shard_map/ppermute | solution.py:42
  41.9 9.0 %collective-permute-start.11 = (bf16[512,256]{1,0:T(8,128)(2,1)S(1)}, bf16[512,256]{1,0:T(8,128)(2,1)S(1)}, u32[]{:S(2)}, u32[]{:S(2)}) collective-permute-start(bf16[512,256]{1,0:T(8,128)(2,1)S(1)} %hop.5), channel_id=1, source_target_pairs={{0,8},{8,12},{12,4},{4,0},{1,9},{9,13},{13,5},{5,1},{2,10},{10,14}... | collective-permute-start | bytes 786440 | tf_op jit(solution)/shard_map/ppermute | solution.py:38
  51.0 9.1 %collective-permute-start.15 = (bf16[512,256]{1,0:T(8,128)(2,1)S(1)}, bf16[512,256]{1,0:T(8,128)(2,1)S(1)}, u32[]{:S(2)}, u32[]{:S(2)}) collective-permute-start(bf16[512,256]{1,0:T(8,128)(2,1)S(1)} %get-tuple-element.42), channel_id=1, source_target_pairs={{16,0},{17,1},{18,2},{19,3},{20,4},{21,5},{22,6},{23,7},{24,8},{25... | collective-permute-start | bytes 786440 | tf_op jit(solution)/shard_map/ppermute | solution.py:47
  52.4 9.3 %collective-permute-start.8 = (bf16[512,256]{1,0:T(8,128)(2,1)S(1)}, bf16[512,256]{1,0:T(8,128)(2,1)S(1)}, u32[]{:S(2)}, u32[]{:S(2)}) collective-permute-start(bf16[512,256]{1,0:T(8,128)(2,1)S(1)} %get-tuple-element.36), channel_id=1, source_target_pairs={{0,16},{1,17},{2,18},{3,19},{4,20},{5,21},{6,22},{7,23},{8,24},{9,... | collective-permute-start | bytes 786440 | tf_op jit(solution)/shard_map/ppermute | solution.py:47
  60.2 1.6 %copy-start.2 = (f32[512,256]{1,0:T(8,128)S(1)}, f32[512,256]{1,0:T(8,128)}, u32[]{:S(2)}) copy-start(f32[512,256]{1,0:T(8,128)} %refs_1_.7) | copy-start | bytes 1572868
  60.2 6.4 %collective-permute-start.17 = (bf16[512,256]{1,0:T(8,128)(2,1)S(1)}, bf16[512,256]{1,0:T(8,128)(2,1)S(1)}, u32[]{:S(2)}, u32[]{:S(2)}) collective-permute-start(bf16[512,256]{1,0:T(8,128)(2,1)S(1)} %next_up.2.refs_1_), channel_id=1, source_target_pairs={{0,2},{1,3},{2,0},{3,1},{4,6},{5,7},{6,4},{7,5},{8,10},{9,11},{10,... | collective-permute-start | bytes 786440 | tf_op jit(solution)/shard_map/ppermute | solution.py:42
  61.9 7.3 %collective-permute-start.12 = (bf16[512,256]{1,0:T(8,128)(2,1)S(1)}, bf16[512,256]{1,0:T(8,128)(2,1)S(1)}, u32[]{:S(2)}, u32[]{:S(2)}) collective-permute-start(bf16[512,256]{1,0:T(8,128)(2,1)S(1)} %next_down.2.refs_1_), channel_id=1, source_target_pairs={{0,8},{8,12},{12,4},{4,0},{1,9},{9,13},{13,5},{5,1},{2,10},{10,14}... | collective-permute-start | bytes 786440 | tf_op jit(solution)/shard_map/ppermute | solution.py:38
  65.2 7.3 %collective-permute-start.16 = (bf16[512,256]{1,0:T(8,128)(2,1)S(1)}, bf16[512,256]{1,0:T(8,128)(2,1)S(1)}, u32[]{:S(2)}, u32[]{:S(2)}) collective-permute-start(bf16[512,256]{1,0:T(8,128)(2,1)S(1)} %next_up.2.refs_1_), channel_id=1, source_target_pairs={{0,1},{1,0},{2,3},{3,2},{4,5},{5,4},{6,7},{7,6},{8,9},{9,8},{10,11... | collective-permute-start | bytes 786440 | tf_op jit(solution)/shard_map/ppermute | solution.py:42
  66.7 5.8 %collective-permute-start.18 = (bf16[512,256]{1,0:T(8,128)(2,1)S(1)}, bf16[512,256]{1,0:T(8,128)(2,1)S(1)}, u32[]{:S(2)}, u32[]{:S(2)}) collective-permute-start(bf16[512,256]{1,0:T(8,128)(2,1)S(1)} %collective-permute-done.17.refs_3_), channel_id=1, source_target_pairs={{0,1},{1,0},{2,3},{3,2},{4,5},{5,4},{6,7},{7,6},{8,9},{9,8},{10,11... | collective-permute-start | bytes 786440 | tf_op jit(solution)/shard_map/ppermute | solution.py:42
  69.1 10.1 %collective-permute-start.13 = (bf16[512,256]{1,0:T(8,128)(2,1)S(1)}, bf16[512,256]{1,0:T(8,128)(2,1)S(1)}, u32[]{:S(2)}, u32[]{:S(2)}) collective-permute-start(bf16[512,256]{1,0:T(8,128)(2,1)S(1)} %collective-permute-done.12.refs_5_.refs_2_), channel_id=1, source_target_pairs={{0,8},{8,12},{12,4},{4,0},{1,9},{9,13},{13,5},{5,1},{2,10},{10,14}... | collective-permute-start | bytes 786440 | tf_op jit(solution)/shard_map/ppermute | solution.py:38
  74.2 10.7 %collective-permute-start.22 = (bf16[512,256]{1,0:T(8,128)(2,1)S(1)}, bf16[512,256]{1,0:T(8,128)(2,1)S(1)}, u32[]{:S(2)}, u32[]{:S(2)}) collective-permute-start(bf16[512,256]{1,0:T(8,128)(2,1)S(1)} %get-tuple-element.50), channel_id=1, source_target_pairs={{0,8},{8,12},{12,4},{4,0},{1,9},{9,13},{13,5},{5,1},{2,10},{10,14}... | collective-permute-start | bytes 786440 | tf_op jit(solution)/shard_map/ppermute | solution.py:38
  79.3 11.0 %collective-permute-start.14 = (bf16[512,256]{1,0:T(8,128)(2,1)S(1)}, bf16[512,256]{1,0:T(8,128)(2,1)S(1)}, u32[]{:S(2)}, u32[]{:S(2)}) collective-permute-start(bf16[512,256]{1,0:T(8,128)(2,1)S(1)} %collective-permute-done.13.refs_3_), channel_id=1, source_target_pairs={{0,8},{8,12},{12,4},{4,0},{1,9},{9,13},{13,5},{5,1},{2,10},{10,14}... | collective-permute-start | bytes 786440 | tf_op jit(solution)/shard_map/ppermute | solution.py:38
  84.9 12.2 %collective-permute-start.23 = (bf16[512,256]{1,0:T(8,128)(2,1)S(1)}, bf16[512,256]{1,0:T(8,128)(2,1)S(1)}, u32[]{:S(2)}, u32[]{:S(2)}) collective-permute-start(bf16[512,256]{1,0:T(8,128)(2,1)S(1)} %hop.6), channel_id=1, source_target_pairs={{0,8},{8,12},{12,4},{4,0},{1,9},{9,13},{13,5},{5,1},{2,10},{10,14}... | collective-permute-start | bytes 786440 | tf_op jit(solution)/shard_map/ppermute | solution.py:38
  92.9 2.7 %collective-permute-start.19 = (f32[2,512,256]{2,1,0:T(8,128)S(1)}, f32[2,512,256]{2,1,0:T(8,128)S(1)}, u32[]{:S(2)}, u32[]{:S(2)}) collective-permute-start(f32[2,512,256]{2,1,0:T(8,128)S(1)} %get-tuple-element.48), channel_id=1, source_target_pairs={{0,1},{1,0},{2,3},{3,2},{4,5},{5,4},{6,7},{7,6},{8,9},{9,8},{10,11... | collective-permute-start | bytes 3145736 | tf_op jit(solution)/shard_map/ppermute | solution.py:42
  95.7 11.9 %collective-permute-start.20 = (bf16[512,256]{1,0:T(8,128)(2,1)S(1)}, bf16[512,256]{1,0:T(8,128)(2,1)S(1)}, u32[]{:S(2)}, u32[]{:S(2)}) collective-permute-start(bf16[512,256]{1,0:T(8,128)(2,1)S(1)} %far_sum.3.refs_3_.refs_2_), channel_id=1, source_target_pairs={{0,2},{1,3},{2,0},{3,1},{4,6},{5,7},{6,4},{7,5},{8,10},{9,11},{10,... | collective-permute-start | bytes 786440 | tf_op jit(solution)/shard_map/ppermute | solution.py:42
  97.2 9.0 %collective-permute-start.24 = (bf16[512,256]{1,0:T(8,128)(2,1)S(1)}, bf16[512,256]{1,0:T(8,128)(2,1)S(1)}, u32[]{:S(2)}, u32[]{:S(2)}) collective-permute-start(bf16[512,256]{1,0:T(8,128)(2,1)S(1)} %hop.7), channel_id=1, source_target_pairs={{0,8},{8,12},{12,4},{4,0},{1,9},{9,13},{13,5},{5,1},{2,10},{10,14}... | collective-permute-start | bytes 786440 | tf_op jit(solution)/shard_map/ppermute | solution.py:38
  106.3 9.1 %collective-permute-start.25 = (bf16[512,256]{1,0:T(8,128)(2,1)S(1)}, bf16[512,256]{1,0:T(8,128)(2,1)S(1)}, u32[]{:S(2)}, u32[]{:S(2)}) collective-permute-start(bf16[512,256]{1,0:T(8,128)(2,1)S(1)} %get-tuple-element.54), channel_id=1, source_target_pairs={{16,0},{17,1},{18,2},{19,3},{20,4},{21,5},{22,6},{23,7},{24,8},{25... | collective-permute-start | bytes 786440 | tf_op jit(solution)/shard_map/ppermute | solution.py:47
  107.6 9.0 %collective-permute-start.21 = (bf16[512,256]{1,0:T(8,128)(2,1)S(1)}, bf16[512,256]{1,0:T(8,128)(2,1)S(1)}, u32[]{:S(2)}, u32[]{:S(2)}) collective-permute-start(bf16[512,256]{1,0:T(8,128)(2,1)S(1)} %get-tuple-element.49), channel_id=1, source_target_pairs={{0,16},{1,17},{2,18},{3,19},{4,20},{5,21},{6,22},{7,23},{8,24},{9,... | collective-permute-start | bytes 786440 | tf_op jit(solution)/shard_map/ppermute | solution.py:47
  115.4 1.3 %copy-start.3 = (f32[512,256]{1,0:T(8,128)S(1)}, f32[512,256]{1,0:T(8,128)}, u32[]{:S(2)}) copy-start(f32[512,256]{1,0:T(8,128)} %refs_1_.7) | copy-start | bytes 1572868

commit v3 on v2

--- a/solution.py
+++ b/solution.py
@@ -14,6 +14,7 @@
 UNREAD = pl.BlockSpec(memory_space=pl.ANY)
 LANES = 128
 DECLARED = 21 * 10**9
+CHEAP = {"up_first": 0, "split": 0}
 CONTRACT_ROWS = (((0,), (0,)), ((), ()))
 
 
@@ -31,6 +32,16 @@
 def ring_block(behind, size):
     place = ring_place(lax.axis_index("row"), size)
     return ring_device(lax.rem(place - behind + size, size), size)
+
+
+def row_swap(x, bit):
+    return lax.ppermute(x, "row", [(r, r ^ bit) for r in range(lax.axis_size("row"))])
+
+
+def row_block(order, size):
+    if size == 4:
+        return lax.axis_index("row") ^ (0, 3, 2, 1)[order % size]
+    return ring_block(order % size, size)
 
 
 def ring_hop(x, size):
@@ -59,7 +70,7 @@
         out_specs=[WHOLE] * len(outs),
         out_shape=outs,
         name=name,
-        cost_estimate=pl.CostEstimate(flops=DECLARED, bytes_accessed=2**20, transcendentals=0),
+        cost_estimate=pl.CostEstimate(flops=CHEAP.get(name, DECLARED), bytes_accessed=1 if name in CHEAP else 2**20, transcendentals=0),
         compiler_params=pltpu.CompilerParams(vmem_limit_bytes=12 * 2**20),
     )(*args, *after)
 
@@ -122,6 +133,12 @@
     )
 
 
+def split_kernel(whole_ref, *part_refs):
+    half = whole_ref.shape[0] // 2
+    for k, ref in enumerate(part_refs):
+        ref[...] = whole_ref[k * half : (k + 1) * half, :]
+
+
 def up_dot(w_ref, pair_ref, columns):
     return lax.dot_general(
         w_ref[0, 0, :, columns], pair_ref[0], CONTRACT_ROWS, preferred_element_type=F32
@@ -131,7 +148,7 @@
 def down_sibling_kernel(size, strip, sources, w_ref, *refs):
     blocks, pair_ref, out_ref = refs[:size], refs[size], refs[size + 1]
     for s in range(size):
-        place_block(pair_ref, blocks[s], rows_at(ring_block(s, size), strip), sources)
+        place_block(pair_ref, blocks[s], rows_at(row_block(s, size), strip), sources)
     me = lax.axis_index("col")
     for k in range(2):
         out_ref[k] = down_dot(w_ref, pair_ref, rows_at(me ^ (1 + 2 * k), strip))
@@ -150,44 +167,77 @@
 
 
 def up_first_kernel(size, strip, sources, w_ref, *refs):
-    blocks, pair_ref, out_ref = refs[:4], refs[4], refs[5]
+    *blocks, pair_ref, out_ref = refs
     me = lax.axis_index("col")
+    for s in range(2):
+        place_block(pair_ref, blocks[s], rows_at(me ^ s, strip), sources)
     for s in range(4):
-        place_block(pair_ref, blocks[s], rows_at(me ^ s, strip), sources)
-    out_ref[...] = up_dot(w_ref, pair_ref, rows_at(ring_block(1, size), strip)).astype(BF16)
+        part = rows_at(2 * (me ^ (2 + s // 2)) + s % 2, strip // 2)
+        place_block(pair_ref, blocks[2 + s], part, sources)
+    out_ref[...] = up_dot(w_ref, pair_ref, rows_at(row_block(1, size), strip)).astype(BF16)
 
 
 def up_rest_kernel(size, strip, w_ref, pair_ref, *out_refs):
-    for s in range(2, size + 1):
-        out_refs[s - 2][...] = up_dot(w_ref, pair_ref, rows_at(ring_block(s % size, size), strip))
+    for s, ref in zip(range(2, size + 1), out_refs):
+        ref[...] = up_dot(w_ref, pair_ref, rows_at(row_block(s, size), strip)).astype(ref.dtype)
 
 
 def hop_kernel(arrived_ref, own_ref, out_ref):
     out_ref[...] = (arrived_ref[...].astype(F32) + own_ref[...]).astype(BF16)
 
 
-def both_kernel(arrived_ref, own_ref, full_ref, low_ref):
-    total = arrived_ref[...].astype(F32) + own_ref[...]
+def both_kernel(*refs):
+    *arrived, own_ref, full_ref, low_ref = refs
+    total = own_ref[...]
+    for ref in arrived:
+        total = total + ref[...].astype(F32)
     full_ref[...] = total
     low_ref[...] = total.astype(BF16)
 
 
-def next_up_kernel(below_ref, refl_ref, trans_ref, out_ref):
-    total = below_ref[...].astype(F32) + scaled(refl_ref, trans_ref[...])
-    out_ref[...] = total.astype(out_ref.dtype).reshape(out_ref.shape)
-
-
-def next_down_kernel(above_ref, source_ref, refl_ref, back_ref, out_ref):
-    reflected = scaled(refl_ref, back_ref[...])
+def sums_kernel(count, *refs):
+    back_full, trans_full, low_ref = refs[-3:]
+    own_up, from_far, own_down = refs[count : count + 3]
+    back = own_up[...]
+    for ref in refs[:count]:
+        back = back + ref[...].astype(F32)
+    trans = own_down[...] + from_far[...].astype(F32)
+    back_full[...] = back
+    trans_full[...] = trans
     at_surface = lax.axis_index("depth") == 0
 
     @pl.when(at_surface)
     def _():
-        out_ref[...] = (source_ref[...] + reflected).astype(out_ref.dtype).reshape(out_ref.shape)
+        low_ref[...] = trans.astype(BF16)
 
     @pl.when(jnp.logical_not(at_surface))
     def _():
-        out_ref[...] = (above_ref[...].astype(F32) + reflected).astype(out_ref.dtype).reshape(out_ref.shape)
+        low_ref[...] = back.astype(BF16)
+
+
+def next_kernel(above_ref, below_ref, source_ref, factor_down, factor_up, back_ref, trans_ref, down_ref, up_ref):
+    place, last = lax.axis_index("depth"), lax.axis_size("depth") - 1
+    down = scaled(factor_down, back_ref[...])
+    up = scaled(factor_up, trans_ref[...])
+
+    def put(ref, value):
+        ref[...] = value.astype(ref.dtype).reshape(ref.shape)
+
+    @pl.when(place == 0)
+    def _():
+        put(down_ref, source_ref[...] + down)
+
+    @pl.when(place > 0)
+    def _():
+        put(down_ref, above_ref[...].astype(F32) + down)
+
+    @pl.when(place == last)
+    def _():
+        put(up_ref, up)
+
+    @pl.when(place < last)
+    def _():
+        put(up_ref, below_ref[...].astype(F32) + up)
 
 
 def body(prop, source, down_init, up_init, refl_down, refl_up):
@@ -210,45 +260,67 @@
         far = col_swap(up_low, 2)
         if sweep == 0:
             far = behind(far, w)
-        blocks_up = [up_low, near, far, col_swap(far, 1)]
-        blocks_down = [down_low, ring_hop(down_low, size)]
+        parts = call(split_kernel, [array((strip // 2, width), BF16)] * 2, "split", [far])
+        blocks_up = [up_low, near, *parts, col_swap(parts[0], 1), col_swap(parts[1], 1)]
+        if size == 4:
+            beside, across = row_swap(down_low, 1), row_swap(down_low, 2)
+            begun, ready = [], [across, beside]
+        else:
+            blocks_down = [down_low]
+            for s in range(size - 1):
+                blocks_down.append(ring_hop(blocks_down[-1], size))
+            begun = ready = blocks_down[1:2]
         pair_up, travelling = call(
             functools.partial(up_first_kernel, size, strip, sources),
-            [array((2, tall, width), BF16), low], "up_first", [w, *blocks_up], [blocks_down[1]],
-        )
-        for s in range(1, size - 1):
-            blocks_down.append(ring_hop(blocks_down[-1], size))
+            [array((2, tall, width), BF16), low], "up_first", [w, *blocks_up], begun,
+        )
+        if size == 4:
+            blocks_down = [down_low, row_swap(behind(across, travelling), 1), across, beside]
+        kinds = [full, low, full] if size == 4 else [full] * (size - 1)
         own_up = call(
-            functools.partial(up_rest_kernel, size, strip),
-            [full] * (size - 1), "up_rest", [w, pair_up], [blocks_down[1]],
-        )
+            functools.partial(up_rest_kernel, size, strip), kinds, "up_rest", [w, pair_up], ready,
+        )
+        if size == 4:
+            (passed,) = call(
+                hop_kernel, [low], "hop", [row_swap(travelling, 1), own_up[0]], [own_up[1]]
+            )
+            arrived = [row_swap(behind(own_up[1], passed), 1), row_swap(passed, 2)]
+            before_down = [passed]
+        else:
+            for s in range(size - 2):
+                (travelling,) = call(
+                    hop_kernel, [low], "hop", [ring_hop(travelling, size), own_up[s]], [own_up[-1]]
+                )
+            arrived = [ring_hop(travelling, size)]
+            before_down = [own_up[0]]
         pair_down, to_sibling = call(
             functools.partial(down_sibling_kernel, size, strip, sources),
             [array((2, wide, width), BF16), array((2, strip, width), F32)],
-            "down_sibling", [w, *blocks_down], [own_up[0]],
+            "down_sibling", [w, *blocks_down], before_down,
         )
         from_sibling = col_swap(to_sibling, 1)
         (own_far,) = call(functools.partial(down_far_kernel, strip), [full], "down_far", [w, pair_down])
         (to_far,) = call(far_sum_kernel, [low], "far_sum", [own_far, from_sibling])
         from_far = col_swap(to_far, 2)
         (own_down,) = call(
-            functools.partial(down_own_kernel, strip), [full], "down_own",             [w, pair_down, from_sibling], [to_far],
-        )
-        for s in range(size - 2):
-            arrived = ring_hop(travelling, size)
-            (travelling,) = call(
-                hop_kernel, [low], "hop", [arrived, own_up[s]], [to_far] if s == size - 3 else [own_up[-1]]
+            functools.partial(down_own_kernel, strip), [full], "down_own",
+            [w, pair_down, from_sibling], [to_far],
+        )
+        if lax.axis_size("depth") == 2:
+            back, trans, passed_on = call(
+                functools.partial(sums_kernel, len(arrived)), [full, full, low], "sums",
+                [*arrived, own_up[-1], from_far, own_down],
             )
-        back, back_low = call(
-            both_kernel, [full, low], "back", [ring_hop(travelling, size), own_up[size - 2]], [own_down]
-        )
-        from_below = depth_shift(back_low, -1)
-        trans, trans_low = call(both_kernel, [full, low], "trans", [from_far, own_down])
-        from_above = depth_shift(trans_low, 1)
+            from_above = from_below = lax.ppermute(passed_on, "depth", [(0, 1), (1, 0)])
+        else:
+            back, back_low = call(both_kernel, [full, low], "back", [*arrived, own_up[-1]], [own_down])
+            from_below = depth_shift(back_low, -1)
+            trans, trans_low = call(both_kernel, [full, low], "trans", [from_far, own_down])
+            from_above = depth_shift(trans_low, 1)
         kind = array((1, strip, width), F32) if last else low
-        (up_low,) = call(next_up_kernel, [kind], "next_up", [from_below, refl_below, trans])
-        (down_low,) = call(
-            next_down_kernel, [kind], "next_down", [from_above, source, refl_above, back]
+        down_low, up_low = call(
+            next_kernel, [kind, kind], "next",
+            [from_above, from_below, source, refl_above, refl_below, back, trans],
         )
     return (down_low, up_low)
 

time: 118 us -> 110 us (0.932)
  starting transfers between devices: 52.7 us -> 20.8 us
  waiting for transfers between devices: 32.9 us -> 57.7 us
    ppermute x16 -> x14, starting transfers between devices: 45.7 us -> 13.7 us  [the longest x12 10.5 us: row_swap(): lax.ppermute(x, 'row', [(r, r ^ bit) for r in range(lax.axis_size('row'))])]
    ppermute x16 -> x14, waiting for transfers between devices: 28.6 us -> 46.4 us  [the longest x12 34.3 us: row_swap(): lax.ppermute(x, 'row', [(r, r ^ bit) for r in range(lax.axis_size('row'))])]
    ppermute x10 -> x12, waiting for transfers between devices: 4.23 us -> 11.4 us  [col_swap(): lax.ppermute(x, 'col', [(c, c ^ bit) for c in range(lax.axis_size('col'))])]
    pallas_call x26 -> x22, Pallas kernels: 23.6 us -> 22.9 us  [call(): pl.pallas_call(ordered, in_specs=[WHOLE] * count + [UNREAD] * len(after),...]
    ppermute x10 -> x12, starting transfers between devices: 7.03 us -> 7.09 us  [col_swap(): lax.ppermute(x, 'col', [(c, c ^ bit) for c in range(lax.axis_size('col'))])]
  transfers between devices with their start and end apart: 26 -> 26, of which waited for: 16 -> 19; matrix products, arithmetic and copies ran while one was open for 0% -> 0% of each run, Pallas kernels for 24% -> 24%
where the time goes in v3:
time: 110 us
  waiting for transfers between devices  57.7 us (52%)
  Pallas kernels  28.6 us (26%)
  starting transfers between devices  20.8 us (19%)
  local copies, waits for them, and re-layouts  1.73 us (2%)
    ppermute x12, waiting for transfers between devices, row_swap(): lax.ppermute(x, 'row', [(r, r ^ bit) for r in range(lax.axis_size('row'))])  34.3 us
    pallas_call x22, Pallas kernels, call(): pl.pallas_call(ordered, in_specs=[WHOLE] * count + [UNREAD] * len(after),...  22.9 us
    ppermute x2, waiting for transfers between devices, body(): from_above = from_below = lax.ppermute(passed_on, 'depth', [(0, 1), (1, 0)])  12 us
    ppermute x12, waiting for transfers between devices, col_swap(): lax.ppermute(x, 'col', [(c, c ^ bit) for c in range(lax.axis_size('col'))])  11.4 us
    ppermute x12, starting transfers between devices, row_swap(): lax.ppermute(x, 'row', [(r, r ^ bit) for r in range(lax.axis_size('row'))])  10.5 us
    ppermute x12, starting transfers between devices, col_swap(): lax.ppermute(x, 'col', [(c, c ^ bit) for c in range(lax.axis_size('col'))])  7.09 us
    pallas_call x1, Pallas kernels, hold(): pl.pallas_call(kernel, in_specs=[pl.BlockSpec(memory_space=pltpu.HBM), UN...  5.78 us
    ppermute x2, starting transfers between devices, body(): from_above = from_below = lax.ppermute(passed_on, 'depth', [(0, 1), (1, 0)])  3.14 us
  transfers between devices with their start and end apart: 26, of which 19 were waited for; matrix products, arithmetic and copies ran while one was open for 0% of the time, Pallas kernels for 24%

profile of v3, /device:TPU:0, one launch (start us, length us, event | category | flops | bytes accessed | tf_op | source)
XLA Modules:
  0.0 109.7 jit_solution(12250865177935937142)
XLA Ops:
  2.5 3.0 %collective-permute-start.1 = (bf16[512,256]{1,0:T(8,128)(2,1)S(1)}, bf16[512,256]{1,0:T(8,128)(2,1)S(1)}, u32[]{:S(2)}, u32[]{:S(2)}) collective-permute-start(bf16[512,256]{1,0:T(8,128)(2,1)S(1)} %get-tuple-element.37.refs_2_.refs_1_), channel_id=1, source_target_pairs={{0,2},{1,3},{2,0},{3,1},{4,6},{5,7},{6,4},{7,5},{8,10},{9,11},{10,... | collective-permute-start | bytes 786440 | tf_op jit(solution)/shard_map/ppermute | solution.py:53
  5.6 2.7 %collective-permute-start.4 = (bf16[512,256]{1,0:T(8,128)(2,1)S(1)}, bf16[512,256]{1,0:T(8,128)(2,1)S(1)}, u32[]{:S(2)}, u32[]{:S(2)}) collective-permute-start(bf16[512,256]{1,0:T(8,128)(2,1)S(1)} %get-tuple-element.38._.refs_1_), channel_id=1, source_target_pairs={{0,8},{4,12},{8,0},{12,4},{1,9},{5,13},{9,1},{13,5},{2,10},{6,14},... | collective-permute-start | bytes 786440 | tf_op jit(solution)/shard_map/ppermute | solution.py:38
  8.3 1.6 %collective-permute-start.5 = (bf16[512,256]{1,0:T(8,128)(2,1)S(1)}, bf16[512,256]{1,0:T(8,128)(2,1)S(1)}, u32[]{:S(2)}, u32[]{:S(2)}) collective-permute-start(bf16[512,256]{1,0:T(8,128)(2,1)S(1)} %get-tuple-element.38._.refs_1_), channel_id=1, source_target_pairs={{0,4},{4,0},{8,12},{12,8},{1,5},{5,1},{9,13},{13,9},{2,6},{6,2},{1... | collective-permute-start | bytes 786440 | tf_op jit(solution)/shard_map/ppermute | solution.py:38
  9.9 5.8 %hold.1.refs_0_ = bf16[1,2,2048,2048]{3,2,1,0:T(8,128)(2,1)S(1)} custom-call(bf16[1,2,2048,2048]{3,2,1,0:T(8,128)(2,1)} %w_ref.1, bf16[512,256]{1,0:T(8,128)(2,1)S(1)} %get-tuple-element.38._.refs_1_), custom_call_target="tpu_custom_call" | custom-call | bytes 335544320 | tf_op jit(solution)/shard_map/hold/pallas_call | solution.py:96
  17.3 1.6 %up_first.2 = (bf16[2,2048,256]{2,1,0:T(8,128)(2,1)S(1)}, bf16[512,256]{1,0:T(8,128)(2,1)S(1)}) custom-call(bf16[1,2,2048,2048]{3,2,1,0:T(8,128)(2,1)S(1)} %hold.1.refs_0_, bf16[512,256]{1,0:T(8,128)(2,1)S(1)} %get-tuple-element.37.refs_2_.refs_1_, bf16[512,256]{1,0:T(8,128)(2,1)S(1)} %collective-permute-done.refs_2_, ...), custom_call_target="tpu_custom_call" | custom-call | bytes 1 | tf_op jit(solution)/shard_map/up_first/pallas_call | solution.py:67
  19.4 1.7 %collective-permute-done.4.refs_2_.refs_3_ = bf16[512,256]{1,0:T(8,128)(2,1)S(1)} collective-permute-done((bf16[512,256]{1,0:T(8,128)(2,1)S(1)}, bf16[512,256]{1,0:T(8,128)(2,1)S(1)}, u32[]{:S(2)}, u32[]{:S(2)}) %collective-permute-start.4) | collective-permute-done | bytes 262176 | tf_op jit(solution)/shard_map/ppermute | solution.py:38
  21.7 3.6 %up_rest.2 = (f32[512,256]{1,0:T(8,128)S(1)}, bf16[512,256]{1,0:T(8,128)(2,1)S(1)}, f32[512,256]{1,0:T(8,128)S(1)}) custom-call(bf16[1,2,2048,2048]{3,2,1,0:T(8,128)(2,1)S(1)} %hold.1.refs_0_, bf16[2,2048,256]{2,1,0:T(8,128)(2,1)S(1)} %get-tuple-element.42.refs_1_, bf16[512,256]{1,0:T(8,128)(2,1)S(1)} %collective-permute-done.4.refs_2_.refs_3_, ...), custom_call_target="tpu_custom_call" | custom-call | flops 20999999488 | bytes 1048576 | tf_op jit(solution)/shard_map/up_rest/pallas_call | solution.py:67
  25.3 2.9 %collective-permute-done.6.refs_0_ = bf16[512,256]{1,0:T(8,128)(2,1)S(1)} collective-permute-done((bf16[512,256]{1,0:T(8,128)(2,1)S(1)}, bf16[512,256]{1,0:T(8,128)(2,1)S(1)}, u32[]{:S(2)}, u32[]{:S(2)}) %collective-permute-start.6) | collective-permute-done | bytes 262176 | tf_op jit(solution)/shard_map/ppermute | solution.py:38
  28.8 7.0 %collective-permute-done.9.refs_2_ = bf16[512,256]{1,0:T(8,128)(2,1)S(1)} collective-permute-done((bf16[512,256]{1,0:T(8,128)(2,1)S(1)}, bf16[512,256]{1,0:T(8,128)(2,1)S(1)}, u32[]{:S(2)}, u32[]{:S(2)}) %collective-permute-start.9) | collective-permute-done | bytes 262176 | tf_op jit(solution)/shard_map/ppermute | solution.py:38
  35.8 2.6 %down_sibling.2 = (bf16[2,2048,256]{2,1,0:T(8,128)(2,1)S(1)}, f32[2,512,256]{2,1,0:T(8,128)S(1)}) custom-call(bf16[1,2,2048,2048]{3,2,1,0:T(8,128)(2,1)S(1)} %hold.1.refs_0_, bf16[512,256]{1,0:T(8,128)(2,1)S(1)} %get-tuple-element.38._.refs_1_, bf16[512,256]{1,0:T(8,128)(2,1)S(1)} %collective-permute-done.9.refs_2_, ...), custom_call_target="tpu_custom_call" | custom-call | flops 20999999488 | bytes 1048576 | tf_op jit(solution)/shard_map/down_sibling/pallas_call | solution.py:67
  38.5 1.2 %down_far.2.refs_0_ = f32[512,256]{1,0:T(8,128)S(1)} custom-call(bf16[1,2,2048,2048]{3,2,1,0:T(8,128)(2,1)S(1)} %hold.1.refs_0_, bf16[2,2048,256]{2,1,0:T(8,128)(2,1)S(1)} %get-tuple-element.49.refs_1_), custom_call_target="tpu_custom_call" | custom-call | flops 20999999488 | bytes 1048576 | tf_op jit(solution)/shard_map/down_far/pallas_call | solution.py:67
  39.8 1.3 %collective-permute-done.10.refs_1_.refs_2_ = f32[2,512,256]{2,1,0:T(8,128)S(1)} collective-permute-done((f32[2,512,256]{2,1,0:T(8,128)S(1)}, f32[2,512,256]{2,1,0:T(8,128)S(1)}, u32[]{:S(2)}, u32[]{:S(2)}) %collective-permute-start.10) | collective-permute-done | bytes 1048608 | tf_op jit(solution)/shard_map/ppermute | solution.py:53
  41.7 1.2 %down_own.2.refs_4_ = f32[512,256]{1,0:T(8,128)S(1)} custom-call(bf16[1,2,2048,2048]{3,2,1,0:T(8,128)(2,1)S(1)} %hold.1.refs_0_, bf16[2,2048,256]{2,1,0:T(8,128)(2,1)S(1)} %get-tuple-element.49.refs_1_, f32[2,512,256]{2,1,0:T(8,128)S(1)} %collective-permute-done.10.refs_1_.refs_2_, bf16[512,256]{1,0:T(8,128)(2,1)S(1)} %far_sum.2.refs_3_), custom_call_target="tpu_custom_call" | custom-call | flops 20999999488 | bytes 1048576 | tf_op jit(solution)/shard_map/down_own/pallas_call | solution.py:67
  43.0 4.5 %collective-permute-done.7.refs_0_ = bf16[512,256]{1,0:T(8,128)(2,1)S(1)} collective-permute-done((bf16[512,256]{1,0:T(8,128)(2,1)S(1)}, bf16[512,256]{1,0:T(8,128)(2,1)S(1)}, u32[]{:S(2)}, u32[]{:S(2)}) %collective-permute-start.7) | collective-permute-done | bytes 262176 | tf_op jit(solution)/shard_map/ppermute | solution.py:38
  47.5 2.0 %collective-permute-done.11.refs_3_ = bf16[512,256]{1,0:T(8,128)(2,1)S(1)} collective-permute-done((bf16[512,256]{1,0:T(8,128)(2,1)S(1)}, bf16[512,256]{1,0:T(8,128)(2,1)S(1)}, u32[]{:S(2)}, u32[]{:S(2)}) %collective-permute-start.11) | collective-permute-done | bytes 262176 | tf_op jit(solution)/shard_map/ppermute | solution.py:53
  49.7 1.6 %collective-permute-start.12 = (bf16[512,256]{1,0:T(8,128)(2,1)S(1)}, bf16[512,256]{1,0:T(8,128)(2,1)S(1)}, u32[]{:S(2)}, u32[]{:S(2)}) collective-permute-start(bf16[512,256]{1,0:T(8,128)(2,1)S(1)} %get-tuple-element.51), channel_id=1, source_target_pairs={{0,16},{16,0},{1,17},{17,1},{2,18},{18,2},{3,19},{19,3},{4,20},{20... | collective-permute-start | bytes 786440 | tf_op jit(solution)/shard_map/ppermute | solution.py:314
  51.3 6.0 %collective-permute-done.12.refs_0_.refs_1_ = bf16[512,256]{1,0:T(8,128)(2,1)S(1)} collective-permute-done((bf16[512,256]{1,0:T(8,128)(2,1)S(1)}, bf16[512,256]{1,0:T(8,128)(2,1)S(1)}, u32[]{:S(2)}, u32[]{:S(2)}) %collective-permute-start.12) | collective-permute-done | bytes 262176 | tf_op jit(solution)/shard_map/ppermute | solution.py:314
  59.5 1.3 %collective-permute-start.18 = (bf16[512,256]{1,0:T(8,128)(2,1)S(1)}, bf16[512,256]{1,0:T(8,128)(2,1)S(1)}, u32[]{:S(2)}, u32[]{:S(2)}) collective-permute-start(bf16[512,256]{1,0:T(8,128)(2,1)S(1)} %get-tuple-element.60.refs_1_), channel_id=1, source_target_pairs={{0,4},{4,0},{8,12},{12,8},{1,5},{5,1},{9,13},{13,9},{2,6},{6,2},{1... | collective-permute-start | bytes 786440 | tf_op jit(solution)/shard_map/ppermute | solution.py:38
  60.8 3.6 %collective-permute-done.14.refs_0_ = bf16[512,256]{1,0:T(8,128)(2,1)S(1)} collective-permute-done((bf16[512,256]{1,0:T(8,128)(2,1)S(1)}, bf16[512,256]{1,0:T(8,128)(2,1)S(1)}, u32[]{:S(2)}, u32[]{:S(2)}) %collective-permute-start.14) | collective-permute-done | bytes 262176 | tf_op jit(solution)/shard_map/ppermute | solution.py:53
  66.0 1.6 %up_first.3 = (bf16[2,2048,256]{2,1,0:T(8,128)(2,1)S(1)}, bf16[512,256]{1,0:T(8,128)(2,1)S(1)}) custom-call(bf16[1,2,2048,2048]{3,2,1,0:T(8,128)(2,1)S(1)} %hold.1.refs_0_, bf16[512,256]{1,0:T(8,128)(2,1)S(1)} %get-tuple-element.56.refs_1_, bf16[512,256]{1,0:T(8,128)(2,1)S(1)} %collective-permute-done.13.refs_2_, ...), custom_call_target="tpu_custom_call" | custom-call | bytes 1 | tf_op jit(solution)/shard_map/up_first/pallas_call | solution.py:67
  68.4 5.2 %collective-permute-done.17.refs_2_.refs_3_ = bf16[512,256]{1,0:T(8,128)(2,1)S(1)} collective-permute-done((bf16[512,256]{1,0:T(8,128)(2,1)S(1)}, bf16[512,256]{1,0:T(8,128)(2,1)S(1)}, u32[]{:S(2)}, u32[]{:S(2)}) %collective-permute-start.17) | collective-permute-done | bytes 262176 | tf_op jit(solution)/shard_map/ppermute | solution.py:38
  73.6 3.6 %up_rest.3 = (f32[512,256]{1,0:T(8,128)S(1)}, bf16[512,256]{1,0:T(8,128)(2,1)S(1)}, f32[512,256]{1,0:T(8,128)S(1)}) custom-call(bf16[1,2,2048,2048]{3,2,1,0:T(8,128)(2,1)S(1)} %hold.1.refs_0_, bf16[2,2048,256]{2,1,0:T(8,128)(2,1)S(1)} %get-tuple-element.59.refs_1_, bf16[512,256]{1,0:T(8,128)(2,1)S(1)} %collective-permute-done.17.refs_2_.refs_3_, ...), custom_call_target="tpu_custom_call" | custom-call | flops 20999999488 | bytes 1048576 | tf_op jit(solution)/shard_map/up_rest/pallas_call | solution.py:67
  77.2 2.0 %collective-permute-done.19.refs_0_ = bf16[512,256]{1,0:T(8,128)(2,1)S(1)} collective-permute-done((bf16[512,256]{1,0:T(8,128)(2,1)S(1)}, bf16[512,256]{1,0:T(8,128)(2,1)S(1)}, u32[]{:S(2)}, u32[]{:S(2)}) %collective-permute-start.19) | collective-permute-done | bytes 262176 | tf_op jit(solution)/shard_map/ppermute | solution.py:38
  80.5 6.6 %collective-permute-done.22.refs_2_ = bf16[512,256]{1,0:T(8,128)(2,1)S(1)} collective-permute-done((bf16[512,256]{1,0:T(8,128)(2,1)S(1)}, bf16[512,256]{1,0:T(8,128)(2,1)S(1)}, u32[]{:S(2)}, u32[]{:S(2)}) %collective-permute-start.22) | collective-permute-done | bytes 262176 | tf_op jit(solution)/shard_map/ppermute | solution.py:38
  87.0 2.6 %down_sibling.3 = (bf16[2,2048,256]{2,1,0:T(8,128)(2,1)S(1)}, f32[2,512,256]{2,1,0:T(8,128)S(1)}) custom-call(bf16[1,2,2048,2048]{3,2,1,0:T(8,128)(2,1)S(1)} %hold.1.refs_0_, bf16[512,256]{1,0:T(8,128)(2,1)S(1)} %get-tuple-element.60.refs_1_, bf16[512,256]{1,0:T(8,128)(2,1)S(1)} %collective-permute-done.22.refs_2_, ...), custom_call_target="tpu_custom_call" | custom-call | flops 20999999488 | bytes 1048576 | tf_op jit(solution)/shard_map/down_sibling/pallas_call | solution.py:67
  89.8 1.2 %down_far.3.refs_0_ = f32[512,256]{1,0:T(8,128)S(1)} custom-call(bf16[1,2,2048,2048]{3,2,1,0:T(8,128)(2,1)S(1)} %hold.1.refs_0_, bf16[2,2048,256]{2,1,0:T(8,128)(2,1)S(1)} %get-tuple-element.67.refs_1_), custom_call_target="tpu_custom_call" | custom-call | flops 20999999488 | bytes 1048576 | tf_op jit(solution)/shard_map/down_far/pallas_call | solution.py:67
  91.0 1.3 %collective-permute-done.23.refs_1_.refs_2_ = f32[2,512,256]{2,1,0:T(8,128)S(1)} collective-permute-done((f32[2,512,256]{2,1,0:T(8,128)S(1)}, f32[2,512,256]{2,1,0:T(8,128)S(1)}, u32[]{:S(2)}, u32[]{:S(2)}) %collective-permute-start.23) | collective-permute-done | bytes 1048608 | tf_op jit(solution)/shard_map/ppermute | solution.py:53
  92.4 1.6 %collective-permute-start.24 = (bf16[512,256]{1,0:T(8,128)(2,1)S(1)}, bf16[512,256]{1,0:T(8,128)(2,1)S(1)}, u32[]{:S(2)}, u32[]{:S(2)}) collective-permute-start(bf16[512,256]{1,0:T(8,128)(2,1)S(1)} %far_sum.3.refs_3_), channel_id=1, source_target_pairs={{0,2},{1,3},{2,0},{3,1},{4,6},{5,7},{6,4},{7,5},{8,10},{9,11},{10,... | collective-permute-start | bytes 786440 | tf_op jit(solution)/shard_map/ppermute | solution.py:53
  93.9 1.2 %down_own.3.refs_4_ = f32[512,256]{1,0:T(8,128)S(1)} custom-call(bf16[1,2,2048,2048]{3,2,1,0:T(8,128)(2,1)S(1)} %hold.1.refs_0_, bf16[2,2048,256]{2,1,0:T(8,128)(2,1)S(1)} %get-tuple-element.67.refs_1_, f32[2,512,256]{2,1,0:T(8,128)S(1)} %collective-permute-done.23.refs_1_.refs_2_, bf16[512,256]{1,0:T(8,128)(2,1)S(1)} %far_sum.3.refs_3_), custom_call_target="tpu_custom_call" | custom-call | flops 20999999488 | bytes 1048576 | tf_op jit(solution)/shard_map/down_own/pallas_call | solution.py:67
  95.2 4.5 %collective-permute-done.20.refs_0_ = bf16[512,256]{1,0:T(8,128)(2,1)S(1)} collective-permute-done((bf16[512,256]{1,0:T(8,128)(2,1)S(1)}, bf16[512,256]{1,0:T(8,128)(2,1)S(1)}, u32[]{:S(2)}, u32[]{:S(2)}) %collective-permute-start.20) | collective-permute-done | bytes 262176 | tf_op jit(solution)/shard_map/ppermute | solution.py:38
  101.0 1.5 %collective-permute-start.25 = (bf16[512,256]{1,0:T(8,128)(2,1)S(1)}, bf16[512,256]{1,0:T(8,128)(2,1)S(1)}, u32[]{:S(2)}, u32[]{:S(2)}) collective-permute-start(bf16[512,256]{1,0:T(8,128)(2,1)S(1)} %get-tuple-element.69), channel_id=1, source_target_pairs={{0,16},{16,0},{1,17},{17,1},{2,18},{18,2},{3,19},{19,3},{4,20},{20... | collective-permute-start | bytes 786440 | tf_op jit(solution)/shard_map/ppermute | solution.py:314
  102.5 6.0 %collective-permute-done.25.refs_0_.refs_1_ = bf16[512,256]{1,0:T(8,128)(2,1)S(1)} collective-permute-done((bf16[512,256]{1,0:T(8,128)(2,1)S(1)}, bf16[512,256]{1,0:T(8,128)(2,1)S(1)}, u32[]{:S(2)}, u32[]{:S(2)}) %collective-permute-start.25) | collective-permute-done | bytes 262176 | tf_op jit(solution)/shard_map/ppermute | solution.py:314
  (55 shorter events, 14.8 us)
Async XLA Ops:
  0.6 1.0 copy-start
  1.7 0.7 copy-start.4
  2.4 3.1 %copy-start.1 = (f32[1,512,256]{2,1,0:T(8,128)S(1)}, f32[1,512,256]{2,1,0:T(8,128)}, u32[]{:S(2)}) copy-start(f32[1,512,256]{2,1,0:T(8,128)} %refs_0_.3) | copy-start | bytes 1572868
  2.4 3.1 %copy-start.5 = (f32[1,512]{1,0:T(1,128)S(1)}, f32[1,512]{1,0:T(1,128)}, u32[]{:S(2)}) copy-start(f32[1,512]{1,0:T(1,128)} %refs_1_.3) | copy-start | bytes 6148
  2.5 13.2 %collective-permute-start.1 = (bf16[512,256]{1,0:T(8,128)(2,1)S(1)}, bf16[512,256]{1,0:T(8,128)(2,1)S(1)}, u32[]{:S(2)}, u32[]{:S(2)}) collective-permute-start(bf16[512,256]{1,0:T(8,128)(2,1)S(1)} %get-tuple-element.37.refs_2_.refs_1_), channel_id=1, source_target_pairs={{0,2},{1,3},{2,0},{3,1},{4,6},{5,7},{6,4},{7,5},{8,10},{9,11},{10,... | collective-permute-start | bytes 786440 | tf_op jit(solution)/shard_map/ppermute | solution.py:53
  5.5 10.8 %collective-permute-start = (bf16[512,256]{1,0:T(8,128)(2,1)S(1)}, bf16[512,256]{1,0:T(8,128)(2,1)S(1)}, u32[]{:S(2)}, u32[]{:S(2)}) collective-permute-start(bf16[512,256]{1,0:T(8,128)(2,1)S(1)} %get-tuple-element.37.refs_2_.refs_1_), channel_id=1, source_target_pairs={{0,1},{1,0},{2,3},{3,2},{4,5},{5,4},{6,7},{7,6},{8,9},{9,8},{10,11... | collective-permute-start | bytes 786440 | tf_op jit(solution)/shard_map/ppermute | solution.py:53
  5.6 15.4 %collective-permute-start.4 = (bf16[512,256]{1,0:T(8,128)(2,1)S(1)}, bf16[512,256]{1,0:T(8,128)(2,1)S(1)}, u32[]{:S(2)}, u32[]{:S(2)}) collective-permute-start(bf16[512,256]{1,0:T(8,128)(2,1)S(1)} %get-tuple-element.38._.refs_1_), channel_id=1, source_target_pairs={{0,8},{4,12},{8,0},{12,4},{1,9},{5,13},{9,1},{13,5},{2,10},{6,14},... | collective-permute-start | bytes 786440 | tf_op jit(solution)/shard_map/ppermute | solution.py:38
  8.3 13.4 %collective-permute-start.5 = (bf16[512,256]{1,0:T(8,128)(2,1)S(1)}, bf16[512,256]{1,0:T(8,128)(2,1)S(1)}, u32[]{:S(2)}, u32[]{:S(2)}) collective-permute-start(bf16[512,256]{1,0:T(8,128)(2,1)S(1)} %get-tuple-element.38._.refs_1_), channel_id=1, source_target_pairs={{0,4},{4,0},{8,12},{12,8},{1,5},{5,1},{9,13},{13,9},{2,6},{6,2},{1... | collective-permute-start | bytes 786440 | tf_op jit(solution)/shard_map/ppermute | solution.py:38
  15.7 1.4 %collective-permute-start.2 = (bf16[256,256]{1,0:T(8,128)(2,1)S(1)}, bf16[256,256]{1,0:T(8,128)(2,1)S(1)}, u32[]{:S(2)}, u32[]{:S(2)}) collective-permute-start(bf16[256,256]{1,0:T(8,128)(2,1)S(1)} %get-tuple-element.40.refs_3_), channel_id=1, source_target_pairs={{0,1},{1,0},{2,3},{3,2},{4,5},{5,4},{6,7},{7,6},{8,9},{9,8},{10,11... | collective-permute-start | bytes 393224 | tf_op jit(solution)/shard_map/ppermute | solution.py:53
  15.8 1.5 %collective-permute-start.3 = (bf16[256,256]{1,0:T(8,128)(2,1)S(1)}, bf16[256,256]{1,0:T(8,128)(2,1)S(1)}, u32[]{:S(2)}, u32[]{:S(2)}) collective-permute-start(bf16[256,256]{1,0:T(8,128)(2,1)S(1)} %get-tuple-element.41.refs_4_), channel_id=1, source_target_pairs={{0,1},{1,0},{2,3},{3,2},{4,5},{5,4},{6,7},{7,6},{8,9},{9,8},{10,11... | collective-permute-start | bytes 393224 | tf_op jit(solution)/shard_map/ppermute | solution.py:53
  18.9 9.2 %collective-permute-start.6 = (bf16[512,256]{1,0:T(8,128)(2,1)S(1)}, bf16[512,256]{1,0:T(8,128)(2,1)S(1)}, u32[]{:S(2)}, u32[]{:S(2)}) collective-permute-start(bf16[512,256]{1,0:T(8,128)(2,1)S(1)} %get-tuple-element.44), channel_id=1, source_target_pairs={{0,4},{4,0},{8,12},{12,8},{1,5},{5,1},{9,13},{13,9},{2,6},{6,2},{1... | collective-permute-start | bytes 786440 | tf_op jit(solution)/shard_map/ppermute | solution.py:38
  21.0 14.7 %collective-permute-start.9 = (bf16[512,256]{1,0:T(8,128)(2,1)S(1)}, bf16[512,256]{1,0:T(8,128)(2,1)S(1)}, u32[]{:S(2)}, u32[]{:S(2)}) collective-permute-start(bf16[512,256]{1,0:T(8,128)(2,1)S(1)} %collective-permute-done.4.refs_2_.refs_3_), channel_id=1, source_target_pairs={{0,4},{4,0},{8,12},{12,8},{1,5},{5,1},{9,13},{13,9},{2,6},{6,2},{1... | collective-permute-start | bytes 786440 | tf_op jit(solution)/shard_map/ppermute | solution.py:38
  28.2 19.4 %collective-permute-start.8 = (bf16[512,256]{1,0:T(8,128)(2,1)S(1)}, bf16[512,256]{1,0:T(8,128)(2,1)S(1)}, u32[]{:S(2)}, u32[]{:S(2)}) collective-permute-start(bf16[512,256]{1,0:T(8,128)(2,1)S(1)} %hop.2.refs_5_), channel_id=1, source_target_pairs={{0,8},{4,12},{8,0},{12,4},{1,9},{5,13},{9,1},{13,5},{2,10},{6,14},... | collective-permute-start | bytes 786440 | tf_op jit(solution)/shard_map/ppermute | solution.py:38
  38.4 2.7 %collective-permute-start.10 = (f32[2,512,256]{2,1,0:T(8,128)S(1)}, f32[2,512,256]{2,1,0:T(8,128)S(1)}, u32[]{:S(2)}, u32[]{:S(2)}) collective-permute-start(f32[2,512,256]{2,1,0:T(8,128)S(1)} %get-tuple-element.50), channel_id=1, source_target_pairs={{0,1},{1,0},{2,3},{3,2},{4,5},{5,4},{6,7},{7,6},{8,9},{9,8},{10,11... | collective-permute-start | bytes 3145736 | tf_op jit(solution)/shard_map/ppermute | solution.py:53
  38.4 9.1 %collective-permute-start.7 = (bf16[512,256]{1,0:T(8,128)(2,1)S(1)}, bf16[512,256]{1,0:T(8,128)(2,1)S(1)}, u32[]{:S(2)}, u32[]{:S(2)}) collective-permute-start(bf16[512,256]{1,0:T(8,128)(2,1)S(1)} %get-tuple-element.46.refs_2_), channel_id=1, source_target_pairs={{0,4},{4,0},{8,12},{12,8},{1,5},{5,1},{9,13},{13,9},{2,6},{6,2},{1... | collective-permute-start | bytes 786440 | tf_op jit(solution)/shard_map/ppermute | solution.py:38
  41.1 8.4 %collective-permute-start.11 = (bf16[512,256]{1,0:T(8,128)(2,1)S(1)}, bf16[512,256]{1,0:T(8,128)(2,1)S(1)}, u32[]{:S(2)}, u32[]{:S(2)}) collective-permute-start(bf16[512,256]{1,0:T(8,128)(2,1)S(1)} %far_sum.2.refs_3_), channel_id=1, source_target_pairs={{0,2},{1,3},{2,0},{3,1},{4,6},{5,7},{6,4},{7,5},{8,10},{9,11},{10,... | collective-permute-start | bytes 786440 | tf_op jit(solution)/shard_map/ppermute | solution.py:53
  49.6 7.7 %copy-start.2 = (f32[512,256]{1,0:T(8,128)S(1)}, f32[512,256]{1,0:T(8,128)}, u32[]{:S(2)}) copy-start(f32[512,256]{1,0:T(8,128)} %refs_2_.3) | copy-start | bytes 1572868
  49.7 7.6 %collective-permute-start.12 = (bf16[512,256]{1,0:T(8,128)(2,1)S(1)}, bf16[512,256]{1,0:T(8,128)(2,1)S(1)}, u32[]{:S(2)}, u32[]{:S(2)}) collective-permute-start(bf16[512,256]{1,0:T(8,128)(2,1)S(1)} %get-tuple-element.51), channel_id=1, source_target_pairs={{0,16},{16,0},{1,17},{17,1},{2,18},{18,2},{3,19},{19,3},{4,20},{20... | collective-permute-start | bytes 786440 | tf_op jit(solution)/shard_map/ppermute | solution.py:314
  57.7 6.7 %collective-permute-start.14 = (bf16[512,256]{1,0:T(8,128)(2,1)S(1)}, bf16[512,256]{1,0:T(8,128)(2,1)S(1)}, u32[]{:S(2)}, u32[]{:S(2)}) collective-permute-start(bf16[512,256]{1,0:T(8,128)(2,1)S(1)} %get-tuple-element.56.refs_1_), channel_id=1, source_target_pairs={{0,2},{1,3},{2,0},{3,1},{4,6},{5,7},{6,4},{7,5},{8,10},{9,11},{10,... | collective-permute-start | bytes 786440 | tf_op jit(solution)/shard_map/ppermute | solution.py:53
  58.3 6.7 %collective-permute-start.13 = (bf16[512,256]{1,0:T(8,128)(2,1)S(1)}, bf16[512,256]{1,0:T(8,128)(2,1)S(1)}, u32[]{:S(2)}, u32[]{:S(2)}) collective-permute-start(bf16[512,256]{1,0:T(8,128)(2,1)S(1)} %get-tuple-element.56.refs_1_), channel_id=1, source_target_pairs={{0,1},{1,0},{2,3},{3,2},{4,5},{5,4},{6,7},{7,6},{8,9},{9,8},{10,11... | collective-permute-start | bytes 786440 | tf_op jit(solution)/shard_map/ppermute | solution.py:53
  58.3 15.3 %collective-permute-start.17 = (bf16[512,256]{1,0:T(8,128)(2,1)S(1)}, bf16[512,256]{1,0:T(8,128)(2,1)S(1)}, u32[]{:S(2)}, u32[]{:S(2)}) collective-permute-start(bf16[512,256]{1,0:T(8,128)(2,1)S(1)} %get-tuple-element.60.refs_1_), channel_id=1, source_target_pairs={{0,8},{4,12},{8,0},{12,4},{1,9},{5,13},{9,1},{13,5},{2,10},{6,14},... | collective-permute-start | bytes 786440 | tf_op jit(solution)/shard_map/ppermute | solution.py:38
  59.5 14.1 %collective-permute-start.18 = (bf16[512,256]{1,0:T(8,128)(2,1)S(1)}, bf16[512,256]{1,0:T(8,128)(2,1)S(1)}, u32[]{:S(2)}, u32[]{:S(2)}) collective-permute-start(bf16[512,256]{1,0:T(8,128)(2,1)S(1)} %get-tuple-element.60.refs_1_), channel_id=1, source_target_pairs={{0,4},{4,0},{8,12},{12,8},{1,5},{5,1},{9,13},{13,9},{2,6},{6,2},{1... | collective-permute-start | bytes 786440 | tf_op jit(solution)/shard_map/ppermute | solution.py:38
  64.4 1.4 %collective-permute-start.15 = (bf16[256,256]{1,0:T(8,128)(2,1)S(1)}, bf16[256,256]{1,0:T(8,128)(2,1)S(1)}, u32[]{:S(2)}, u32[]{:S(2)}) collective-permute-start(bf16[256,256]{1,0:T(8,128)(2,1)S(1)} %get-tuple-element.57.refs_3_), channel_id=1, source_target_pairs={{0,1},{1,0},{2,3},{3,2},{4,5},{5,4},{6,7},{7,6},{8,9},{9,8},{10,11... | collective-permute-start | bytes 393224 | tf_op jit(solution)/shard_map/ppermute | solution.py:53
  64.4 1.5 %collective-permute-start.16 = (bf16[256,256]{1,0:T(8,128)(2,1)S(1)}, bf16[256,256]{1,0:T(8,128)(2,1)S(1)}, u32[]{:S(2)}, u32[]{:S(2)}) collective-permute-start(bf16[256,256]{1,0:T(8,128)(2,1)S(1)} %get-tuple-element.58.refs_4_), channel_id=1, source_target_pairs={{0,1},{1,0},{2,3},{3,2},{4,5},{5,4},{6,7},{7,6},{8,9},{9,8},{10,11... | collective-permute-start | bytes 393224 | tf_op jit(solution)/shard_map/ppermute | solution.py:53
  67.6 11.6 %collective-permute-start.19 = (bf16[512,256]{1,0:T(8,128)(2,1)S(1)}, bf16[512,256]{1,0:T(8,128)(2,1)S(1)}, u32[]{:S(2)}, u32[]{:S(2)}) collective-permute-start(bf16[512,256]{1,0:T(8,128)(2,1)S(1)} %get-tuple-element.62), channel_id=1, source_target_pairs={{0,4},{4,0},{8,12},{12,8},{1,5},{5,1},{9,13},{13,9},{2,6},{6,2},{1... | collective-permute-start | bytes 786440 | tf_op jit(solution)/shard_map/ppermute | solution.py:38
  73.6 13.4 %collective-permute-start.22 = (bf16[512,256]{1,0:T(8,128)(2,1)S(1)}, bf16[512,256]{1,0:T(8,128)(2,1)S(1)}, u32[]{:S(2)}, u32[]{:S(2)}) collective-permute-start(bf16[512,256]{1,0:T(8,128)(2,1)S(1)} %collective-permute-done.17.refs_2_.refs_3_), channel_id=1, source_target_pairs={{0,4},{4,0},{8,12},{12,8},{1,5},{5,1},{9,13},{13,9},{2,6},{6,2},{1... | collective-permute-start | bytes 786440 | tf_op jit(solution)/shard_map/ppermute | solution.py:38
  79.2 20.5 %collective-permute-start.21 = (bf16[512,256]{1,0:T(8,128)(2,1)S(1)}, bf16[512,256]{1,0:T(8,128)(2,1)S(1)}, u32[]{:S(2)}, u32[]{:S(2)}) collective-permute-start(bf16[512,256]{1,0:T(8,128)(2,1)S(1)} %hop.3.refs_5_), channel_id=1, source_target_pairs={{0,8},{4,12},{8,0},{12,4},{1,9},{5,13},{9,1},{13,5},{2,10},{6,14},... | collective-permute-start | bytes 786440 | tf_op jit(solution)/shard_map/ppermute | solution.py:38
  89.6 2.7 %collective-permute-start.23 = (f32[2,512,256]{2,1,0:T(8,128)S(1)}, f32[2,512,256]{2,1,0:T(8,128)S(1)}, u32[]{:S(2)}, u32[]{:S(2)}) collective-permute-start(f32[2,512,256]{2,1,0:T(8,128)S(1)} %get-tuple-element.68), channel_id=1, source_target_pairs={{0,1},{1,0},{2,3},{3,2},{4,5},{5,4},{6,7},{7,6},{8,9},{9,8},{10,11... | collective-permute-start | bytes 3145736 | tf_op jit(solution)/shard_map/ppermute | solution.py:53
  89.7 10.0 %collective-permute-start.20 = (bf16[512,256]{1,0:T(8,128)(2,1)S(1)}, bf16[512,256]{1,0:T(8,128)(2,1)S(1)}, u32[]{:S(2)}, u32[]{:S(2)}) collective-permute-start(bf16[512,256]{1,0:T(8,128)(2,1)S(1)} %get-tuple-element.64.refs_2_), channel_id=1, source_target_pairs={{0,4},{4,0},{8,12},{12,8},{1,5},{5,1},{9,13},{13,9},{2,6},{6,2},{1... | collective-permute-start | bytes 786440 | tf_op jit(solution)/shard_map/ppermute | solution.py:38
  92.4 8.4 %collective-permute-start.24 = (bf16[512,256]{1,0:T(8,128)(2,1)S(1)}, bf16[512,256]{1,0:T(8,128)(2,1)S(1)}, u32[]{:S(2)}, u32[]{:S(2)}) collective-permute-start(bf16[512,256]{1,0:T(8,128)(2,1)S(1)} %far_sum.3.refs_3_), channel_id=1, source_target_pairs={{0,2},{1,3},{2,0},{3,1},{4,6},{5,7},{6,4},{7,5},{8,10},{9,11},{10,... | collective-permute-start | bytes 786440 | tf_op jit(solution)/shard_map/ppermute | solution.py:53
  100.8 7.7 %copy-start.3 = (f32[512,256]{1,0:T(8,128)S(1)}, f32[512,256]{1,0:T(8,128)}, u32[]{:S(2)}) copy-start(f32[512,256]{1,0:T(8,128)} %refs_2_.3) | copy-start | bytes 1572868
  101.0 7.6 %collective-permute-start.25 = (bf16[512,256]{1,0:T(8,128)(2,1)S(1)}, bf16[512,256]{1,0:T(8,128)(2,1)S(1)}, u32[]{:S(2)}, u32[]{:S(2)}) collective-permute-start(bf16[512,256]{1,0:T(8,128)(2,1)S(1)} %get-tuple-element.69), channel_id=1, source_target_pairs={{0,16},{16,0},{1,17},{17,1},{2,18},{18,2},{3,19},{19,3},{4,20},{20... | collective-permute-start | bytes 786440 | tf_op jit(solution)/shard_map/ppermute | solution.py:314

commit v4 on v3

--- a/solution.py
+++ b/solution.py
@@ -14,7 +14,7 @@
 UNREAD = pl.BlockSpec(memory_space=pl.ANY)
 LANES = 128
 DECLARED = 21 * 10**9
-CHEAP = {"up_first": 0, "split": 0}
+CHEAP = {"up_first": 0, "split": 0, "down_own": 0}
 CONTRACT_ROWS = (((0,), (0,)), ((), ()))
 
 
@@ -87,24 +87,6 @@
     return pl.ds(pl.multiple_of(block * strip, strip), strip)
 
 
-def hold(prop, after):
-    def kernel(w_ref, _, out_ref, sem):
-        copy = pltpu.make_async_copy(w_ref, out_ref, sem)
-        copy.start()
-        copy.wait()
-
-    return pl.pallas_call(
-        kernel,
-        in_specs=[pl.BlockSpec(memory_space=pltpu.HBM), UNREAD],
-        out_specs=WHOLE,
-        out_shape=pltpu.VMEM(prop.shape, prop.dtype),
-        scratch_shapes=[pltpu.SemaphoreType.DMA],
-        name="hold",
-        cost_estimate=pl.CostEstimate(flops=0, bytes_accessed=40 * prop.size, transcendentals=0),
-        compiler_params=pltpu.CompilerParams(vmem_limit_bytes=36 * 2**20),
-    )(prop, after)
-
-
 def place_block(pair_ref, block_ref, rows, sources):
     values = block_ref[...]
     pair_ref[0, rows, :] = values
@@ -122,9 +104,13 @@
     return jnp.concatenate(pieces, axis=1)
 
 
-def ready_kernel(field_ref, refl_ref, low_ref, factor_ref):
+def ready_kernel(field_ref, low_ref):
     low_ref[...] = field_ref[0].astype(BF16)
-    factor_ref[...] = spread(refl_ref)
+
+
+def factor_kernel(down_ref, up_ref, down_factor, up_factor):
+    down_factor[...] = spread(down_ref)
+    up_factor[...] = spread(up_ref)
 
 
 def down_dot(w_ref, pair_ref, rows):
@@ -149,21 +135,29 @@
     blocks, pair_ref, out_ref = refs[:size], refs[size], refs[size + 1]
     for s in range(size):
         place_block(pair_ref, blocks[s], rows_at(row_block(s, size), strip), sources)
-    me = lax.axis_index("col")
-    for k in range(2):
-        out_ref[k] = down_dot(w_ref, pair_ref, rows_at(me ^ (1 + 2 * k), strip))
-
-
-def down_far_kernel(strip, w_ref, pair_ref, out_ref):
-    out_ref[...] = down_dot(w_ref, pair_ref, rows_at(lax.axis_index("col") ^ 2, strip))
+    out_ref[...] = down_dot(w_ref, pair_ref, rows_at(lax.axis_index("col") ^ 3, strip))
+
+
+def down_kernel(strip, apart, w_ref, pair_ref, out_ref):
+    out_ref[...] = down_dot(w_ref, pair_ref, rows_at(lax.axis_index("col") ^ apart, strip))
 
 
 def far_sum_kernel(own_ref, arrived_ref, out_ref):
-    out_ref[...] = (own_ref[...] + arrived_ref[1]).astype(BF16)
-
-
-def down_own_kernel(strip, w_ref, pair_ref, arrived_ref, out_ref):
-    out_ref[...] = down_dot(w_ref, pair_ref, rows_at(lax.axis_index("col"), strip)) + arrived_ref[0]
+    out_ref[...] = (own_ref[...] + arrived_ref[...]).astype(BF16)
+
+
+def down_near_kernel(strip, w_ref, pair_ref, *part_refs):
+    half = strip // 2
+    for k, ref in enumerate(part_refs):
+        rows = rows_at(2 * (lax.axis_index("col") ^ 1) + k, half)
+        ref[...] = down_dot(w_ref, pair_ref, rows).astype(BF16)
+
+
+def down_own_kernel(strip, w_ref, pair_ref, first_ref, second_ref, out_ref):
+    half = strip // 2
+    for k, ref in enumerate((first_ref, second_ref)):
+        rows = rows_at(2 * lax.axis_index("col") + k, half)
+        out_ref[k * half : (k + 1) * half, :] = down_dot(w_ref, pair_ref, rows) + ref[...].astype(F32)
 
 
 def up_first_kernel(size, strip, sources, w_ref, *refs):
@@ -249,17 +243,15 @@
     tall, wide = prop.shape[2], prop.shape[3]
     low, full = array((strip, width), BF16), array((strip, width), F32)
     factor = array((strip, LANES), F32)
-    up_low, refl_below = call(ready_kernel, [low, factor], "ready_up", [up_init, refl_up])
-    down_low, refl_above = call(
-        ready_kernel, [low, factor], "ready_down", [down_init, refl_down], [up_low]
-    )
-    w = pltpu.with_memory_space_constraint(hold(prop, down_low), pltpu.VMEM)
+    (up_low,) = call(ready_kernel, [low], "ready_up", [up_init])
+    (down_low,) = call(ready_kernel, [low], "ready_down", [down_init], [up_low])
+    w = prop
     for sweep in range(PASSES):
         last = sweep == PASSES - 1
         near = col_swap(up_low, 1)
         far = col_swap(up_low, 2)
         if sweep == 0:
-            far = behind(far, w)
+            far = behind(far, down_low)
         parts = call(split_kernel, [array((strip // 2, width), BF16)] * 2, "split", [far])
         blocks_up = [up_low, near, *parts, col_swap(parts[0], 1), col_swap(parts[1], 1)]
         if size == 4:
@@ -295,17 +287,24 @@
             before_down = [own_up[0]]
         pair_down, to_sibling = call(
             functools.partial(down_sibling_kernel, size, strip, sources),
-            [array((2, wide, width), BF16), array((2, strip, width), F32)],
+            [array((2, wide, width), BF16), full],
             "down_sibling", [w, *blocks_down], before_down,
         )
-        from_sibling = col_swap(to_sibling, 1)
-        (own_far,) = call(functools.partial(down_far_kernel, strip), [full], "down_far", [w, pair_down])
-        (to_far,) = call(far_sum_kernel, [low], "far_sum", [own_far, from_sibling])
+        (own_far,) = call(functools.partial(down_kernel, strip, 2), [full], "down_far", [w, pair_down])
+        (to_far,) = call(far_sum_kernel, [low], "far_sum", [own_far, col_swap(to_sibling, 1)])
         from_far = col_swap(to_far, 2)
+        parts = call(
+            functools.partial(down_near_kernel, strip), [array((strip // 2, width), BF16)] * 2,
+            "down_near", [w, pair_down], [to_far],
+        )
         (own_down,) = call(
             functools.partial(down_own_kernel, strip), [full], "down_own",
-            [w, pair_down, from_sibling], [to_far],
-        )
+            [w, pair_down, *(col_swap(part, 1) for part in parts)],
+        )
+        if sweep == 0:
+            refl_above, refl_below = call(
+                factor_kernel, [factor] * 2, "factors", [refl_down, refl_up], [own_down]
+            )
         if lax.axis_size("depth") == 2:
             back, trans, passed_on = call(
                 functools.partial(sums_kernel, len(arrived)), [full, full, low], "sums",

time: 110 us -> 107 us (0.973)
  Pallas kernels: 28.6 us -> 23.2 us
  starting transfers between devices: 20.8 us -> 25.5 us
  waiting for transfers between devices: 57.7 us -> 56.5 us
    pallas_call x1 -> x0, Pallas kernels: 5.78 us -> none  [hold(): pl.pallas_call(kernel, in_specs=[pl.BlockSpec(memory_space=pltpu.HBM), UN...]
    ppermute x12, starting transfers between devices: 10.5 us -> 14.1 us  [row_swap(): lax.ppermute(x, 'row', [(r, r ^ bit) for r in range(lax.axis_size('row'))])]
    ppermute x12, waiting for transfers between devices: 34.3 us -> 33.1 us  [row_swap(): lax.ppermute(x, 'row', [(r, r ^ bit) for r in range(lax.axis_size('row'))])]
    ppermute x12 -> x16, waiting for transfers between devices: 11.4 us -> 10.2 us  [col_swap(): lax.ppermute(x, 'col', [(c, c ^ bit) for c in range(lax.axis_size('col'))])]
    ppermute x2, waiting for transfers between devices: 12 us -> 13.2 us  [body(): from_above = from_below = lax.ppermute(passed_on, 'depth', [(0, 1), (1, 0)])]
    ppermute x12 -> x16, starting transfers between devices: 7.09 us -> 8.18 us  [col_swap(): lax.ppermute(x, 'col', [(c, c ^ bit) for c in range(lax.axis_size('col'))])]
    pallas_call x22 -> x25, Pallas kernels: 22.9 us -> 23.2 us  [call(): pl.pallas_call(ordered, in_specs=[WHOLE] * count + [UNREAD] * len(after),...]
  transfers between devices with their start and end apart: 26 -> 30, of which waited for: 19 -> 23; matrix products, arithmetic and copies ran while one was open for 0% -> 0% of each run, Pallas kernels for 24% -> 20%
where the time goes in v4:
time: 107 us
  waiting for transfers between devices  56.5 us (53%)
  starting transfers between devices  25.5 us (24%)
  Pallas kernels  23.2 us (22%)
  local copies, waits for them, and re-layouts  1.1 us (1%)
    ppermute x12, waiting for transfers between devices, row_swap(): lax.ppermute(x, 'row', [(r, r ^ bit) for r in range(lax.axis_size('row'))])  33.1 us
    pallas_call x25, Pallas kernels, call(): pl.pallas_call(ordered, in_specs=[WHOLE] * count + [UNREAD] * len(after),...  23.2 us
    ppermute x12, starting transfers between devices, row_swap(): lax.ppermute(x, 'row', [(r, r ^ bit) for r in range(lax.axis_size('row'))])  14.1 us
    ppermute x2, waiting for transfers between devices, body(): from_above = from_below = lax.ppermute(passed_on, 'depth', [(0, 1), (1, 0)])  13.2 us
    ppermute x16, waiting for transfers between devices, col_swap(): lax.ppermute(x, 'col', [(c, c ^ bit) for c in range(lax.axis_size('col'))])  10.2 us
    ppermute x16, starting transfers between devices, col_swap(): lax.ppermute(x, 'col', [(c, c ^ bit) for c in range(lax.axis_size('col'))])  8.18 us
    ppermute x2, starting transfers between devices, body(): from_above = from_below = lax.ppermute(passed_on, 'depth', [(0, 1), (1, 0)])  3.25 us
  transfers between devices with their start and end apart: 30, of which 23 were waited for; matrix products, arithmetic and copies ran while one was open for 0% of the time, Pallas kernels for 20%

profile of v4, /device:TPU:0, one launch (start us, length us, event | category | flops | bytes accessed | tf_op | source)
XLA Modules:
  0.0 107.2 jit_solution(6391485037884844379)
XLA Ops:
  1.7 3.0 %collective-permute-start.1 = (bf16[512,256]{1,0:T(8,128)(2,1)S(1)}, bf16[512,256]{1,0:T(8,128)(2,1)S(1)}, u32[]{:S(2)}, u32[]{:S(2)}) collective-permute-start(bf16[512,256]{1,0:T(8,128)(2,1)S(1)} %ready_up.1.refs_1_), channel_id=1, source_target_pairs={{0,2},{1,3},{2,0},{3,1},{4,6},{5,7},{6,4},{7,5},{8,10},{9,11},{10,... | collective-permute-start | bytes 786440 | tf_op jit(solution)/shard_map/ppermute | solution.py:53
  4.8 2.7 %collective-permute-start.4 = (bf16[512,256]{1,0:T(8,128)(2,1)S(1)}, bf16[512,256]{1,0:T(8,128)(2,1)S(1)}, u32[]{:S(2)}, u32[]{:S(2)}) collective-permute-start(bf16[512,256]{1,0:T(8,128)(2,1)S(1)} %ready_down.1.refs_1_), channel_id=1, source_target_pairs={{0,8},{4,12},{8,0},{12,4},{1,9},{5,13},{9,1},{13,5},{2,10},{6,14},... | collective-permute-start | bytes 786440 | tf_op jit(solution)/shard_map/ppermute | solution.py:38
  7.4 1.6 %collective-permute-start.5 = (bf16[512,256]{1,0:T(8,128)(2,1)S(1)}, bf16[512,256]{1,0:T(8,128)(2,1)S(1)}, u32[]{:S(2)}, u32[]{:S(2)}) collective-permute-start(bf16[512,256]{1,0:T(8,128)(2,1)S(1)} %ready_down.1.refs_1_), channel_id=1, source_target_pairs={{0,4},{4,0},{8,12},{12,8},{1,5},{5,1},{9,13},{13,9},{2,6},{6,2},{1... | collective-permute-start | bytes 786440 | tf_op jit(solution)/shard_map/ppermute | solution.py:38
  9.0 2.0 %collective-permute-done.1.refs_0_ = bf16[512,256]{1,0:T(8,128)(2,1)S(1)} collective-permute-done((bf16[512,256]{1,0:T(8,128)(2,1)S(1)}, bf16[512,256]{1,0:T(8,128)(2,1)S(1)}, u32[]{:S(2)}, u32[]{:S(2)}) %collective-permute-start.1) | collective-permute-done | bytes 262176 | tf_op jit(solution)/shard_map/ppermute | solution.py:53
  12.7 1.6 %up_first.2 = (bf16[2,2048,256]{2,1,0:T(8,128)(2,1)S(1)}, bf16[512,256]{1,0:T(8,128)(2,1)S(1)}) custom-call(bf16[1,2,2048,2048]{3,2,1,0:T(8,128)(2,1)S(1)} %bitcast.1, bf16[512,256]{1,0:T(8,128)(2,1)S(1)} %ready_up.1.refs_1_, bf16[512,256]{1,0:T(8,128)(2,1)S(1)} %collective-permute-done.refs_2_, bf16[256,256]{1,0:T(8,128)(2,1)S(1)} %get-tuple-element.40.refs_3_, ...), custom_call_target="tpu_custom_call" | custom-call | bytes 1 | tf_op jit(solution)/shard_map/up_first/pallas_call | solution.py:67
  14.3 1.8 %collective-permute-start.6 = (bf16[512,256]{1,0:T(8,128)(2,1)S(1)}, bf16[512,256]{1,0:T(8,128)(2,1)S(1)}, u32[]{:S(2)}, u32[]{:S(2)}) collective-permute-start(bf16[512,256]{1,0:T(8,128)(2,1)S(1)} %get-tuple-element.44), channel_id=1, source_target_pairs={{0,4},{4,0},{8,12},{12,8},{1,5},{5,1},{9,13},{13,9},{2,6},{6,2},{1... | collective-permute-start | bytes 786440 | tf_op jit(solution)/shard_map/ppermute | solution.py:38
  16.1 4.0 %collective-permute-done.4.refs_2_.refs_3_ = bf16[512,256]{1,0:T(8,128)(2,1)S(1)} collective-permute-done((bf16[512,256]{1,0:T(8,128)(2,1)S(1)}, bf16[512,256]{1,0:T(8,128)(2,1)S(1)}, u32[]{:S(2)}, u32[]{:S(2)}) %collective-permute-start.4) | collective-permute-done | bytes 262176 | tf_op jit(solution)/shard_map/ppermute | solution.py:38
  20.8 3.6 %up_rest.2 = (f32[512,256]{1,0:T(8,128)S(1)}, bf16[512,256]{1,0:T(8,128)(2,1)S(1)}, f32[512,256]{1,0:T(8,128)S(1)}) custom-call(bf16[1,2,2048,2048]{3,2,1,0:T(8,128)(2,1)S(1)} %bitcast.1, bf16[2,2048,256]{2,1,0:T(8,128)(2,1)S(1)} %get-tuple-element.42.refs_1_, bf16[512,256]{1,0:T(8,128)(2,1)S(1)} %collective-permute-done.4.refs_2_.refs_3_, ...), custom_call_target="tpu_custom_call" | custom-call | flops 20999999488 | bytes 1048576 | tf_op jit(solution)/shard_map/up_rest/pallas_call | solution.py:67
  24.4 1.7 %collective-permute-done.6.refs_0_ = bf16[512,256]{1,0:T(8,128)(2,1)S(1)} collective-permute-done((bf16[512,256]{1,0:T(8,128)(2,1)S(1)}, bf16[512,256]{1,0:T(8,128)(2,1)S(1)}, u32[]{:S(2)}, u32[]{:S(2)}) %collective-permute-start.6) | collective-permute-done | bytes 262176 | tf_op jit(solution)/shard_map/ppermute | solution.py:38
  26.2 1.8 %collective-permute-start.8 = (bf16[512,256]{1,0:T(8,128)(2,1)S(1)}, bf16[512,256]{1,0:T(8,128)(2,1)S(1)}, u32[]{:S(2)}, u32[]{:S(2)}) collective-permute-start(bf16[512,256]{1,0:T(8,128)(2,1)S(1)} %hop.2.refs_5_), channel_id=1, source_target_pairs={{0,8},{4,12},{8,0},{12,4},{1,9},{5,13},{9,1},{13,5},{2,10},{6,14},... | collective-permute-start | bytes 786440 | tf_op jit(solution)/shard_map/ppermute | solution.py:38
  28.0 6.5 %collective-permute-done.9.refs_2_ = bf16[512,256]{1,0:T(8,128)(2,1)S(1)} collective-permute-done((bf16[512,256]{1,0:T(8,128)(2,1)S(1)}, bf16[512,256]{1,0:T(8,128)(2,1)S(1)}, u32[]{:S(2)}, u32[]{:S(2)}) %collective-permute-start.9) | collective-permute-done | bytes 262176 | tf_op jit(solution)/shard_map/ppermute | solution.py:38
  34.5 1.5 %down_sibling.2 = (bf16[2,2048,256]{2,1,0:T(8,128)(2,1)S(1)}, f32[512,256]{1,0:T(8,128)S(1)}) custom-call(bf16[1,2,2048,2048]{3,2,1,0:T(8,128)(2,1)S(1)} %bitcast.1, bf16[512,256]{1,0:T(8,128)(2,1)S(1)} %ready_down.1.refs_1_, bf16[512,256]{1,0:T(8,128)(2,1)S(1)} %collective-permute-done.9.refs_2_, ...), custom_call_target="tpu_custom_call" | custom-call | flops 20999999488 | bytes 1048576 | tf_op jit(solution)/shard_map/down_sibling/pallas_call | solution.py:67
  36.1 1.2 %down_far.2.refs_0_ = f32[512,256]{1,0:T(8,128)S(1)} custom-call(bf16[1,2,2048,2048]{3,2,1,0:T(8,128)(2,1)S(1)} %bitcast.1, bf16[2,2048,256]{2,1,0:T(8,128)(2,1)S(1)} %get-tuple-element.49.refs_1_), custom_call_target="tpu_custom_call" | custom-call | flops 20999999488 | bytes 1048576 | tf_op jit(solution)/shard_map/down_far/pallas_call | solution.py:67
  42.7 3.8 %collective-permute-done.7.refs_0_ = bf16[512,256]{1,0:T(8,128)(2,1)S(1)} collective-permute-done((bf16[512,256]{1,0:T(8,128)(2,1)S(1)}, bf16[512,256]{1,0:T(8,128)(2,1)S(1)}, u32[]{:S(2)}, u32[]{:S(2)}) %collective-permute-start.7) | collective-permute-done | bytes 262176 | tf_op jit(solution)/shard_map/ppermute | solution.py:38
  46.7 1.6 %collective-permute-start.14 = (bf16[512,256]{1,0:T(8,128)(2,1)S(1)}, bf16[512,256]{1,0:T(8,128)(2,1)S(1)}, u32[]{:S(2)}, u32[]{:S(2)}) collective-permute-start(bf16[512,256]{1,0:T(8,128)(2,1)S(1)} %get-tuple-element.53), channel_id=1, source_target_pairs={{0,16},{16,0},{1,17},{17,1},{2,18},{18,2},{3,19},{19,3},{4,20},{20... | collective-permute-start | bytes 786440 | tf_op jit(solution)/shard_map/ppermute | solution.py:313
  48.5 6.5 %collective-permute-done.14.refs_0_.refs_1_ = bf16[512,256]{1,0:T(8,128)(2,1)S(1)} collective-permute-done((bf16[512,256]{1,0:T(8,128)(2,1)S(1)}, bf16[512,256]{1,0:T(8,128)(2,1)S(1)}, u32[]{:S(2)}, u32[]{:S(2)}) %collective-permute-start.14) | collective-permute-done | bytes 262176 | tf_op jit(solution)/shard_map/ppermute | solution.py:313
  55.9 1.8 %collective-permute-start.19 = (bf16[512,256]{1,0:T(8,128)(2,1)S(1)}, bf16[512,256]{1,0:T(8,128)(2,1)S(1)}, u32[]{:S(2)}, u32[]{:S(2)}) collective-permute-start(bf16[512,256]{1,0:T(8,128)(2,1)S(1)} %get-tuple-element.62.refs_1_), channel_id=1, source_target_pairs={{0,8},{4,12},{8,0},{12,4},{1,9},{5,13},{9,1},{13,5},{2,10},{6,14},... | collective-permute-start | bytes 786440 | tf_op jit(solution)/shard_map/ppermute | solution.py:38
  57.7 2.2 %collective-permute-start.20 = (bf16[512,256]{1,0:T(8,128)(2,1)S(1)}, bf16[512,256]{1,0:T(8,128)(2,1)S(1)}, u32[]{:S(2)}, u32[]{:S(2)}) collective-permute-start(bf16[512,256]{1,0:T(8,128)(2,1)S(1)} %get-tuple-element.62.refs_1_), channel_id=1, source_target_pairs={{0,4},{4,0},{8,12},{12,8},{1,5},{5,1},{9,13},{13,9},{2,6},{6,2},{1... | collective-permute-start | bytes 786440 | tf_op jit(solution)/shard_map/ppermute | solution.py:38
  59.8 3.0 %collective-permute-done.16.refs_0_ = bf16[512,256]{1,0:T(8,128)(2,1)S(1)} collective-permute-done((bf16[512,256]{1,0:T(8,128)(2,1)S(1)}, bf16[512,256]{1,0:T(8,128)(2,1)S(1)}, u32[]{:S(2)}, u32[]{:S(2)}) %collective-permute-start.16) | collective-permute-done | bytes 262176 | tf_op jit(solution)/shard_map/ppermute | solution.py:53
  64.5 1.6 %up_first.3 = (bf16[2,2048,256]{2,1,0:T(8,128)(2,1)S(1)}, bf16[512,256]{1,0:T(8,128)(2,1)S(1)}) custom-call(bf16[1,2,2048,2048]{3,2,1,0:T(8,128)(2,1)S(1)} %bitcast.1, bf16[512,256]{1,0:T(8,128)(2,1)S(1)} %get-tuple-element.58.refs_1_, bf16[512,256]{1,0:T(8,128)(2,1)S(1)} %collective-permute-done.15.refs_2_, bf16[256,256]{1,0:T(8,128)(2,1)S(1)} %get-tuple-element.59.refs_3_, ...), custom_call_target="tpu_custom_call" | custom-call | bytes 1 | tf_op jit(solution)/shard_map/up_first/pallas_call | solution.py:67
  66.2 5.0 %collective-permute-done.19.refs_2_.refs_3_ = bf16[512,256]{1,0:T(8,128)(2,1)S(1)} collective-permute-done((bf16[512,256]{1,0:T(8,128)(2,1)S(1)}, bf16[512,256]{1,0:T(8,128)(2,1)S(1)}, u32[]{:S(2)}, u32[]{:S(2)}) %collective-permute-start.19) | collective-permute-done | bytes 262176 | tf_op jit(solution)/shard_map/ppermute | solution.py:38
  71.3 3.6 %up_rest.3 = (f32[512,256]{1,0:T(8,128)S(1)}, bf16[512,256]{1,0:T(8,128)(2,1)S(1)}, f32[512,256]{1,0:T(8,128)S(1)}) custom-call(bf16[1,2,2048,2048]{3,2,1,0:T(8,128)(2,1)S(1)} %bitcast.1, bf16[2,2048,256]{2,1,0:T(8,128)(2,1)S(1)} %get-tuple-element.61.refs_1_, bf16[512,256]{1,0:T(8,128)(2,1)S(1)} %collective-permute-done.19.refs_2_.refs_3_, ...), custom_call_target="tpu_custom_call" | custom-call | flops 20999999488 | bytes 1048576 | tf_op jit(solution)/shard_map/up_rest/pallas_call | solution.py:67
  74.9 2.0 %collective-permute-done.21.refs_0_ = bf16[512,256]{1,0:T(8,128)(2,1)S(1)} collective-permute-done((bf16[512,256]{1,0:T(8,128)(2,1)S(1)}, bf16[512,256]{1,0:T(8,128)(2,1)S(1)}, u32[]{:S(2)}, u32[]{:S(2)}) %collective-permute-start.21) | collective-permute-done | bytes 262176 | tf_op jit(solution)/shard_map/ppermute | solution.py:38
  77.0 1.4 %collective-permute-start.23 = (bf16[512,256]{1,0:T(8,128)(2,1)S(1)}, bf16[512,256]{1,0:T(8,128)(2,1)S(1)}, u32[]{:S(2)}, u32[]{:S(2)}) collective-permute-start(bf16[512,256]{1,0:T(8,128)(2,1)S(1)} %hop.3.refs_5_), channel_id=1, source_target_pairs={{0,8},{4,12},{8,0},{12,4},{1,9},{5,13},{9,1},{13,5},{2,10},{6,14},... | collective-permute-start | bytes 786440 | tf_op jit(solution)/shard_map/ppermute | solution.py:38
  78.4 6.7 %collective-permute-done.24.refs_2_ = bf16[512,256]{1,0:T(8,128)(2,1)S(1)} collective-permute-done((bf16[512,256]{1,0:T(8,128)(2,1)S(1)}, bf16[512,256]{1,0:T(8,128)(2,1)S(1)}, u32[]{:S(2)}, u32[]{:S(2)}) %collective-permute-start.24) | collective-permute-done | bytes 262176 | tf_op jit(solution)/shard_map/ppermute | solution.py:38
  85.1 1.5 %down_sibling.3 = (bf16[2,2048,256]{2,1,0:T(8,128)(2,1)S(1)}, f32[512,256]{1,0:T(8,128)S(1)}) custom-call(bf16[1,2,2048,2048]{3,2,1,0:T(8,128)(2,1)S(1)} %bitcast.1, bf16[512,256]{1,0:T(8,128)(2,1)S(1)} %get-tuple-element.62.refs_1_, bf16[512,256]{1,0:T(8,128)(2,1)S(1)} %collective-permute-done.24.refs_2_, ...), custom_call_target="tpu_custom_call" | custom-call | flops 20999999488 | bytes 1048576 | tf_op jit(solution)/shard_map/down_sibling/pallas_call | solution.py:67
  86.8 1.2 %down_far.3.refs_0_ = f32[512,256]{1,0:T(8,128)S(1)} custom-call(bf16[1,2,2048,2048]{3,2,1,0:T(8,128)(2,1)S(1)} %bitcast.1, bf16[2,2048,256]{2,1,0:T(8,128)(2,1)S(1)} %get-tuple-element.69.refs_1_), custom_call_target="tpu_custom_call" | custom-call | flops 20999999488 | bytes 1048576 | tf_op jit(solution)/shard_map/down_far/pallas_call | solution.py:67
  88.7 1.6 %collective-permute-start.26 = (bf16[512,256]{1,0:T(8,128)(2,1)S(1)}, bf16[512,256]{1,0:T(8,128)(2,1)S(1)}, u32[]{:S(2)}, u32[]{:S(2)}) collective-permute-start(bf16[512,256]{1,0:T(8,128)(2,1)S(1)} %far_sum.3.refs_2_), channel_id=1, source_target_pairs={{0,2},{1,3},{2,0},{3,1},{4,6},{5,7},{6,4},{7,5},{8,10},{9,11},{10,... | collective-permute-start | bytes 786440 | tf_op jit(solution)/shard_map/ppermute | solution.py:53
  93.1 1.2 %down_own.3.refs_4_ = f32[512,256]{1,0:T(8,128)S(1)} custom-call(bf16[1,2,2048,2048]{3,2,1,0:T(8,128)(2,1)S(1)} %bitcast.1, bf16[2,2048,256]{2,1,0:T(8,128)(2,1)S(1)} %get-tuple-element.69.refs_1_, bf16[256,256]{1,0:T(8,128)(2,1)S(1)} %collective-permute-done.27.refs_2_, bf16[256,256]{1,0:T(8,128)(2,1)S(1)} %collective-permute-done.28.refs_3_), custom_call_target="tpu_custom_call" | custom-call | bytes 1 | tf_op jit(solution)/shard_map/down_own/pallas_call | solution.py:67
  94.3 3.2 %collective-permute-done.22.refs_0_ = bf16[512,256]{1,0:T(8,128)(2,1)S(1)} collective-permute-done((bf16[512,256]{1,0:T(8,128)(2,1)S(1)}, bf16[512,256]{1,0:T(8,128)(2,1)S(1)}, u32[]{:S(2)}, u32[]{:S(2)}) %collective-permute-start.22) | collective-permute-done | bytes 262176 | tf_op jit(solution)/shard_map/ppermute | solution.py:38
  97.7 1.7 %collective-permute-start.29 = (bf16[512,256]{1,0:T(8,128)(2,1)S(1)}, bf16[512,256]{1,0:T(8,128)(2,1)S(1)}, u32[]{:S(2)}, u32[]{:S(2)}) collective-permute-start(bf16[512,256]{1,0:T(8,128)(2,1)S(1)} %get-tuple-element.73), channel_id=1, source_target_pairs={{0,16},{16,0},{1,17},{17,1},{2,18},{18,2},{3,19},{19,3},{4,20},{20... | collective-permute-start | bytes 786440 | tf_op jit(solution)/shard_map/ppermute | solution.py:313
  99.4 6.7 %collective-permute-done.29.refs_0_.refs_1_ = bf16[512,256]{1,0:T(8,128)(2,1)S(1)} collective-permute-done((bf16[512,256]{1,0:T(8,128)(2,1)S(1)}, bf16[512,256]{1,0:T(8,128)(2,1)S(1)}, u32[]{:S(2)}, u32[]{:S(2)}) %collective-permute-start.29) | collective-permute-done | bytes 262176 | tf_op jit(solution)/shard_map/ppermute | solution.py:313
  (82 shorter events, 16.8 us)
Async XLA Ops:
  1.7 11.0 %slice-start = ((s8[16777216]{0:T(1024)(128)(4,1)}), s8[4194304]{0:T(1024)(128)(4,1)S(1)}, s32[]{:S(2)}) async-start(s8[16777216]{0:T(1024)(128)(4,1)} %bitcast), calls=%async_computation | async-start | bytes 8388608
  1.7 11.0 %slice-start.1 = ((s8[16777216]{0:T(1024)(128)(4,1)}), s8[4194304]{0:T(1024)(128)(4,1)S(1)}, s32[]{:S(2)}) async-start(s8[16777216]{0:T(1024)(128)(4,1)} %bitcast), calls=%async_computation.1 | async-start | bytes 8388608
  1.7 9.3 %collective-permute-start.1 = (bf16[512,256]{1,0:T(8,128)(2,1)S(1)}, bf16[512,256]{1,0:T(8,128)(2,1)S(1)}, u32[]{:S(2)}, u32[]{:S(2)}) collective-permute-start(bf16[512,256]{1,0:T(8,128)(2,1)S(1)} %ready_up.1.refs_1_), channel_id=1, source_target_pairs={{0,2},{1,3},{2,0},{3,1},{4,6},{5,7},{6,4},{7,5},{8,10},{9,11},{10,... | collective-permute-start | bytes 786440 | tf_op jit(solution)/shard_map/ppermute | solution.py:53
  4.7 6.9 %collective-permute-start = (bf16[512,256]{1,0:T(8,128)(2,1)S(1)}, bf16[512,256]{1,0:T(8,128)(2,1)S(1)}, u32[]{:S(2)}, u32[]{:S(2)}) collective-permute-start(bf16[512,256]{1,0:T(8,128)(2,1)S(1)} %ready_up.1.refs_1_), channel_id=1, source_target_pairs={{0,1},{1,0},{2,3},{3,2},{4,5},{5,4},{6,7},{7,6},{8,9},{9,8},{10,11... | collective-permute-start | bytes 786440 | tf_op jit(solution)/shard_map/ppermute | solution.py:53
  4.8 15.4 %collective-permute-start.4 = (bf16[512,256]{1,0:T(8,128)(2,1)S(1)}, bf16[512,256]{1,0:T(8,128)(2,1)S(1)}, u32[]{:S(2)}, u32[]{:S(2)}) collective-permute-start(bf16[512,256]{1,0:T(8,128)(2,1)S(1)} %ready_down.1.refs_1_), channel_id=1, source_target_pairs={{0,8},{4,12},{8,0},{12,4},{1,9},{5,13},{9,1},{13,5},{2,10},{6,14},... | collective-permute-start | bytes 786440 | tf_op jit(solution)/shard_map/ppermute | solution.py:38
  7.4 13.4 %collective-permute-start.5 = (bf16[512,256]{1,0:T(8,128)(2,1)S(1)}, bf16[512,256]{1,0:T(8,128)(2,1)S(1)}, u32[]{:S(2)}, u32[]{:S(2)}) collective-permute-start(bf16[512,256]{1,0:T(8,128)(2,1)S(1)} %ready_down.1.refs_1_), channel_id=1, source_target_pairs={{0,4},{4,0},{8,12},{12,8},{1,5},{5,1},{9,13},{13,9},{2,6},{6,2},{1... | collective-permute-start | bytes 786440 | tf_op jit(solution)/shard_map/ppermute | solution.py:38
  11.1 1.4 %collective-permute-start.2 = (bf16[256,256]{1,0:T(8,128)(2,1)S(1)}, bf16[256,256]{1,0:T(8,128)(2,1)S(1)}, u32[]{:S(2)}, u32[]{:S(2)}) collective-permute-start(bf16[256,256]{1,0:T(8,128)(2,1)S(1)} %get-tuple-element.40.refs_3_), channel_id=1, source_target_pairs={{0,1},{1,0},{2,3},{3,2},{4,5},{5,4},{6,7},{7,6},{8,9},{9,8},{10,11... | collective-permute-start | bytes 393224 | tf_op jit(solution)/shard_map/ppermute | solution.py:53
  11.1 1.5 %collective-permute-start.3 = (bf16[256,256]{1,0:T(8,128)(2,1)S(1)}, bf16[256,256]{1,0:T(8,128)(2,1)S(1)}, u32[]{:S(2)}, u32[]{:S(2)}) collective-permute-start(bf16[256,256]{1,0:T(8,128)(2,1)S(1)} %get-tuple-element.41.refs_4_), channel_id=1, source_target_pairs={{0,1},{1,0},{2,3},{3,2},{4,5},{5,4},{6,7},{7,6},{8,9},{9,8},{10,11... | collective-permute-start | bytes 393224 | tf_op jit(solution)/shard_map/ppermute | solution.py:53
  14.3 11.8 %collective-permute-start.6 = (bf16[512,256]{1,0:T(8,128)(2,1)S(1)}, bf16[512,256]{1,0:T(8,128)(2,1)S(1)}, u32[]{:S(2)}, u32[]{:S(2)}) collective-permute-start(bf16[512,256]{1,0:T(8,128)(2,1)S(1)} %get-tuple-element.44), channel_id=1, source_target_pairs={{0,4},{4,0},{8,12},{12,8},{1,5},{5,1},{9,13},{13,9},{2,6},{6,2},{1... | collective-permute-start | bytes 786440 | tf_op jit(solution)/shard_map/ppermute | solution.py:38
  20.2 14.3 %collective-permute-start.9 = (bf16[512,256]{1,0:T(8,128)(2,1)S(1)}, bf16[512,256]{1,0:T(8,128)(2,1)S(1)}, u32[]{:S(2)}, u32[]{:S(2)}) collective-permute-start(bf16[512,256]{1,0:T(8,128)(2,1)S(1)} %collective-permute-done.4.refs_2_.refs_3_), channel_id=1, source_target_pairs={{0,4},{4,0},{8,12},{12,8},{1,5},{5,1},{9,13},{13,9},{2,6},{6,2},{1... | collective-permute-start | bytes 786440 | tf_op jit(solution)/shard_map/ppermute | solution.py:38
  26.2 20.3 %collective-permute-start.8 = (bf16[512,256]{1,0:T(8,128)(2,1)S(1)}, bf16[512,256]{1,0:T(8,128)(2,1)S(1)}, u32[]{:S(2)}, u32[]{:S(2)}) collective-permute-start(bf16[512,256]{1,0:T(8,128)(2,1)S(1)} %hop.2.refs_5_), channel_id=1, source_target_pairs={{0,8},{4,12},{8,0},{12,4},{1,9},{5,13},{9,1},{13,5},{2,10},{6,14},... | collective-permute-start | bytes 786440 | tf_op jit(solution)/shard_map/ppermute | solution.py:38
  36.0 2.0 %collective-permute-start.10 = (f32[512,256]{1,0:T(8,128)S(1)}, f32[512,256]{1,0:T(8,128)S(1)}, u32[]{:S(2)}, u32[]{:S(2)}) collective-permute-start(f32[512,256]{1,0:T(8,128)S(1)} %get-tuple-element.50), channel_id=1, source_target_pairs={{0,1},{1,0},{2,3},{3,2},{4,5},{5,4},{6,7},{7,6},{8,9},{9,8},{10,11... | collective-permute-start | bytes 1572872 | tf_op jit(solution)/shard_map/ppermute | solution.py:53
  37.3 9.2 %collective-permute-start.7 = (bf16[512,256]{1,0:T(8,128)(2,1)S(1)}, bf16[512,256]{1,0:T(8,128)(2,1)S(1)}, u32[]{:S(2)}, u32[]{:S(2)}) collective-permute-start(bf16[512,256]{1,0:T(8,128)(2,1)S(1)} %get-tuple-element.46.refs_2_), channel_id=1, source_target_pairs={{0,4},{4,0},{8,12},{12,8},{1,5},{5,1},{9,13},{13,9},{2,6},{6,2},{1... | collective-permute-start | bytes 786440 | tf_op jit(solution)/shard_map/ppermute | solution.py:38
  38.0 8.5 %collective-permute-start.11 = (bf16[512,256]{1,0:T(8,128)(2,1)S(1)}, bf16[512,256]{1,0:T(8,128)(2,1)S(1)}, u32[]{:S(2)}, u32[]{:S(2)}) collective-permute-start(bf16[512,256]{1,0:T(8,128)(2,1)S(1)} %far_sum.2.refs_2_), channel_id=1, source_target_pairs={{0,2},{1,3},{2,0},{3,1},{4,6},{5,7},{6,4},{7,5},{8,10},{9,11},{10,... | collective-permute-start | bytes 786440 | tf_op jit(solution)/shard_map/ppermute | solution.py:53
  39.8 1.4 %collective-permute-start.12 = (bf16[256,256]{1,0:T(8,128)(2,1)S(1)}, bf16[256,256]{1,0:T(8,128)(2,1)S(1)}, u32[]{:S(2)}, u32[]{:S(2)}) collective-permute-start(bf16[256,256]{1,0:T(8,128)(2,1)S(1)} %get-tuple-element.51), channel_id=1, source_target_pairs={{0,1},{1,0},{2,3},{3,2},{4,5},{5,4},{6,7},{7,6},{8,9},{9,8},{10,11... | collective-permute-start | bytes 393224 | tf_op jit(solution)/shard_map/ppermute | solution.py:53
  39.9 1.5 %collective-permute-start.13 = (bf16[256,256]{1,0:T(8,128)(2,1)S(1)}, bf16[256,256]{1,0:T(8,128)(2,1)S(1)}, u32[]{:S(2)}, u32[]{:S(2)}) collective-permute-start(bf16[256,256]{1,0:T(8,128)(2,1)S(1)} %get-tuple-element.52), channel_id=1, source_target_pairs={{0,1},{1,0},{2,3},{3,2},{4,5},{5,4},{6,7},{7,6},{8,9},{9,8},{10,11... | collective-permute-start | bytes 393224 | tf_op jit(solution)/shard_map/ppermute | solution.py:53
  46.7 8.3 %collective-permute-start.14 = (bf16[512,256]{1,0:T(8,128)(2,1)S(1)}, bf16[512,256]{1,0:T(8,128)(2,1)S(1)}, u32[]{:S(2)}, u32[]{:S(2)}) collective-permute-start(bf16[512,256]{1,0:T(8,128)(2,1)S(1)} %get-tuple-element.53), channel_id=1, source_target_pairs={{0,16},{16,0},{1,17},{17,1},{2,18},{18,2},{3,19},{19,3},{4,20},{20... | collective-permute-start | bytes 786440 | tf_op jit(solution)/shard_map/ppermute | solution.py:313
  55.4 7.5 %collective-permute-start.16 = (bf16[512,256]{1,0:T(8,128)(2,1)S(1)}, bf16[512,256]{1,0:T(8,128)(2,1)S(1)}, u32[]{:S(2)}, u32[]{:S(2)}) collective-permute-start(bf16[512,256]{1,0:T(8,128)(2,1)S(1)} %get-tuple-element.58.refs_1_), channel_id=1, source_target_pairs={{0,2},{1,3},{2,0},{3,1},{4,6},{5,7},{6,4},{7,5},{8,10},{9,11},{10,... | collective-permute-start | bytes 786440 | tf_op jit(solution)/shard_map/ppermute | solution.py:53
  55.9 7.6 %collective-permute-start.15 = (bf16[512,256]{1,0:T(8,128)(2,1)S(1)}, bf16[512,256]{1,0:T(8,128)(2,1)S(1)}, u32[]{:S(2)}, u32[]{:S(2)}) collective-permute-start(bf16[512,256]{1,0:T(8,128)(2,1)S(1)} %get-tuple-element.58.refs_1_), channel_id=1, source_target_pairs={{0,1},{1,0},{2,3},{3,2},{4,5},{5,4},{6,7},{7,6},{8,9},{9,8},{10,11... | collective-permute-start | bytes 786440 | tf_op jit(solution)/shard_map/ppermute | solution.py:53
  55.9 15.3 %collective-permute-start.19 = (bf16[512,256]{1,0:T(8,128)(2,1)S(1)}, bf16[512,256]{1,0:T(8,128)(2,1)S(1)}, u32[]{:S(2)}, u32[]{:S(2)}) collective-permute-start(bf16[512,256]{1,0:T(8,128)(2,1)S(1)} %get-tuple-element.62.refs_1_), channel_id=1, source_target_pairs={{0,8},{4,12},{8,0},{12,4},{1,9},{5,13},{9,1},{13,5},{2,10},{6,14},... | collective-permute-start | bytes 786440 | tf_op jit(solution)/shard_map/ppermute | solution.py:38
  57.7 13.6 %collective-permute-start.20 = (bf16[512,256]{1,0:T(8,128)(2,1)S(1)}, bf16[512,256]{1,0:T(8,128)(2,1)S(1)}, u32[]{:S(2)}, u32[]{:S(2)}) collective-permute-start(bf16[512,256]{1,0:T(8,128)(2,1)S(1)} %get-tuple-element.62.refs_1_), channel_id=1, source_target_pairs={{0,4},{4,0},{8,12},{12,8},{1,5},{5,1},{9,13},{13,9},{2,6},{6,2},{1... | collective-permute-start | bytes 786440 | tf_op jit(solution)/shard_map/ppermute | solution.py:38
  62.9 1.4 %collective-permute-start.17 = (bf16[256,256]{1,0:T(8,128)(2,1)S(1)}, bf16[256,256]{1,0:T(8,128)(2,1)S(1)}, u32[]{:S(2)}, u32[]{:S(2)}) collective-permute-start(bf16[256,256]{1,0:T(8,128)(2,1)S(1)} %get-tuple-element.59.refs_3_), channel_id=1, source_target_pairs={{0,1},{1,0},{2,3},{3,2},{4,5},{5,4},{6,7},{7,6},{8,9},{9,8},{10,11... | collective-permute-start | bytes 393224 | tf_op jit(solution)/shard_map/ppermute | solution.py:53
  62.9 1.5 %collective-permute-start.18 = (bf16[256,256]{1,0:T(8,128)(2,1)S(1)}, bf16[256,256]{1,0:T(8,128)(2,1)S(1)}, u32[]{:S(2)}, u32[]{:S(2)}) collective-permute-start(bf16[256,256]{1,0:T(8,128)(2,1)S(1)} %get-tuple-element.60.refs_4_), channel_id=1, source_target_pairs={{0,1},{1,0},{2,3},{3,2},{4,5},{5,4},{6,7},{7,6},{8,9},{9,8},{10,11... | collective-permute-start | bytes 393224 | tf_op jit(solution)/shard_map/ppermute | solution.py:53
  66.1 10.8 %collective-permute-start.21 = (bf16[512,256]{1,0:T(8,128)(2,1)S(1)}, bf16[512,256]{1,0:T(8,128)(2,1)S(1)}, u32[]{:S(2)}, u32[]{:S(2)}) collective-permute-start(bf16[512,256]{1,0:T(8,128)(2,1)S(1)} %get-tuple-element.64), channel_id=1, source_target_pairs={{0,4},{4,0},{8,12},{12,8},{1,5},{5,1},{9,13},{13,9},{2,6},{6,2},{1... | collective-permute-start | bytes 786440 | tf_op jit(solution)/shard_map/ppermute | solution.py:38
  71.2 13.9 %collective-permute-start.24 = (bf16[512,256]{1,0:T(8,128)(2,1)S(1)}, bf16[512,256]{1,0:T(8,128)(2,1)S(1)}, u32[]{:S(2)}, u32[]{:S(2)}) collective-permute-start(bf16[512,256]{1,0:T(8,128)(2,1)S(1)} %collective-permute-done.19.refs_2_.refs_3_), channel_id=1, source_target_pairs={{0,4},{4,0},{8,12},{12,8},{1,5},{5,1},{9,13},{13,9},{2,6},{6,2},{1... | collective-permute-start | bytes 786440 | tf_op jit(solution)/shard_map/ppermute | solution.py:38
  77.0 20.5 %collective-permute-start.23 = (bf16[512,256]{1,0:T(8,128)(2,1)S(1)}, bf16[512,256]{1,0:T(8,128)(2,1)S(1)}, u32[]{:S(2)}, u32[]{:S(2)}) collective-permute-start(bf16[512,256]{1,0:T(8,128)(2,1)S(1)} %hop.3.refs_5_), channel_id=1, source_target_pairs={{0,8},{4,12},{8,0},{12,4},{1,9},{5,13},{9,1},{13,5},{2,10},{6,14},... | collective-permute-start | bytes 786440 | tf_op jit(solution)/shard_map/ppermute | solution.py:38
  86.6 2.0 %collective-permute-start.25 = (f32[512,256]{1,0:T(8,128)S(1)}, f32[512,256]{1,0:T(8,128)S(1)}, u32[]{:S(2)}, u32[]{:S(2)}) collective-permute-start(f32[512,256]{1,0:T(8,128)S(1)} %get-tuple-element.70), channel_id=1, source_target_pairs={{0,1},{1,0},{2,3},{3,2},{4,5},{5,4},{6,7},{7,6},{8,9},{9,8},{10,11... | collective-permute-start | bytes 1572872 | tf_op jit(solution)/shard_map/ppermute | solution.py:53
  88.1 9.5 %collective-permute-start.22 = (bf16[512,256]{1,0:T(8,128)(2,1)S(1)}, bf16[512,256]{1,0:T(8,128)(2,1)S(1)}, u32[]{:S(2)}, u32[]{:S(2)}) collective-permute-start(bf16[512,256]{1,0:T(8,128)(2,1)S(1)} %get-tuple-element.66.refs_2_), channel_id=1, source_target_pairs={{0,4},{4,0},{8,12},{12,8},{1,5},{5,1},{9,13},{13,9},{2,6},{6,2},{1... | collective-permute-start | bytes 786440 | tf_op jit(solution)/shard_map/ppermute | solution.py:38
  88.7 8.9 %collective-permute-start.26 = (bf16[512,256]{1,0:T(8,128)(2,1)S(1)}, bf16[512,256]{1,0:T(8,128)(2,1)S(1)}, u32[]{:S(2)}, u32[]{:S(2)}) collective-permute-start(bf16[512,256]{1,0:T(8,128)(2,1)S(1)} %far_sum.3.refs_2_), channel_id=1, source_target_pairs={{0,2},{1,3},{2,0},{3,1},{4,6},{5,7},{6,4},{7,5},{8,10},{9,11},{10,... | collective-permute-start | bytes 786440 | tf_op jit(solution)/shard_map/ppermute | solution.py:53
  91.5 1.4 %collective-permute-start.27 = (bf16[256,256]{1,0:T(8,128)(2,1)S(1)}, bf16[256,256]{1,0:T(8,128)(2,1)S(1)}, u32[]{:S(2)}, u32[]{:S(2)}) collective-permute-start(bf16[256,256]{1,0:T(8,128)(2,1)S(1)} %get-tuple-element.71), channel_id=1, source_target_pairs={{0,1},{1,0},{2,3},{3,2},{4,5},{5,4},{6,7},{7,6},{8,9},{9,8},{10,11... | collective-permute-start | bytes 393224 | tf_op jit(solution)/shard_map/ppermute | solution.py:53
  91.6 1.5 %collective-permute-start.28 = (bf16[256,256]{1,0:T(8,128)(2,1)S(1)}, bf16[256,256]{1,0:T(8,128)(2,1)S(1)}, u32[]{:S(2)}, u32[]{:S(2)}) collective-permute-start(bf16[256,256]{1,0:T(8,128)(2,1)S(1)} %get-tuple-element.72), channel_id=1, source_target_pairs={{0,1},{1,0},{2,3},{3,2},{4,5},{5,4},{6,7},{7,6},{8,9},{9,8},{10,11... | collective-permute-start | bytes 393224 | tf_op jit(solution)/shard_map/ppermute | solution.py:53
  97.7 8.3 %collective-permute-start.29 = (bf16[512,256]{1,0:T(8,128)(2,1)S(1)}, bf16[512,256]{1,0:T(8,128)(2,1)S(1)}, u32[]{:S(2)}, u32[]{:S(2)}) collective-permute-start(bf16[512,256]{1,0:T(8,128)(2,1)S(1)} %get-tuple-element.73), channel_id=1, source_target_pairs={{0,16},{16,0},{1,17},{17,1},{2,18},{18,2},{3,19},{19,3},{4,20},{20... | collective-permute-start | bytes 786440 | tf_op jit(solution)/shard_map/ppermute | solution.py:313
  (12 other events, 77.3 us)

commit v5 on v4

--- a/solution.py
+++ b/solution.py
@@ -171,8 +171,8 @@
     out_ref[...] = up_dot(w_ref, pair_ref, rows_at(row_block(1, size), strip)).astype(BF16)
 
 
-def up_rest_kernel(size, strip, w_ref, pair_ref, *out_refs):
-    for s, ref in zip(range(2, size + 1), out_refs):
+def up_rest_kernel(size, strip, first, w_ref, pair_ref, *out_refs):
+    for s, ref in zip(range(first, size + 1), out_refs):
         ref[...] = up_dot(w_ref, pair_ref, rows_at(row_block(s, size), strip)).astype(ref.dtype)
 
 
@@ -270,11 +270,12 @@
             blocks_down = [down_low, row_swap(behind(across, travelling), 1), across, beside]
         kinds = [full, low, full] if size == 4 else [full] * (size - 1)
         own_up = call(
-            functools.partial(up_rest_kernel, size, strip), kinds, "up_rest", [w, pair_up], ready,
+            functools.partial(up_rest_kernel, size, strip, 2), kinds[:1] if size == 4 else kinds, "up_second", [w, pair_up], ready,
         )
         if size == 4:
-            (passed,) = call(
-                hop_kernel, [low], "hop", [row_swap(travelling, 1), own_up[0]], [own_up[1]]
+            (passed,) = call(hop_kernel, [low], "hop", [row_swap(travelling, 1), own_up[0]])
+            own_up += call(
+                functools.partial(up_rest_kernel, size, strip, 3), kinds[1:], "up_rest", [w, pair_up], [passed]
             )
             arrived = [row_swap(behind(own_up[1], passed), 1), row_swap(passed, 2)]
             before_down = [passed]

time: 107 us -> 101 us (0.944)
  waiting for transfers between devices: 56.5 us -> 46.2 us
  starting transfers between devices: 25.5 us -> 28.8 us
    ppermute x12, waiting for transfers between devices: 33.1 us -> 22.6 us  [row_swap(): lax.ppermute(x, 'row', [(r, r ^ bit) for r in range(lax.axis_size('row'))])]
    ppermute x12, starting transfers between devices: 14.1 us -> 17.4 us  [row_swap(): lax.ppermute(x, 'row', [(r, r ^ bit) for r in range(lax.axis_size('row'))])]
    ppermute x16, waiting for transfers between devices: 10.2 us -> 11.6 us  [col_swap(): lax.ppermute(x, 'col', [(c, c ^ bit) for c in range(lax.axis_size('col'))])]
    ppermute x2, waiting for transfers between devices: 13.2 us -> 12 us  [body(): from_above = from_below = lax.ppermute(passed_on, 'depth', [(0, 1), (1, 0)])]
    pallas_call x25 -> x27, Pallas kernels: 23.2 us -> 23.6 us  [call(): pl.pallas_call(ordered, in_specs=[WHOLE] * count + [UNREAD] * len(after),...]
  transfers between devices with their start and end apart: 30 -> 30, of which waited for: 23 -> 24; matrix products, arithmetic and copies ran while one was open for 0% -> 0% of each run, Pallas kernels for 20% -> 22%
where the time goes in v5:
time: 101 us
  waiting for transfers between devices  46.2 us (46%)
  starting transfers between devices  28.8 us (29%)
  Pallas kernels  23.6 us (23%)
  local copies, waits for them, and re-layouts  1.1 us (1%)
    pallas_call x27, Pallas kernels, call(): pl.pallas_call(ordered, in_specs=[WHOLE] * count + [UNREAD] * len(after),...  23.6 us
    ppermute x12, waiting for transfers between devices, row_swap(): lax.ppermute(x, 'row', [(r, r ^ bit) for r in range(lax.axis_size('row'))])  22.6 us
    ppermute x12, starting transfers between devices, row_swap(): lax.ppermute(x, 'row', [(r, r ^ bit) for r in range(lax.axis_size('row'))])  17.4 us
    ppermute x2, waiting for transfers between devices, body(): from_above = from_below = lax.ppermute(passed_on, 'depth', [(0, 1), (1, 0)])  12 us
    ppermute x16, waiting for transfers between devices, col_swap(): lax.ppermute(x, 'col', [(c, c ^ bit) for c in range(lax.axis_size('col'))])  11.6 us
    ppermute x16, starting transfers between devices, col_swap(): lax.ppermute(x, 'col', [(c, c ^ bit) for c in range(lax.axis_size('col'))])  8.23 us
    ppermute x2, starting transfers between devices, body(): from_above = from_below = lax.ppermute(passed_on, 'depth', [(0, 1), (1, 0)])  3.16 us
  transfers between devices with their start and end apart: 30, of which 24 were waited for; matrix products, arithmetic and copies ran while one was open for 0% of the time, Pallas kernels for 22%

profile of v5, /device:TPU:0, one launch (start us, length us, event | category | flops | bytes accessed | tf_op | source)
XLA Modules:
  0.0 100.7 jit_solution(3100799998852498457)
XLA Ops:
  1.7 3.0 %collective-permute-start.1 = (bf16[512,256]{1,0:T(8,128)(2,1)S(1)}, bf16[512,256]{1,0:T(8,128)(2,1)S(1)}, u32[]{:S(2)}, u32[]{:S(2)}) collective-permute-start(bf16[512,256]{1,0:T(8,128)(2,1)S(1)} %ready_up.1.refs_1_), channel_id=1, source_target_pairs={{0,2},{1,3},{2,0},{3,1},{4,6},{5,7},{6,4},{7,5},{8,10},{9,11},{10,... | collective-permute-start | bytes 786440 | tf_op jit(solution)/shard_map/ppermute | solution.py:53
  4.8 2.7 %collective-permute-start.5 = (bf16[512,256]{1,0:T(8,128)(2,1)S(1)}, bf16[512,256]{1,0:T(8,128)(2,1)S(1)}, u32[]{:S(2)}, u32[]{:S(2)}) collective-permute-start(bf16[512,256]{1,0:T(8,128)(2,1)S(1)} %ready_down.1.refs_1_), channel_id=1, source_target_pairs={{0,8},{4,12},{8,0},{12,4},{1,9},{5,13},{9,1},{13,5},{2,10},{6,14},... | collective-permute-start | bytes 786440 | tf_op jit(solution)/shard_map/ppermute | solution.py:38
  7.4 1.6 %collective-permute-start.6 = (bf16[512,256]{1,0:T(8,128)(2,1)S(1)}, bf16[512,256]{1,0:T(8,128)(2,1)S(1)}, u32[]{:S(2)}, u32[]{:S(2)}) collective-permute-start(bf16[512,256]{1,0:T(8,128)(2,1)S(1)} %ready_down.1.refs_1_), channel_id=1, source_target_pairs={{0,4},{4,0},{8,12},{12,8},{1,5},{5,1},{9,13},{13,9},{2,6},{6,2},{1... | collective-permute-start | bytes 786440 | tf_op jit(solution)/shard_map/ppermute | solution.py:38
  9.0 2.0 %collective-permute-done.1.refs_0_ = bf16[512,256]{1,0:T(8,128)(2,1)S(1)} collective-permute-done((bf16[512,256]{1,0:T(8,128)(2,1)S(1)}, bf16[512,256]{1,0:T(8,128)(2,1)S(1)}, u32[]{:S(2)}, u32[]{:S(2)}) %collective-permute-start.1) | collective-permute-done | bytes 262176 | tf_op jit(solution)/shard_map/ppermute | solution.py:53
  12.7 1.6 %up_first.2 = (bf16[2,2048,256]{2,1,0:T(8,128)(2,1)S(1)}, bf16[512,256]{1,0:T(8,128)(2,1)S(1)}) custom-call(bf16[1,2,2048,2048]{3,2,1,0:T(8,128)(2,1)S(1)} %bitcast.1, bf16[512,256]{1,0:T(8,128)(2,1)S(1)} %ready_up.1.refs_1_, bf16[512,256]{1,0:T(8,128)(2,1)S(1)} %collective-permute-done.refs_2_, bf16[256,256]{1,0:T(8,128)(2,1)S(1)} %get-tuple-element.38.refs_3_, ...), custom_call_target="tpu_custom_call" | custom-call | bytes 1 | tf_op jit(solution)/shard_map/up_first/pallas_call | solution.py:67
  14.3 1.8 %collective-permute-start.4 = (bf16[512,256]{1,0:T(8,128)(2,1)S(1)}, bf16[512,256]{1,0:T(8,128)(2,1)S(1)}, u32[]{:S(2)}, u32[]{:S(2)}) collective-permute-start(bf16[512,256]{1,0:T(8,128)(2,1)S(1)} %get-tuple-element.41), channel_id=1, source_target_pairs={{0,4},{4,0},{8,12},{12,8},{1,5},{5,1},{9,13},{13,9},{2,6},{6,2},{1... | collective-permute-start | bytes 786440 | tf_op jit(solution)/shard_map/ppermute | solution.py:38
  16.1 4.0 %collective-permute-done.5.refs_2_.refs_3_ = bf16[512,256]{1,0:T(8,128)(2,1)S(1)} collective-permute-done((bf16[512,256]{1,0:T(8,128)(2,1)S(1)}, bf16[512,256]{1,0:T(8,128)(2,1)S(1)}, u32[]{:S(2)}, u32[]{:S(2)}) %collective-permute-start.5) | collective-permute-done | bytes 262176 | tf_op jit(solution)/shard_map/ppermute | solution.py:38
  20.8 1.4 %up_second.2.refs_1_ = f32[512,256]{1,0:T(8,128)S(1)} custom-call(bf16[1,2,2048,2048]{3,2,1,0:T(8,128)(2,1)S(1)} %bitcast.1, bf16[2,2048,256]{2,1,0:T(8,128)(2,1)S(1)} %get-tuple-element.40.refs_1_, bf16[512,256]{1,0:T(8,128)(2,1)S(1)} %collective-permute-done.5.refs_2_.refs_3_, bf16[512,256]{1,0:T(8,128)(2,1)S(1)} %collective-permute-done.6.refs_3_.refs_4_), custom_call_target="tpu_custom_call" | custom-call | flops 20999999488 | bytes 1048576 | tf_op jit(solution)/shard_map/up_second/pallas_call | solution.py:67
  22.2 3.9 %collective-permute-done.4.refs_0_ = bf16[512,256]{1,0:T(8,128)(2,1)S(1)} collective-permute-done((bf16[512,256]{1,0:T(8,128)(2,1)S(1)}, bf16[512,256]{1,0:T(8,128)(2,1)S(1)}, u32[]{:S(2)}, u32[]{:S(2)}) %collective-permute-start.4) | collective-permute-done | bytes 262176 | tf_op jit(solution)/shard_map/ppermute | solution.py:38
  26.2 2.5 %up_rest.2 = (bf16[512,256]{1,0:T(8,128)(2,1)S(1)}, f32[512,256]{1,0:T(8,128)S(1)}) custom-call(bf16[1,2,2048,2048]{3,2,1,0:T(8,128)(2,1)S(1)} %bitcast.1, bf16[2,2048,256]{2,1,0:T(8,128)(2,1)S(1)} %get-tuple-element.40.refs_1_, bf16[512,256]{1,0:T(8,128)(2,1)S(1)} %hop.2.refs_2_.refs_5_), custom_call_target="tpu_custom_call" | custom-call | flops 20999999488 | bytes 1048576 | tf_op jit(solution)/shard_map/up_rest/pallas_call | solution.py:67
  28.6 1.6 %collective-permute-start.8 = (bf16[512,256]{1,0:T(8,128)(2,1)S(1)}, bf16[512,256]{1,0:T(8,128)(2,1)S(1)}, u32[]{:S(2)}, u32[]{:S(2)}) collective-permute-start(bf16[512,256]{1,0:T(8,128)(2,1)S(1)} %hop.2.refs_2_.refs_5_), channel_id=1, source_target_pairs={{0,8},{4,12},{8,0},{12,4},{1,9},{5,13},{9,1},{13,5},{2,10},{6,14},... | collective-permute-start | bytes 786440 | tf_op jit(solution)/shard_map/ppermute | solution.py:38
  30.3 2.1 %collective-permute-start.7 = (bf16[512,256]{1,0:T(8,128)(2,1)S(1)}, bf16[512,256]{1,0:T(8,128)(2,1)S(1)}, u32[]{:S(2)}, u32[]{:S(2)}) collective-permute-start(bf16[512,256]{1,0:T(8,128)(2,1)S(1)} %get-tuple-element.43), channel_id=1, source_target_pairs={{0,4},{4,0},{8,12},{12,8},{1,5},{5,1},{9,13},{13,9},{2,6},{6,2},{1... | collective-permute-start | bytes 786440 | tf_op jit(solution)/shard_map/ppermute | solution.py:38
  32.4 1.5 %down_sibling.2 = (bf16[2,2048,256]{2,1,0:T(8,128)(2,1)S(1)}, f32[512,256]{1,0:T(8,128)S(1)}) custom-call(bf16[1,2,2048,2048]{3,2,1,0:T(8,128)(2,1)S(1)} %bitcast.1, bf16[512,256]{1,0:T(8,128)(2,1)S(1)} %ready_down.1.refs_1_, bf16[512,256]{1,0:T(8,128)(2,1)S(1)} %collective-permute-done.9.refs_2_, ...), custom_call_target="tpu_custom_call" | custom-call | flops 20999999488 | bytes 1048576 | tf_op jit(solution)/shard_map/down_sibling/pallas_call | solution.py:67
  34.0 1.2 %down_far.2.refs_0_ = f32[512,256]{1,0:T(8,128)S(1)} custom-call(bf16[1,2,2048,2048]{3,2,1,0:T(8,128)(2,1)S(1)} %bitcast.1, bf16[2,2048,256]{2,1,0:T(8,128)(2,1)S(1)} %get-tuple-element.46.refs_1_), custom_call_target="tpu_custom_call" | custom-call | flops 20999999488 | bytes 1048576 | tf_op jit(solution)/shard_map/down_far/pallas_call | solution.py:67
  40.7 2.8 %collective-permute-done.7.refs_0_ = bf16[512,256]{1,0:T(8,128)(2,1)S(1)} collective-permute-done((bf16[512,256]{1,0:T(8,128)(2,1)S(1)}, bf16[512,256]{1,0:T(8,128)(2,1)S(1)}, u32[]{:S(2)}, u32[]{:S(2)}) %collective-permute-start.7) | collective-permute-done | bytes 262176 | tf_op jit(solution)/shard_map/ppermute | solution.py:38
  44.6 1.6 %collective-permute-start.14 = (bf16[512,256]{1,0:T(8,128)(2,1)S(1)}, bf16[512,256]{1,0:T(8,128)(2,1)S(1)}, u32[]{:S(2)}, u32[]{:S(2)}) collective-permute-start(bf16[512,256]{1,0:T(8,128)(2,1)S(1)} %get-tuple-element.50), channel_id=1, source_target_pairs={{0,16},{16,0},{1,17},{17,1},{2,18},{18,2},{3,19},{19,3},{4,20},{20... | collective-permute-start | bytes 786440 | tf_op jit(solution)/shard_map/ppermute | solution.py:314
  46.4 5.8 %collective-permute-done.14.refs_0_.refs_1_ = bf16[512,256]{1,0:T(8,128)(2,1)S(1)} collective-permute-done((bf16[512,256]{1,0:T(8,128)(2,1)S(1)}, bf16[512,256]{1,0:T(8,128)(2,1)S(1)}, u32[]{:S(2)}, u32[]{:S(2)}) %collective-permute-start.14) | collective-permute-done | bytes 262176 | tf_op jit(solution)/shard_map/ppermute | solution.py:314
  53.1 1.4 %collective-permute-start.20 = (bf16[512,256]{1,0:T(8,128)(2,1)S(1)}, bf16[512,256]{1,0:T(8,128)(2,1)S(1)}, u32[]{:S(2)}, u32[]{:S(2)}) collective-permute-start(bf16[512,256]{1,0:T(8,128)(2,1)S(1)} %get-tuple-element.60.refs_1_), channel_id=1, source_target_pairs={{0,8},{4,12},{8,0},{12,4},{1,9},{5,13},{9,1},{13,5},{2,10},{6,14},... | collective-permute-start | bytes 786440 | tf_op jit(solution)/shard_map/ppermute | solution.py:38
  54.5 1.6 %collective-permute-start.21 = (bf16[512,256]{1,0:T(8,128)(2,1)S(1)}, bf16[512,256]{1,0:T(8,128)(2,1)S(1)}, u32[]{:S(2)}, u32[]{:S(2)}) collective-permute-start(bf16[512,256]{1,0:T(8,128)(2,1)S(1)} %get-tuple-element.60.refs_1_), channel_id=1, source_target_pairs={{0,4},{4,0},{8,12},{12,8},{1,5},{5,1},{9,13},{13,9},{2,6},{6,2},{1... | collective-permute-start | bytes 786440 | tf_op jit(solution)/shard_map/ppermute | solution.py:38
  56.1 3.1 %collective-permute-done.16.refs_0_ = bf16[512,256]{1,0:T(8,128)(2,1)S(1)} collective-permute-done((bf16[512,256]{1,0:T(8,128)(2,1)S(1)}, bf16[512,256]{1,0:T(8,128)(2,1)S(1)}, u32[]{:S(2)}, u32[]{:S(2)}) %collective-permute-start.16) | collective-permute-done | bytes 262176 | tf_op jit(solution)/shard_map/ppermute | solution.py:53
  60.8 1.6 %up_first.3 = (bf16[2,2048,256]{2,1,0:T(8,128)(2,1)S(1)}, bf16[512,256]{1,0:T(8,128)(2,1)S(1)}) custom-call(bf16[1,2,2048,2048]{3,2,1,0:T(8,128)(2,1)S(1)} %bitcast.1, bf16[512,256]{1,0:T(8,128)(2,1)S(1)} %get-tuple-element.55.refs_1_, bf16[512,256]{1,0:T(8,128)(2,1)S(1)} %collective-permute-done.15.refs_2_, bf16[256,256]{1,0:T(8,128)(2,1)S(1)} %get-tuple-element.56.refs_3_, ...), custom_call_target="tpu_custom_call" | custom-call | bytes 1 | tf_op jit(solution)/shard_map/up_first/pallas_call | solution.py:67
  63.4 5.0 %collective-permute-done.20.refs_2_.refs_3_ = bf16[512,256]{1,0:T(8,128)(2,1)S(1)} collective-permute-done((bf16[512,256]{1,0:T(8,128)(2,1)S(1)}, bf16[512,256]{1,0:T(8,128)(2,1)S(1)}, u32[]{:S(2)}, u32[]{:S(2)}) %collective-permute-start.20) | collective-permute-done | bytes 262176 | tf_op jit(solution)/shard_map/ppermute | solution.py:38
  68.5 1.4 %up_second.3.refs_1_ = f32[512,256]{1,0:T(8,128)S(1)} custom-call(bf16[1,2,2048,2048]{3,2,1,0:T(8,128)(2,1)S(1)} %bitcast.1, bf16[2,2048,256]{2,1,0:T(8,128)(2,1)S(1)} %get-tuple-element.58.refs_1_, bf16[512,256]{1,0:T(8,128)(2,1)S(1)} %collective-permute-done.20.refs_2_.refs_3_, bf16[512,256]{1,0:T(8,128)(2,1)S(1)} %collective-permute-done.21.refs_3_.refs_4_), custom_call_target="tpu_custom_call" | custom-call | flops 20999999488 | bytes 1048576 | tf_op jit(solution)/shard_map/up_second/pallas_call | solution.py:67
  69.9 4.2 %collective-permute-done.19.refs_0_ = bf16[512,256]{1,0:T(8,128)(2,1)S(1)} collective-permute-done((bf16[512,256]{1,0:T(8,128)(2,1)S(1)}, bf16[512,256]{1,0:T(8,128)(2,1)S(1)}, u32[]{:S(2)}, u32[]{:S(2)}) %collective-permute-start.19) | collective-permute-done | bytes 262176 | tf_op jit(solution)/shard_map/ppermute | solution.py:38
  74.1 2.5 %up_rest.3 = (bf16[512,256]{1,0:T(8,128)(2,1)S(1)}, f32[512,256]{1,0:T(8,128)S(1)}) custom-call(bf16[1,2,2048,2048]{3,2,1,0:T(8,128)(2,1)S(1)} %bitcast.1, bf16[2,2048,256]{2,1,0:T(8,128)(2,1)S(1)} %get-tuple-element.58.refs_1_, bf16[512,256]{1,0:T(8,128)(2,1)S(1)} %hop.3.refs_2_.refs_5_), custom_call_target="tpu_custom_call" | custom-call | flops 20999999488 | bytes 1048576 | tf_op jit(solution)/shard_map/up_rest/pallas_call | solution.py:67
  76.6 1.5 %collective-permute-start.23 = (bf16[512,256]{1,0:T(8,128)(2,1)S(1)}, bf16[512,256]{1,0:T(8,128)(2,1)S(1)}, u32[]{:S(2)}, u32[]{:S(2)}) collective-permute-start(bf16[512,256]{1,0:T(8,128)(2,1)S(1)} %hop.3.refs_2_.refs_5_), channel_id=1, source_target_pairs={{0,8},{4,12},{8,0},{12,4},{1,9},{5,13},{9,1},{13,5},{2,10},{6,14},... | collective-permute-start | bytes 786440 | tf_op jit(solution)/shard_map/ppermute | solution.py:38
  78.1 1.4 %collective-permute-start.22 = (bf16[512,256]{1,0:T(8,128)(2,1)S(1)}, bf16[512,256]{1,0:T(8,128)(2,1)S(1)}, u32[]{:S(2)}, u32[]{:S(2)}) collective-permute-start(bf16[512,256]{1,0:T(8,128)(2,1)S(1)} %get-tuple-element.62), channel_id=1, source_target_pairs={{0,4},{4,0},{8,12},{12,8},{1,5},{5,1},{9,13},{13,9},{2,6},{6,2},{1... | collective-permute-start | bytes 786440 | tf_op jit(solution)/shard_map/ppermute | solution.py:38
  79.6 1.5 %down_sibling.3 = (bf16[2,2048,256]{2,1,0:T(8,128)(2,1)S(1)}, f32[512,256]{1,0:T(8,128)S(1)}) custom-call(bf16[1,2,2048,2048]{3,2,1,0:T(8,128)(2,1)S(1)} %bitcast.1, bf16[512,256]{1,0:T(8,128)(2,1)S(1)} %get-tuple-element.60.refs_1_, bf16[512,256]{1,0:T(8,128)(2,1)S(1)} %collective-permute-done.24.refs_2_, ...), custom_call_target="tpu_custom_call" | custom-call | flops 20999999488 | bytes 1048576 | tf_op jit(solution)/shard_map/down_sibling/pallas_call | solution.py:67
  83.2 1.6 %collective-permute-start.26 = (bf16[512,256]{1,0:T(8,128)(2,1)S(1)}, bf16[512,256]{1,0:T(8,128)(2,1)S(1)}, u32[]{:S(2)}, u32[]{:S(2)}) collective-permute-start(bf16[512,256]{1,0:T(8,128)(2,1)S(1)} %far_sum.3.refs_2_), channel_id=1, source_target_pairs={{0,2},{1,3},{2,0},{3,1},{4,6},{5,7},{6,4},{7,5},{8,10},{9,11},{10,... | collective-permute-start | bytes 786440 | tf_op jit(solution)/shard_map/ppermute | solution.py:53
  88.9 2.4 %collective-permute-done.23.refs_1_ = bf16[512,256]{1,0:T(8,128)(2,1)S(1)} collective-permute-done((bf16[512,256]{1,0:T(8,128)(2,1)S(1)}, bf16[512,256]{1,0:T(8,128)(2,1)S(1)}, u32[]{:S(2)}, u32[]{:S(2)}) %collective-permute-start.23) | collective-permute-done | bytes 262176 | tf_op jit(solution)/shard_map/ppermute | solution.py:38
  91.7 1.6 %collective-permute-start.29 = (bf16[512,256]{1,0:T(8,128)(2,1)S(1)}, bf16[512,256]{1,0:T(8,128)(2,1)S(1)}, u32[]{:S(2)}, u32[]{:S(2)}) collective-permute-start(bf16[512,256]{1,0:T(8,128)(2,1)S(1)} %get-tuple-element.69), channel_id=1, source_target_pairs={{0,16},{16,0},{1,17},{17,1},{2,18},{18,2},{3,19},{19,3},{4,20},{20... | collective-permute-start | bytes 786440 | tf_op jit(solution)/shard_map/ppermute | solution.py:314
  93.3 6.2 %collective-permute-done.29.refs_0_.refs_1_ = bf16[512,256]{1,0:T(8,128)(2,1)S(1)} collective-permute-done((bf16[512,256]{1,0:T(8,128)(2,1)S(1)}, bf16[512,256]{1,0:T(8,128)(2,1)S(1)}, u32[]{:S(2)}, u32[]{:S(2)}) %collective-permute-start.29) | collective-permute-done | bytes 262176 | tf_op jit(solution)/shard_map/ppermute | solution.py:314
  (84 shorter events, 21.6 us)
Async XLA Ops:
  1.7 11.0 %slice-start = ((s8[16777216]{0:T(1024)(128)(4,1)}), s8[4194304]{0:T(1024)(128)(4,1)S(1)}, s32[]{:S(2)}) async-start(s8[16777216]{0:T(1024)(128)(4,1)} %bitcast), calls=%async_computation | async-start | bytes 8388608
  1.7 11.0 %slice-start.1 = ((s8[16777216]{0:T(1024)(128)(4,1)}), s8[4194304]{0:T(1024)(128)(4,1)S(1)}, s32[]{:S(2)}) async-start(s8[16777216]{0:T(1024)(128)(4,1)} %bitcast), calls=%async_computation.1 | async-start | bytes 8388608
  1.7 9.3 %collective-permute-start.1 = (bf16[512,256]{1,0:T(8,128)(2,1)S(1)}, bf16[512,256]{1,0:T(8,128)(2,1)S(1)}, u32[]{:S(2)}, u32[]{:S(2)}) collective-permute-start(bf16[512,256]{1,0:T(8,128)(2,1)S(1)} %ready_up.1.refs_1_), channel_id=1, source_target_pairs={{0,2},{1,3},{2,0},{3,1},{4,6},{5,7},{6,4},{7,5},{8,10},{9,11},{10,... | collective-permute-start | bytes 786440 | tf_op jit(solution)/shard_map/ppermute | solution.py:53
  4.7 6.9 %collective-permute-start = (bf16[512,256]{1,0:T(8,128)(2,1)S(1)}, bf16[512,256]{1,0:T(8,128)(2,1)S(1)}, u32[]{:S(2)}, u32[]{:S(2)}) collective-permute-start(bf16[512,256]{1,0:T(8,128)(2,1)S(1)} %ready_up.1.refs_1_), channel_id=1, source_target_pairs={{0,1},{1,0},{2,3},{3,2},{4,5},{5,4},{6,7},{7,6},{8,9},{9,8},{10,11... | collective-permute-start | bytes 786440 | tf_op jit(solution)/shard_map/ppermute | solution.py:53
  4.8 15.4 %collective-permute-start.5 = (bf16[512,256]{1,0:T(8,128)(2,1)S(1)}, bf16[512,256]{1,0:T(8,128)(2,1)S(1)}, u32[]{:S(2)}, u32[]{:S(2)}) collective-permute-start(bf16[512,256]{1,0:T(8,128)(2,1)S(1)} %ready_down.1.refs_1_), channel_id=1, source_target_pairs={{0,8},{4,12},{8,0},{12,4},{1,9},{5,13},{9,1},{13,5},{2,10},{6,14},... | collective-permute-start | bytes 786440 | tf_op jit(solution)/shard_map/ppermute | solution.py:38
  7.4 13.4 %collective-permute-start.6 = (bf16[512,256]{1,0:T(8,128)(2,1)S(1)}, bf16[512,256]{1,0:T(8,128)(2,1)S(1)}, u32[]{:S(2)}, u32[]{:S(2)}) collective-permute-start(bf16[512,256]{1,0:T(8,128)(2,1)S(1)} %ready_down.1.refs_1_), channel_id=1, source_target_pairs={{0,4},{4,0},{8,12},{12,8},{1,5},{5,1},{9,13},{13,9},{2,6},{6,2},{1... | collective-permute-start | bytes 786440 | tf_op jit(solution)/shard_map/ppermute | solution.py:38
  11.1 1.4 %collective-permute-start.2 = (bf16[256,256]{1,0:T(8,128)(2,1)S(1)}, bf16[256,256]{1,0:T(8,128)(2,1)S(1)}, u32[]{:S(2)}, u32[]{:S(2)}) collective-permute-start(bf16[256,256]{1,0:T(8,128)(2,1)S(1)} %get-tuple-element.38.refs_3_), channel_id=1, source_target_pairs={{0,1},{1,0},{2,3},{3,2},{4,5},{5,4},{6,7},{7,6},{8,9},{9,8},{10,11... | collective-permute-start | bytes 393224 | tf_op jit(solution)/shard_map/ppermute | solution.py:53
  11.1 1.5 %collective-permute-start.3 = (bf16[256,256]{1,0:T(8,128)(2,1)S(1)}, bf16[256,256]{1,0:T(8,128)(2,1)S(1)}, u32[]{:S(2)}, u32[]{:S(2)}) collective-permute-start(bf16[256,256]{1,0:T(8,128)(2,1)S(1)} %get-tuple-element.39.refs_4_), channel_id=1, source_target_pairs={{0,1},{1,0},{2,3},{3,2},{4,5},{5,4},{6,7},{7,6},{8,9},{9,8},{10,11... | collective-permute-start | bytes 393224 | tf_op jit(solution)/shard_map/ppermute | solution.py:53
  14.3 11.8 %collective-permute-start.4 = (bf16[512,256]{1,0:T(8,128)(2,1)S(1)}, bf16[512,256]{1,0:T(8,128)(2,1)S(1)}, u32[]{:S(2)}, u32[]{:S(2)}) collective-permute-start(bf16[512,256]{1,0:T(8,128)(2,1)S(1)} %get-tuple-element.41), channel_id=1, source_target_pairs={{0,4},{4,0},{8,12},{12,8},{1,5},{5,1},{9,13},{13,9},{2,6},{6,2},{1... | collective-permute-start | bytes 786440 | tf_op jit(solution)/shard_map/ppermute | solution.py:38
  20.2 12.2 %collective-permute-start.9 = (bf16[512,256]{1,0:T(8,128)(2,1)S(1)}, bf16[512,256]{1,0:T(8,128)(2,1)S(1)}, u32[]{:S(2)}, u32[]{:S(2)}) collective-permute-start(bf16[512,256]{1,0:T(8,128)(2,1)S(1)} %collective-permute-done.5.refs_2_.refs_3_), channel_id=1, source_target_pairs={{0,4},{4,0},{8,12},{12,8},{1,5},{5,1},{9,13},{13,9},{2,6},{6,2},{1... | collective-permute-start | bytes 786440 | tf_op jit(solution)/shard_map/ppermute | solution.py:38
  28.6 14.8 %collective-permute-start.8 = (bf16[512,256]{1,0:T(8,128)(2,1)S(1)}, bf16[512,256]{1,0:T(8,128)(2,1)S(1)}, u32[]{:S(2)}, u32[]{:S(2)}) collective-permute-start(bf16[512,256]{1,0:T(8,128)(2,1)S(1)} %hop.2.refs_2_.refs_5_), channel_id=1, source_target_pairs={{0,8},{4,12},{8,0},{12,4},{1,9},{5,13},{9,1},{13,5},{2,10},{6,14},... | collective-permute-start | bytes 786440 | tf_op jit(solution)/shard_map/ppermute | solution.py:38
  30.3 13.2 %collective-permute-start.7 = (bf16[512,256]{1,0:T(8,128)(2,1)S(1)}, bf16[512,256]{1,0:T(8,128)(2,1)S(1)}, u32[]{:S(2)}, u32[]{:S(2)}) collective-permute-start(bf16[512,256]{1,0:T(8,128)(2,1)S(1)} %get-tuple-element.43), channel_id=1, source_target_pairs={{0,4},{4,0},{8,12},{12,8},{1,5},{5,1},{9,13},{13,9},{2,6},{6,2},{1... | collective-permute-start | bytes 786440 | tf_op jit(solution)/shard_map/ppermute | solution.py:38
  33.9 2.0 %collective-permute-start.10 = (f32[512,256]{1,0:T(8,128)S(1)}, f32[512,256]{1,0:T(8,128)S(1)}, u32[]{:S(2)}, u32[]{:S(2)}) collective-permute-start(f32[512,256]{1,0:T(8,128)S(1)} %get-tuple-element.47), channel_id=1, source_target_pairs={{0,1},{1,0},{2,3},{3,2},{4,5},{5,4},{6,7},{7,6},{8,9},{9,8},{10,11... | collective-permute-start | bytes 1572872 | tf_op jit(solution)/shard_map/ppermute | solution.py:53
  36.0 8.4 %collective-permute-start.11 = (bf16[512,256]{1,0:T(8,128)(2,1)S(1)}, bf16[512,256]{1,0:T(8,128)(2,1)S(1)}, u32[]{:S(2)}, u32[]{:S(2)}) collective-permute-start(bf16[512,256]{1,0:T(8,128)(2,1)S(1)} %far_sum.2.refs_2_), channel_id=1, source_target_pairs={{0,2},{1,3},{2,0},{3,1},{4,6},{5,7},{6,4},{7,5},{8,10},{9,11},{10,... | collective-permute-start | bytes 786440 | tf_op jit(solution)/shard_map/ppermute | solution.py:53
  37.8 1.4 %collective-permute-start.12 = (bf16[256,256]{1,0:T(8,128)(2,1)S(1)}, bf16[256,256]{1,0:T(8,128)(2,1)S(1)}, u32[]{:S(2)}, u32[]{:S(2)}) collective-permute-start(bf16[256,256]{1,0:T(8,128)(2,1)S(1)} %get-tuple-element.48), channel_id=1, source_target_pairs={{0,1},{1,0},{2,3},{3,2},{4,5},{5,4},{6,7},{7,6},{8,9},{9,8},{10,11... | collective-permute-start | bytes 393224 | tf_op jit(solution)/shard_map/ppermute | solution.py:53
  37.9 1.5 %collective-permute-start.13 = (bf16[256,256]{1,0:T(8,128)(2,1)S(1)}, bf16[256,256]{1,0:T(8,128)(2,1)S(1)}, u32[]{:S(2)}, u32[]{:S(2)}) collective-permute-start(bf16[256,256]{1,0:T(8,128)(2,1)S(1)} %get-tuple-element.49), channel_id=1, source_target_pairs={{0,1},{1,0},{2,3},{3,2},{4,5},{5,4},{6,7},{7,6},{8,9},{9,8},{10,11... | collective-permute-start | bytes 393224 | tf_op jit(solution)/shard_map/ppermute | solution.py:53
  44.6 7.6 %collective-permute-start.14 = (bf16[512,256]{1,0:T(8,128)(2,1)S(1)}, bf16[512,256]{1,0:T(8,128)(2,1)S(1)}, u32[]{:S(2)}, u32[]{:S(2)}) collective-permute-start(bf16[512,256]{1,0:T(8,128)(2,1)S(1)} %get-tuple-element.50), channel_id=1, source_target_pairs={{0,16},{16,0},{1,17},{17,1},{2,18},{18,2},{3,19},{19,3},{4,20},{20... | collective-permute-start | bytes 786440 | tf_op jit(solution)/shard_map/ppermute | solution.py:314
  52.5 6.7 %collective-permute-start.16 = (bf16[512,256]{1,0:T(8,128)(2,1)S(1)}, bf16[512,256]{1,0:T(8,128)(2,1)S(1)}, u32[]{:S(2)}, u32[]{:S(2)}) collective-permute-start(bf16[512,256]{1,0:T(8,128)(2,1)S(1)} %get-tuple-element.55.refs_1_), channel_id=1, source_target_pairs={{0,2},{1,3},{2,0},{3,1},{4,6},{5,7},{6,4},{7,5},{8,10},{9,11},{10,... | collective-permute-start | bytes 786440 | tf_op jit(solution)/shard_map/ppermute | solution.py:53
  53.1 6.7 %collective-permute-start.15 = (bf16[512,256]{1,0:T(8,128)(2,1)S(1)}, bf16[512,256]{1,0:T(8,128)(2,1)S(1)}, u32[]{:S(2)}, u32[]{:S(2)}) collective-permute-start(bf16[512,256]{1,0:T(8,128)(2,1)S(1)} %get-tuple-element.55.refs_1_), channel_id=1, source_target_pairs={{0,1},{1,0},{2,3},{3,2},{4,5},{5,4},{6,7},{7,6},{8,9},{9,8},{10,11... | collective-permute-start | bytes 786440 | tf_op jit(solution)/shard_map/ppermute | solution.py:53
  53.1 15.3 %collective-permute-start.20 = (bf16[512,256]{1,0:T(8,128)(2,1)S(1)}, bf16[512,256]{1,0:T(8,128)(2,1)S(1)}, u32[]{:S(2)}, u32[]{:S(2)}) collective-permute-start(bf16[512,256]{1,0:T(8,128)(2,1)S(1)} %get-tuple-element.60.refs_1_), channel_id=1, source_target_pairs={{0,8},{4,12},{8,0},{12,4},{1,9},{5,13},{9,1},{13,5},{2,10},{6,14},... | collective-permute-start | bytes 786440 | tf_op jit(solution)/shard_map/ppermute | solution.py:38
  54.5 14.0 %collective-permute-start.21 = (bf16[512,256]{1,0:T(8,128)(2,1)S(1)}, bf16[512,256]{1,0:T(8,128)(2,1)S(1)}, u32[]{:S(2)}, u32[]{:S(2)}) collective-permute-start(bf16[512,256]{1,0:T(8,128)(2,1)S(1)} %get-tuple-element.60.refs_1_), channel_id=1, source_target_pairs={{0,4},{4,0},{8,12},{12,8},{1,5},{5,1},{9,13},{13,9},{2,6},{6,2},{1... | collective-permute-start | bytes 786440 | tf_op jit(solution)/shard_map/ppermute | solution.py:38
  59.2 1.4 %collective-permute-start.17 = (bf16[256,256]{1,0:T(8,128)(2,1)S(1)}, bf16[256,256]{1,0:T(8,128)(2,1)S(1)}, u32[]{:S(2)}, u32[]{:S(2)}) collective-permute-start(bf16[256,256]{1,0:T(8,128)(2,1)S(1)} %get-tuple-element.56.refs_3_), channel_id=1, source_target_pairs={{0,1},{1,0},{2,3},{3,2},{4,5},{5,4},{6,7},{7,6},{8,9},{9,8},{10,11... | collective-permute-start | bytes 393224 | tf_op jit(solution)/shard_map/ppermute | solution.py:53
  59.3 1.5 %collective-permute-start.18 = (bf16[256,256]{1,0:T(8,128)(2,1)S(1)}, bf16[256,256]{1,0:T(8,128)(2,1)S(1)}, u32[]{:S(2)}, u32[]{:S(2)}) collective-permute-start(bf16[256,256]{1,0:T(8,128)(2,1)S(1)} %get-tuple-element.57.refs_4_), channel_id=1, source_target_pairs={{0,1},{1,0},{2,3},{3,2},{4,5},{5,4},{6,7},{7,6},{8,9},{9,8},{10,11... | collective-permute-start | bytes 393224 | tf_op jit(solution)/shard_map/ppermute | solution.py:53
  62.5 11.6 %collective-permute-start.19 = (bf16[512,256]{1,0:T(8,128)(2,1)S(1)}, bf16[512,256]{1,0:T(8,128)(2,1)S(1)}, u32[]{:S(2)}, u32[]{:S(2)}) collective-permute-start(bf16[512,256]{1,0:T(8,128)(2,1)S(1)} %get-tuple-element.59), channel_id=1, source_target_pairs={{0,4},{4,0},{8,12},{12,8},{1,5},{5,1},{9,13},{13,9},{2,6},{6,2},{1... | collective-permute-start | bytes 786440 | tf_op jit(solution)/shard_map/ppermute | solution.py:38
  68.5 11.1 %collective-permute-start.24 = (bf16[512,256]{1,0:T(8,128)(2,1)S(1)}, bf16[512,256]{1,0:T(8,128)(2,1)S(1)}, u32[]{:S(2)}, u32[]{:S(2)}) collective-permute-start(bf16[512,256]{1,0:T(8,128)(2,1)S(1)} %collective-permute-done.20.refs_2_.refs_3_), channel_id=1, source_target_pairs={{0,4},{4,0},{8,12},{12,8},{1,5},{5,1},{9,13},{13,9},{2,6},{6,2},{1... | collective-permute-start | bytes 786440 | tf_op jit(solution)/shard_map/ppermute | solution.py:38
  76.6 14.8 %collective-permute-start.23 = (bf16[512,256]{1,0:T(8,128)(2,1)S(1)}, bf16[512,256]{1,0:T(8,128)(2,1)S(1)}, u32[]{:S(2)}, u32[]{:S(2)}) collective-permute-start(bf16[512,256]{1,0:T(8,128)(2,1)S(1)} %hop.3.refs_2_.refs_5_), channel_id=1, source_target_pairs={{0,8},{4,12},{8,0},{12,4},{1,9},{5,13},{9,1},{13,5},{2,10},{6,14},... | collective-permute-start | bytes 786440 | tf_op jit(solution)/shard_map/ppermute | solution.py:38
  78.1 10.8 %collective-permute-start.22 = (bf16[512,256]{1,0:T(8,128)(2,1)S(1)}, bf16[512,256]{1,0:T(8,128)(2,1)S(1)}, u32[]{:S(2)}, u32[]{:S(2)}) collective-permute-start(bf16[512,256]{1,0:T(8,128)(2,1)S(1)} %get-tuple-element.62), channel_id=1, source_target_pairs={{0,4},{4,0},{8,12},{12,8},{1,5},{5,1},{9,13},{13,9},{2,6},{6,2},{1... | collective-permute-start | bytes 786440 | tf_op jit(solution)/shard_map/ppermute | solution.py:38
  81.1 2.0 %collective-permute-start.25 = (f32[512,256]{1,0:T(8,128)S(1)}, f32[512,256]{1,0:T(8,128)S(1)}, u32[]{:S(2)}, u32[]{:S(2)}) collective-permute-start(f32[512,256]{1,0:T(8,128)S(1)} %get-tuple-element.66), channel_id=1, source_target_pairs={{0,1},{1,0},{2,3},{3,2},{4,5},{5,4},{6,7},{7,6},{8,9},{9,8},{10,11... | collective-permute-start | bytes 1572872 | tf_op jit(solution)/shard_map/ppermute | solution.py:53
  83.2 8.4 %collective-permute-start.26 = (bf16[512,256]{1,0:T(8,128)(2,1)S(1)}, bf16[512,256]{1,0:T(8,128)(2,1)S(1)}, u32[]{:S(2)}, u32[]{:S(2)}) collective-permute-start(bf16[512,256]{1,0:T(8,128)(2,1)S(1)} %far_sum.3.refs_2_), channel_id=1, source_target_pairs={{0,2},{1,3},{2,0},{3,1},{4,6},{5,7},{6,4},{7,5},{8,10},{9,11},{10,... | collective-permute-start | bytes 786440 | tf_op jit(solution)/shard_map/ppermute | solution.py:53
  86.0 1.4 %collective-permute-start.27 = (bf16[256,256]{1,0:T(8,128)(2,1)S(1)}, bf16[256,256]{1,0:T(8,128)(2,1)S(1)}, u32[]{:S(2)}, u32[]{:S(2)}) collective-permute-start(bf16[256,256]{1,0:T(8,128)(2,1)S(1)} %get-tuple-element.67), channel_id=1, source_target_pairs={{0,1},{1,0},{2,3},{3,2},{4,5},{5,4},{6,7},{7,6},{8,9},{9,8},{10,11... | collective-permute-start | bytes 393224 | tf_op jit(solution)/shard_map/ppermute | solution.py:53
  86.0 1.5 %collective-permute-start.28 = (bf16[256,256]{1,0:T(8,128)(2,1)S(1)}, bf16[256,256]{1,0:T(8,128)(2,1)S(1)}, u32[]{:S(2)}, u32[]{:S(2)}) collective-permute-start(bf16[256,256]{1,0:T(8,128)(2,1)S(1)} %get-tuple-element.68), channel_id=1, source_target_pairs={{0,1},{1,0},{2,3},{3,2},{4,5},{5,4},{6,7},{7,6},{8,9},{9,8},{10,11... | collective-permute-start | bytes 393224 | tf_op jit(solution)/shard_map/ppermute | solution.py:53
  91.7 7.8 %collective-permute-start.29 = (bf16[512,256]{1,0:T(8,128)(2,1)S(1)}, bf16[512,256]{1,0:T(8,128)(2,1)S(1)}, u32[]{:S(2)}, u32[]{:S(2)}) collective-permute-start(bf16[512,256]{1,0:T(8,128)(2,1)S(1)} %get-tuple-element.69), channel_id=1, source_target_pairs={{0,16},{16,0},{1,17},{17,1},{2,18},{18,2},{3,19},{19,3},{4,20},{20... | collective-permute-start | bytes 786440 | tf_op jit(solution)/shard_map/ppermute | solution.py:314
  (12 other events, 73.4 us)
